TPU v7x, 32 devices: a whole 2x2x4 slice. The times are simulated.
32 devices in a mesh: seq: 4 (over x, core), fsdp: 8 (over z, y).
Axes of the slice: x: 2, y: 2, z: 4, core: 2. Of those that a mesh axis runs over, the one named last changes fastest.
Arguments:
- tokens: bfloat16 [2048, 8, 768], P(('seq', 'fsdp')), may hold values from -6 to 6
- pass_index: int32 [2048, 8], P(('seq', 'fsdp')), may hold values from 0 to 4
- lengths: int32 [8], replicated, may hold values from 1 to 2048, 12288 in all
- table: bfloat16 [5, 768], replicated, may hold values from -3 to 3
- gain_attn: bfloat16 [768], P('fsdp'), may hold values from 0.5 to 1.5
- w_qkv: bfloat16 [768, 2304], P('fsdp'), may hold values from -0.21875 to 0.21875
- w_out: bfloat16 [768, 768], P('fsdp'), may hold values from -1.25 to 1.25
- gain_mlp: bfloat16 [768], P('fsdp'), may hold values from 0.5 to 1.5
- w_up: bfloat16 [768, 3072], P('fsdp'), may hold values from -0.21875 to 0.21875
- w_down: bfloat16 [3072, 768], P('fsdp'), may hold values from -0.109375 to 0.109375
- cotangent: bfloat16 [2048, 8, 768], P(('seq', 'fsdp')), may hold values from -6 to 6
Outputs:
- output: bfloat16 [2048, 8, 768], P(('seq', 'fsdp'))
- d_tokens: bfloat16 [2048, 8, 768], P(('seq', 'fsdp'))
- d_table: float32 [5, 768], replicated
- d_gain_attn: float32 [768], P('fsdp')
- d_w_qkv: float32 [768, 2304], P('fsdp')
- d_w_out: float32 [768, 768], P('fsdp')
- d_gain_mlp: float32 [768], P('fsdp')
- d_w_up: float32 [768, 3072], P('fsdp')
- d_w_down: float32 [3072, 768], P('fsdp')
Inputs may be any that keep to these rules, and one draw needn't show every extreme that they name: The longest sequence is exactly 2048 long; all lengths add up to 12288.
All inputs are finite; a program needn't handle non-finite values.
Results may differ from a plain program's by a relative error of at most 0.013.
Values may be sent and summed in bfloat16 or wider, within the bound.
No kernel may reach another device: no remote copies, remote signals or barrier semaphores. Data moves between devices by JAX's collectives and lax.ppermute only.
A program may use at most 192 MiB of HBM per device.

v0:
```python
import functools

import jax
import jax.numpy as jnp
from jax import lax
from jax.experimental import pallas as pl
from jax.experimental.pallas import tpu as pltpu
from jax.sharding import PartitionSpec as P

HEADS = 12
EPSILON = 1e-05
LOG2E = 1.4426950408889634
LN2 = 0.6931471805599453
MASKED = -1e30
DH = 64


def dotg(a, b, ca, cb):
    return lax.dot_general(a, b, (((ca,), (cb,)), ((), ())), preferred_element_type=jnp.float32)


def slot_of(block, info):
    return (((block & 1) << 1) | (block >> 1)) ^ info[0]


def attend_body(info, qkv, *refs, blk):
    out, lse, acc = refs[-3:]
    i = pl.program_id(0)
    length = info[1]
    qt = qkv[slot_of(i, info), 0:DH, :]
    scale = DH ** -0.5 * LOG2E

    def step(j, carry, masked):
        top, tot = carry
        kt = qkv[slot_of(j, info), DH : 2 * DH, :]
        vt = qkv[slot_of(j, info), 2 * DH : 3 * DH, :]
        st = dotg(kt, qt, 0, 0) * scale
        if masked:
            key_at = j * blk + lax.broadcasted_iota(jnp.int32, st.shape, 0)
            query_at = i * blk + lax.broadcasted_iota(jnp.int32, st.shape, 1)
            st = jnp.where((query_at >= key_at) & (key_at < length), st, MASKED)
        new_top = jnp.maximum(top, jnp.max(st, axis=0, keepdims=True))
        fade = jnp.exp2(top - new_top)
        pt = jnp.exp2(st - new_top)
        tot = tot * fade + jnp.sum(pt, axis=0, keepdims=True)
        acc[...] = acc[...] * fade + dotg(vt, pt.astype(jnp.bfloat16), 1, 0)
        return new_top, tot

    acc[...] = jnp.zeros_like(acc)
    carry = (jnp.full((1, blk), MASKED, jnp.float32), jnp.zeros((1, blk), jnp.float32))
    plain = jnp.minimum(i, length // blk)
    stop = jnp.minimum(i + 1, (length + blk - 1) // blk)
    carry = lax.fori_loop(0, plain, functools.partial(step, masked=False), carry)
    top, tot = lax.fori_loop(plain, stop, functools.partial(step, masked=True), carry)
    out[0] = (acc[...] / tot).astype(jnp.bfloat16)
    lse[0] = top + jnp.log2(tot)


def attend(info, qkv):
    blocks, _, blk = qkv.shape
    return pl.pallas_call(
        functools.partial(attend_body, blk=blk),
        grid_spec=pltpu.PrefetchScalarGridSpec(
            num_scalar_prefetch=1,
            grid=(blocks,),
            in_specs=[pl.BlockSpec((blocks, 3 * DH, blk), lambda i, info: (0, info[2], 0))],
            out_specs=[
                pl.BlockSpec((1, DH, blk), lambda i, info: (slot_of(i, info), 0, 0)),
                pl.BlockSpec((1, 1, blk), lambda i, info: (i, 0, 0)),
            ],
            scratch_shapes=[pltpu.VMEM((DH, blk), jnp.float32)],
        ),
        out_shape=[
            jax.ShapeDtypeStruct((blocks, DH, blk), jnp.bfloat16),
            jax.ShapeDtypeStruct((blocks, 1, blk), jnp.float32),
        ],
        compiler_params=pltpu.CompilerParams(vmem_limit_bytes=16 << 20),
        cost_estimate=SMALL,
        name="attend",
    )(info, qkv)


def attend_back_body(info, qkv, att, *refs, blocks, blk):
    came, (lse, dqkv, dq, q_rows, do_rows, delta, datt) = refs[:blocks], refs[blocks:]
    j = pl.program_id(0)
    length = info[1]
    scale = DH ** -0.5
    at_q, at_k, at_v = slice(0, DH), slice(DH, 2 * DH), slice(2 * DH, 3 * DH)

    @pl.when(j == 0)
    def _():
        dq[...] = jnp.zeros_like(dq)
        for b in range(blocks):
            datt[b] = came[b][...]
        for b in range(blocks):
            at = slot_of(b, info)
            dt = datt[at]
            q_rows[b] = qkv[at, at_q, :].T
            do_rows[b] = dt.T
            delta[b] = jnp.sum(dt.astype(jnp.float32) * att[at].astype(jnp.float32), axis=0, keepdims=True)

    kt = qkv[slot_of(j, info), at_k, :]
    vt = qkv[slot_of(j, info), at_v, :]
    k_rows = kt.T
    v_rows = vt.T

    def step(i, carry, masked):
        dk, dv = carry
        qt = qkv[slot_of(i, info), at_q, :]
        st = jnp.dot(k_rows, qt, preferred_element_type=jnp.float32)
        pt = jnp.exp2(st * (scale * LOG2E) - lse[i])
        if masked:
            key_at = j * blk + lax.broadcasted_iota(jnp.int32, st.shape, 0)
            query_at = i * blk + lax.broadcasted_iota(jnp.int32, st.shape, 1)
            pt = jnp.where((query_at >= key_at) & (key_at < length), pt, 0.0)
        dpt = jnp.dot(v_rows, datt[slot_of(i, info)], preferred_element_type=jnp.float32)
        dst = (pt * (dpt - delta[i])).astype(jnp.bfloat16)
        dv = dv + jnp.dot(pt.astype(jnp.bfloat16), do_rows[i], preferred_element_type=jnp.float32)
        dk = dk + jnp.dot(dst, q_rows[i], preferred_element_type=jnp.float32)
        dq[i] = dq[i] + jnp.dot(kt, dst, preferred_element_type=jnp.float32)
        return dk, dv

    zero = jnp.zeros((blk, DH), jnp.float32)
    whole = (j + 1) * blk <= length
    some = j * blk < length
    masked_end = jnp.where(some, jnp.where(whole, j + 1, blocks), j)
    carry = lax.fori_loop(j, masked_end, functools.partial(step, masked=True), (zero, zero))
    dk, dv = lax.fori_loop(
        jnp.where(whole, j + 1, blocks), blocks, functools.partial(step, masked=False), carry
    )
    dqkv[slot_of(j, info), at_k, :] = (dk * scale).astype(jnp.bfloat16).T
    dqkv[slot_of(j, info), at_v, :] = dv.astype(jnp.bfloat16).T
    dqkv[slot_of(j, info), at_q, :] = (dq[j] * scale).astype(jnp.bfloat16)


def attend_back(info, qkv, att, datt, lse):
    blocks, rows, blk = qkv.shape
    third = pl.BlockSpec((blocks, 3 * DH, blk), lambda j, info: (0, info[2], 0))
    return pl.pallas_call(
        functools.partial(attend_back_body, blocks=blocks, blk=blk),
        grid_spec=pltpu.PrefetchScalarGridSpec(
            num_scalar_prefetch=1,
            grid=(blocks,),
            in_specs=[
                third,
                pl.BlockSpec((blocks, DH, blk), lambda j, info: (0, 0, 0)),
                *[pl.BlockSpec((DH, blk), lambda j, info: (info[2], 0))] * blocks,
                pl.BlockSpec((blocks, 1, blk), lambda j, info: (0, 0, 0)),
            ],
            out_specs=pl.BlockSpec((blocks, 3 * DH, blk), lambda j, info: (0, 0, 0)),
            scratch_shapes=[
                pltpu.VMEM((blocks, DH, blk), jnp.float32),
                pltpu.VMEM((blocks, blk, DH), jnp.bfloat16),
                pltpu.VMEM((blocks, blk, DH), jnp.bfloat16),
                pltpu.VMEM((blocks, 1, blk), jnp.float32),
                pltpu.VMEM((blocks, DH, blk), jnp.bfloat16),
            ],
        ),
        out_shape=jax.ShapeDtypeStruct((blocks, 3 * DH, blk), jnp.bfloat16),
        compiler_params=pltpu.CompilerParams(vmem_limit_bytes=18 << 20),
        cost_estimate=SMALL,
        name="attend_back",
    )(info, qkv, att, *datt, lse)


SMALL = pl.CostEstimate(flops=1 << 20, bytes_accessed=1 << 20, transcendentals=0)
GELU_A = 0.7978845608028654
GELU_B = 0.044715


def mlp_body(nm, cot, wu, wd, *refs, begun):
    acc, dnm, dwu, dwd = refs[-4:]

    @pl.when(pl.program_id(0) == 0)
    def _():
        acc[...] = refs[0][...] if begun else jnp.zeros_like(acc)
        dnm[...] = refs[1][...] if begun else jnp.zeros_like(dnm)

    x = nm[...]
    g = cot[...]
    u = jnp.dot(x, wu[...], preferred_element_type=jnp.float32)
    da = dotg(g, wd[...], 1, 1)
    square = u * u
    th = jnp.tanh(GELU_A * u * (1.0 + GELU_B * square))
    half = 0.5 * (1.0 + th)
    a = (u * half).astype(jnp.bfloat16)
    slope = half + 0.5 * u * (1.0 - th * th) * (GELU_A * (1.0 + 3.0 * GELU_B * square))
    du = (da * slope).astype(jnp.bfloat16)
    acc[...] += jnp.dot(a, wd[...], preferred_element_type=jnp.float32)
    dnm[...] += dotg(du, wu[...], 1, 1)
    dwu[...] = dotg(x, du, 0, 0).astype(jnp.bfloat16)
    dwd[...] = dotg(a, g, 0, 0).astype(jnp.bfloat16)


def mlp_part(nm, cot, wu, wd, sums=(), step=256):
    rows, width = nm.shape
    ff = wu.shape[1]
    whole = pl.BlockSpec((rows, width), lambda i: (0, 0))
    up = pl.BlockSpec((width, step), lambda i: (0, i))
    down = pl.BlockSpec((step, width), lambda i: (i, 0))
    return pl.pallas_call(
        functools.partial(mlp_body, begun=bool(sums)),
        grid=(ff // step,),
        in_specs=[whole, whole, up, down] + [whole, whole][: len(sums)],
        out_specs=[whole, whole, up, down],
        out_shape=[
            jax.ShapeDtypeStruct((rows, width), jnp.float32),
            jax.ShapeDtypeStruct((rows, width), jnp.float32),
            jax.ShapeDtypeStruct(wu.shape, jnp.bfloat16),
            jax.ShapeDtypeStruct(wd.shape, jnp.bfloat16),
        ],
        input_output_aliases={4: 0, 5: 1} if sums else {},
        compiler_params=pltpu.CompilerParams(vmem_limit_bytes=26 << 20),
        cost_estimate=SMALL,
        name="mlp_part",
    )(nm, cot, wu, wd, *sums)


ORDER = (0, 2, 1, 3)


def cut(array, axis, steps):
    shape = tuple(n // steps if k == axis else n for k, n in enumerate(array.shape))
    return pl.BlockSpec(shape, lambda i: tuple(i if k == axis else 0 for k in range(len(shape))))


def row_call(body, name, out_shape, place, operands, in_axes, out_axes, steps=1, scratch=()):
    return pl.pallas_call(
        body,
        grid=(steps,),
        in_specs=[pl.BlockSpec(memory_space=pltpu.SMEM)] + [cut(a, k, steps) for a, k in zip(operands, in_axes)],
        out_specs=[cut(a, k, steps) for a, k in zip(out_shape, out_axes)],
        out_shape=out_shape,
        scratch_shapes=scratch,
        compiler_params=pltpu.CompilerParams(vmem_limit_bytes=20 << 20),
        cost_estimate=SMALL,
        name=name,
    )(place, *operands)


def rows_at(place, slot, part):
    return pl.ds(pl.multiple_of((place[0] ^ ORDER[slot]) * part, DH), part)


def project_out_body(place, *refs):
    pieces, (w, inputs, gain, residual, nm) = refs[:-5], refs[-5:]
    part = len(pieces) // 4 * DH
    residual[...] = inputs[...].astype(jnp.float32)
    for s in range(4):
        heads = jnp.concatenate([p[...] for p in pieces[s::4]], axis=0)
        residual[...] += dotg(heads, w[rows_at(place, s, part), :], 0, 0)
    z, _ = norm_stats(residual[...])
    nm[...] = (z * gain[...]).astype(jnp.bfloat16)


def turn_body(place, residual, sum_near, sum_far, grad_near, grad_far, cot, gain, w, *refs):
    result, d_residual, d_branch, d_gain, d_heads = refs
    part = d_heads.shape[1]
    result[...] = (residual[...] + sum_near[...] + sum_far[...].astype(jnp.float32)).astype(jnp.bfloat16)
    z, inverse = norm_stats(residual[...])
    back, gain_part = norm_back(z, inverse, gain[...], grad_near[...] + grad_far[...].astype(jnp.float32))

    @pl.when(pl.program_id(0) == 0)
    def _():
        d_gain[...] = jnp.zeros_like(d_gain)

    d_gain[...] += gain_part
    d_residual[...] = cot[...].astype(jnp.float32) + back
    d_branch[...] = d_residual[...].astype(jnp.bfloat16)
    for s in range(4):
        d_heads[s] = dotg(w[rows_at(place, s, part), :], d_branch[...], 1, 1).astype(jnp.bfloat16)


def join_columns_body(place, *refs):
    pieces, out = refs[:4], refs[4]
    part = pieces[0].shape[1]

    def fill(me):
        for s in range(4):
            d = me ^ ORDER[s]
            out[:, d * part : (d + 1) * part] = pieces[s][...]

    for me in range(4):
        pl.when(place[0] == me)(functools.partial(fill, me))


def out_grad_body(place, *refs):
    came, (d_branch, *pieces, out) = refs[:-6], refs[-6:]
    part = len(came) // 4 * DH
    for s in range(4):
        heads = jnp.concatenate([p[...] for p in came[s::4]], axis=0)
        out[rows_at(place, s, part), :] = jnp.dot(
            heads, d_branch[...], preferred_element_type=jnp.float32
        ).astype(jnp.bfloat16)

    def fill(me):
        for s in range(4):
            d = me ^ ORDER[s]
            pieces[s][...] = out[:, d * part : (d + 1) * part]

    for me in range(4):
        pl.when(place[0] == me)(functools.partial(fill, me))


def rows_grad_body(place, *refs):
    *heads, w, out = refs
    for s in range(out.shape[0]):
        grad = jnp.concatenate([h[s] for h in heads], axis=0)
        out[s] = dotg(grad, w[...], 0, 1).astype(jnp.bfloat16)


def weight_grad_body(place, *refs):
    normed, heads, (*parts, out) = refs[:4], refs[4:-4], refs[-4:]
    total = 0.0
    for s in range(4):
        total += dotg(normed[s][...], jnp.concatenate([h[s] for h in heads], axis=0), 0, 1)
    rest = sum(p[...].astype(jnp.float32) for p in parts).astype(jnp.bfloat16)
    out[...] = jnp.concatenate((total.astype(jnp.bfloat16), rest), axis=1)


def pick_up_body(place, w, out, *, each):
    def fill(me):
        for g in range(out.shape[1] // each):
            out[:, g * each : (g + 1) * each] = w[:, (g * 4 + me) * each : (g * 4 + me + 1) * each]

    for me in range(4):
        pl.when(place[0] == me)(functools.partial(fill, me))


def place_up_body(place, grads, out, *, each):
    for p in range(4):
        for g in range(grads.shape[-1] // each):
            at = (g * 4 + p) * each
            out[:, at : at + each] = grads[p, :, g * each : (g + 1) * each].astype(jnp.float32)


def place_qkv_body(place, grads, qkv, out):
    width = out.shape[1]
    part = width // 4
    heads = part // DH
    for p in range(4):
        out[:, p * part : (p + 1) * part] = grads[p, :, 3 * part :].astype(jnp.float32)
        for h in range(heads):
            for which in range(3):
                at = which * width + (p * heads + h) * DH
                start = (h * 3 + which) * DH
                qkv[:, at : at + DH] = grads[p, :, start : start + DH].astype(jnp.float32)


def swap(value, axis, bit):
    count = lax.axis_size(axis)
    return lax.ppermute(value, axis, [(i, i ^ bit) for i in range(count)])


def bits_of(axis):
    count = lax.axis_size(axis)
    assert count & (count - 1) == 0, "axis size"
    return [1 << b for b in reversed(range(count.bit_length() - 1))]


def is_set(axis, bit):
    return (lax.axis_index(axis) & bit) != 0


def join(own, came, axis, bit, at):
    own, came = (jnp.expand_dims(a, at) for a in (own, came))
    shape = own.shape[:at] + (2,) + own.shape[at + 1 :]
    place = lax.broadcasted_iota(jnp.int32, shape, at)
    return jnp.where(place == is_set(axis, bit).astype(jnp.int32), own, came)


def gather(value, axis, bits, at=0):
    for k, bit in enumerate(bits):
        value = join(value, swap(value, axis, bit), axis, bit, at + k)
    return value


def spread(blocks, bit):
    return blocks | {r ^ bit: swap(b, "seq", bit) for r, b in blocks.items()}


def add(a, b):
    return (a.astype(jnp.float32) + b.astype(jnp.float32)).astype(a.dtype)


def fold(blocks, bit):
    return {r: add(b, swap(blocks[r ^ bit], "seq", bit)) for r, b in blocks.items() if not r & bit}


def halve(value, axis, bit, at, *more):
    mine = is_set(axis, bit).astype(jnp.int32)
    part = lambda which: functools.reduce(
        add, [lax.dynamic_index_in_dim(v, which, at, keepdims=False) for v in (value, *more)]
    )
    return part(mine), swap(part(1 - mine), axis, bit)


def norm_stats(values):
    centre = jnp.mean(values, axis=-1, keepdims=True)
    shifted = values - centre
    spread_of = jnp.mean(shifted * shifted, axis=-1, keepdims=True)
    inverse = lax.rsqrt(spread_of + EPSILON)
    return shifted * inverse, inverse


def norm_back(z, inverse, gain, grad):
    e = grad * gain
    back = (e - jnp.mean(e, axis=-1, keepdims=True) - z * jnp.mean(e * z, axis=-1, keepdims=True)) * inverse
    return back, jnp.sum(grad * z, axis=0, keepdims=True)


def pick_at(value, at):
    return lax.dynamic_index_in_dim(value, at, 1, keepdims=False)


def after(first, *values):
    return lax.optimization_barrier((first, values))[1]


def per_device(
    tokens, pass_index, lengths, table, gain_attn, w_qkv, w_out, gain_mlp, w_up, w_down, cotangent
):
    bf16, f32 = jnp.bfloat16, jnp.float32
    groups, parts = lax.axis_size("fsdp"), lax.axis_size("seq")
    local_len, seq_total, width = tokens.shape
    assert seq_total == groups and parts == 4
    heads = HEADS // parts
    part = width // parts
    ff = w_up.shape[1]
    own_rows = width // groups
    ff_each = ff // groups // parts
    me, group = lax.axis_index("seq"), lax.axis_index("fsdp")
    f_bits = bits_of("fsdp")
    last = len(f_bits) - 1
    top, low, between = f_bits[0], f_bits[-1], f_bits[1:-1]
    sizes = (2,) * len(f_bits)
    span = local_len * groups
    pick = lambda a, at: lax.dynamic_index_in_dim(a, me, at, keepdims=False)
    deal = lambda a: lax.all_to_all(a, "fsdp", split_axis=0, concat_axis=0, tiled=True)
    across = lambda a: [a[0]] + [swap(a[s], "seq", r) for s, r in enumerate(ORDER) if r]

    chooser = (pass_index[..., None] == jnp.arange(table.shape[0], dtype=jnp.int32)).astype(bf16)
    embedded = jnp.einsum("pnc,cd->npd", chooser, table, preferred_element_type=f32)
    summed = (jnp.swapaxes(tokens, 0, 1).astype(f32) + embedded).astype(bf16)
    inputs = deal(summed).reshape(span, width)
    qkv_slice = pick(w_qkv.reshape(own_rows, 3, parts, heads, DH), 2)
    qkv_slice = jnp.swapaxes(qkv_slice, 1, 2).reshape(own_rows, 3 * part)
    out_slice = pick(w_out.reshape(own_rows, parts, part), 1)
    gains = jnp.stack((gain_attn, gain_mlp), axis=1)
    qkv_slice, out_slice = after(summed, qkv_slice, out_slice)
    packet = jnp.concatenate((qkv_slice, out_slice, gains, jnp.zeros((own_rows, 126), bf16)), axis=1)
    packet_came = swap(packet, "fsdp", top)
    place = me.astype(jnp.int32)[None]
    (up,) = row_call(
        functools.partial(pick_up_body, each=ff_each), "pick_up",
        [jax.ShapeDtypeStruct((own_rows, ff // parts), bf16)], place, [w_up], [None], [None],
    )
    down = pick(w_down.reshape(parts, ff_each, width), 0)
    pair = jnp.stack((up, down))

    rows_2, rows_1 = swap(inputs, "seq", 2), swap(inputs, "seq", 1)
    rows = (inputs, rows_2, rows_1, swap(rows_2, "seq", 1))
    packet, packet_came, pair = after(inputs, packet, packet_came, pair)
    packet = gather(join(packet, packet_came, "fsdp", top, 0), "fsdp", between, 1)
    packet, pair = lax.optimization_barrier((packet, pair))
    packet = gather(packet, "fsdp", (low,), last).reshape(width, -1)
    wq = packet[:, : 3 * part]
    out_cols = packet[:, 3 * part : width]
    gain_one = packet[:, width].astype(f32)
    gain_two = packet[:, width + 1].astype(f32)
    pair_came = swap(pair, "fsdp", top)
    marks = jnp.swapaxes(pass_index, 0, 1)[..., None].astype(bf16)
    cot_packet = jnp.concatenate(
        (jnp.swapaxes(cotangent, 0, 1), jnp.broadcast_to(marks, marks.shape[:2] + (128,))), axis=2
    )

    normed = [(norm_stats(b.astype(f32))[0] * gain_one).astype(bf16) for b in rows]
    pair, pair_came, out_cols = after(rows[3], pair, pair_came, out_cols)
    pair = join(pair, pair_came, "fsdp", top, 1)
    pair = gather(pair, "fsdp", between, 2)
    out_2 = swap(out_cols, "seq", 2)
    qkv = jnp.stack([dotg(wq, b, 0, 1).astype(bf16) for b in normed])
    length = lax.dynamic_index_in_dim(lengths, group, 0, keepdims=False)
    slot = (me & 1) * 2 + (me >> 1)
    info = [jnp.stack((slot, length, jnp.int32(h))).astype(jnp.int32) for h in range(heads)]

    att, lse, crossed, many = [None] * heads, [None] * heads, [None] * heads, heads - 1
    att[1], lse[1] = attend(info[1], qkv)
    pair, out_cols, out_2, cot_packet = after(att[1], pair, out_cols, out_2, cot_packet)
    up, down = pair[0], pair[1]
    (qkv,) = after((up, down), qkv)
    cot_packet = deal(cot_packet).reshape(span, -1)
    up_came = swap(up, "fsdp", low)
    down_2 = swap(down, "seq", 2)
    out_1, out_3 = swap(out_cols, "seq", 1), swap(out_2, "seq", 1)
    for h in range(2, heads):
        att[h], lse[h] = attend(info[h], qkv)
    att[1:], out_1, out_3, down = lax.optimization_barrier((att[1:], out_1, out_3, down))
    square = jax.ShapeDtypeStruct((width, width), bf16)
    (w_out_full,) = row_call(
        join_columns_body, "join_columns", [square], place, [out_cols, out_2, out_1, out_3], [None] * 4, [None]
    )
    (qkv,) = after((att[1:], w_out_full), qkv)
    crossed[1:] = [across(a) for a in att[1:]]
    down_came = swap(down, "fsdp", low)
    att[0], lse[0] = attend(info[0], qkv)
    up, up_came, down_2, att[0], crossed[1:] = lax.optimization_barrier((up, up_came, down_2, att[0], crossed[1:]))
    crossed[0] = across(att[0])
    up = join(up, up_came, "fsdp", low, last).reshape(width, ff // parts)

    crossed[0], up, down, down_came, down_2, cot_packet = lax.optimization_barrier(
        (crossed[0], up, down, down_came, down_2, cot_packet)
    )
    crossed = [piece for pieces in crossed for piece in pieces]
    up_2 = swap(up, "seq", 2)
    cot = cot_packet[:, :width]
    passes = cot_packet[:, width]
    cot_far = swap(cot, "seq", 1)
    down_2_came = swap(down_2, "fsdp", low)
    down = join(down, down_came, "fsdp", low, last).reshape(ff // parts, width)
    rows_f32 = jax.ShapeDtypeStruct((span, width), f32)
    rows_bf16 = jax.ShapeDtypeStruct((span, width), bf16)
    residual, nm = row_call(
        project_out_body, "project_out", [rows_f32, rows_bf16], place,
        [*crossed, w_out_full, inputs, gain_two[None]], [1] * len(crossed) + [None, 0, None], [0, 0], parts,
    )
    nm_far = swap(nm, "seq", 1)
    *near, up_0, down_0 = mlp_part(nm, cot, up, down)
    *far, up_1, down_1 = mlp_part(nm_far, cot_far, up, down)
    down_2, down_2_came, up_2 = after(far[0], down_2, down_2_came, up_2)
    down_2 = join(down_2, down_2_came, "fsdp", low, last).reshape(ff // parts, width)
    *far, d_up_2, d_down_2 = mlp_part(nm_far, cot_far, up_2, down_2, far)
    far = [swap(a.astype(bf16), "seq", 1) for a in far]
    *near, up_2, down_2 = mlp_part(nm, cot, up_2, down_2, near)
    up_2 = add(up_2, d_up_2)
    down = jnp.stack((add(down_0, down_1), add(down_2, d_down_2))).reshape(2, *sizes, ff_each, width)
    down = halve(down, "fsdp", low, last + 1)
    head_rows = jax.ShapeDtypeStruct((parts, part, span), bf16)
    result, d_residual, d_branch, d_gain_mlp, d_heads = row_call(
        turn_body,
        "turn",
        [rows_bf16, rows_f32, rows_bf16, jax.ShapeDtypeStruct((1, width), f32), head_rows],
        place,
        [residual, near[0], far[0], near[1], far[1], cot, gain_two[None], w_out_full],
        [0] * 6 + [None] * 2,
        [0, 0, 0, None, 2],
        parts,
    )
    d_heads = across(d_heads)
    piece = jax.ShapeDtypeStruct((width, part), bf16)
    d_out, d_out_x, *d_out_far = row_call(
        out_grad_body, "out_grad", [piece] * 4, place, [*crossed, d_branch], [None] * (len(crossed) + 1), [None] * 4,
        scratch=[pltpu.VMEM((width, width), bf16)],
    )
    d_heads, d_out, d_out_x, d_out_far, up_0, up_1, up_2, result = lax.optimization_barrier(
        (d_heads, d_out, d_out_x, d_out_far, up_0, up_1, up_2, result)
    )

    up_came = swap(up_2, "seq", 2)
    out_back = deal(result.reshape(groups, local_len, width))
    d_out_1, d_out_3 = [swap(a, "seq", 1) for a in d_out_far]
    d_qkv = [attend_back(info[0], qkv, att[0], d_heads, lse[0])]
    down, d_out_x, d_out_3 = after(d_qkv, down, d_out_x, d_out_3)
    down = halve(down[0], "fsdp", f_bits[-2], last, down[1])
    d_out_x = add(d_out_x, d_out_3)
    d_heads = after((down[0], d_out_x), d_heads)[0]
    d_out_x = swap(d_out_x, "seq", 2)
    for h in range(1, many):
        d_qkv.append(attend_back(info[h], qkv, att[h], d_heads, lse[h]))
    up_0, up_1, up_came, down, d_out_x, out_back = after(d_qkv, up_0, up_1, up_came, down, d_out_x, out_back)
    split = lambda a: a.reshape(*sizes, own_rows, ff // parts)
    up = halve(split(up_0), "fsdp", low, last, split(up_1), split(up_came))
    for k in reversed(range(last - 1)):
        down = halve(down[0], "fsdp", f_bits[k], k + 1, down[1])
    (d_heads,) = after((up[0], down[0], out_back), d_heads)
    d_qkv.append(attend_back(info[many], qkv, att[many], d_heads, lse[many]))
    d_qkv, down, up = lax.optimization_barrier((d_qkv, down, up))

    half = jax.ShapeDtypeStruct((2, span, width), bf16)
    project_back = lambda a: row_call(rows_grad_body, "rows_grad", [half], place, [*a, wq], [None] * (heads + 1), [None])[0]
    d_far = swap(project_back([d[2:] for d in d_qkv]), "seq", 1)
    d_near = project_back([d[:2] for d in d_qkv])
    (d_tail,) = after(d_near, d_qkv)
    down = add(*down)
    up = halve(up[0], "fsdp", f_bits[-2], last - 1, up[1])
    (d_wq,) = row_call(
        weight_grad_body, "weight_grad", [square], place, [*normed, *d_tail, d_out, d_out_1, d_out_x],
        [None] * (7 + heads), [None],
    )
    d_near, d_wq, up = lax.optimization_barrier((d_near, d_wq, up))
    d_wq = halve(d_wq.reshape(*sizes, own_rows, width), "fsdp", low, last)
    for k in reversed(range(last - 1)):
        up = halve(up[0], "fsdp", f_bits[k], k, up[1])
    (d_near,) = after(up[0], d_near)
    d_near = add(d_near, d_far)
    d_came = swap(d_near[1], "seq", 2)
    d_wq = halve(d_wq[0], "fsdp", f_bits[-2], last - 1, d_wq[1])
    d_wq, down = after(d_came, d_wq, down)
    down_came = swap(down[1], "seq", 2)
    for k in reversed(range(last - 1)):
        d_wq = halve(d_wq[0], "fsdp", f_bits[k], k, d_wq[1])
    d_normed = d_near[0].astype(f32) + d_came.astype(f32)
    z_one, inverse_one = norm_stats(inputs.astype(f32))
    d_in_norm, d_gain_attn = norm_back(z_one, inverse_one, gain_one, d_normed)
    d_inputs = (d_residual + d_in_norm).astype(bf16)
    d_back = deal(d_inputs.reshape(groups, local_len, width))
    up, d_wq = after(d_inputs, up, d_wq)
    (d_wq,) = after(d_back, d_wq)
    pair = jnp.stack((add(*up), add(down[0], down_came)))
    grads = gather(pair, "seq", (2, 1)).reshape(parts, 2, own_rows, width)
    (g_up,) = row_call(
        functools.partial(place_up_body, each=ff_each), "place_up",
        [jax.ShapeDtypeStruct((own_rows, ff), f32)], place, [grads[:, 0]], [None], [None],
    )
    g_down = grads[:, 1].reshape(ff // groups, width).astype(f32)

    count = table.shape[0]
    picks = (passes[None, :] == jnp.arange(count, dtype=jnp.int32)[:, None].astype(bf16)).astype(bf16)
    d_table = jnp.dot(picks, d_inputs, preferred_element_type=f32)
    small = jnp.concatenate((d_table, d_gain_attn, d_gain_mlp, jnp.zeros_like(d_gain_mlp)), axis=0)
    for bit in (1, 2):
        small = small + swap(small, "seq", bit)
    for bit in reversed(f_bits[1:]):
        small = small + swap(small, "fsdp", bit)
    (small,) = after(d_back, small)
    small = small + swap(small, "fsdp", top)
    owned_gain = lambda row: lax.dynamic_slice_in_dim(small[row], group * own_rows, own_rows)

    d_wq = gather(add(*d_wq), "seq", (2, 1)).reshape(parts, own_rows, width)
    g_qkv, g_out = row_call(
        place_qkv_body, "place_qkv",
        [jax.ShapeDtypeStruct((own_rows, 3 * width), f32), jax.ShapeDtypeStruct((own_rows, width), f32)],
        place, [d_wq], [None], [None] * 2,
    )
    return (
        jnp.swapaxes(out_back, 0, 1),
        jnp.swapaxes(d_back, 0, 1),
        small[:count],
        owned_gain(count),
        g_qkv,
        g_out,
        owned_gain(count + 1),
        g_up,
        g_down,
    )


def solution(mesh):
    return jax.shard_map(
        per_device,
        mesh=mesh,
        in_specs=(
            P(("seq", "fsdp"), None, None),
            P(("seq", "fsdp"), None),
            P(),
            P(),
            P("fsdp"),
            P("fsdp", None),
            P("fsdp", None),
            P("fsdp"),
            P("fsdp", None),
            P("fsdp", None),
            P(("seq", "fsdp"), None, None),
        ),
        out_specs=(
            P(("seq", "fsdp"), None, None),
            P(("seq", "fsdp"), None, None),
            P(),
            P("fsdp"),
            P("fsdp", None),
            P("fsdp", None),
            P("fsdp"),
            P("fsdp", None),
            P("fsdp", None),
        ),
        check_vma=False,
    )
```

profile of v0, /device:TPU:0, one launch (start us, length us, event | category | flops | bytes accessed | tf_op | source)
XLA Modules:
  0.0 362.4 jit_solution(9249311391494601317)
XLA Ops:
  1.5 1.6 fusion.18
  4.1 7.3 %all-to-all-start = ((bf16[8,64,768]{2,1,0:T(8,128)(2,1)}), bf16[8,64,768]{2,1,0:T(8,128)(2,1)S(1)}, u32[]{:S(2)}, u32[]{:S(2)}) async-start(bf16[8,64,768]{2,1,0:T(8,128)(2,1)} %copy.123), calls=%async_computation | async-start | bytes 1572864 | tf_op jit(solution)/shard_map/all_to_all | solution.py:439
  12.7 3.0 collective-permute-start
  20.7 17.1 %all-to-all-done = bf16[8,64,768]{2,1,0:T(8,128)(2,1)S(1)} async-done(((bf16[8,64,768]{2,1,0:T(8,128)(2,1)}), bf16[8,64,768]{2,1,0:T(8,128)(2,1)S(1)}, u32[]{:S(2)}, u32[]{:S(2)}) %all-to-all-start) | async-done | bytes 786464 | tf_op jit(solution)/shard_map/all_to_all | solution.py:439
  37.8 1.5 collective-permute-start.3
  39.3 2.1 collective-permute-done
  42.6 8.3 %collective-permute-done.1 = bf16[2,96,896]{2,1,0:T(8,128)(2,1)S(1)} collective-permute-done((bf16[2,96,896]{2,1,0:T(8,128)(2,1)S(1)}, bf16[2,96,896]{2,1,0:T(8,128)(2,1)S(1)}, u32[]{:S(2)}, u32[]{:S(2)}) %collective-permute-start.1) | collective-permute-done | bytes 344096 | tf_op jit(solution)/shard_map/ppermute | solution.py:352
  52.1 2.0 collective-permute-start.2
  54.3 3.5 collective-permute-done.3
  58.8 10.0 %collective-permute-done.2 = bf16[2,2,96,896]{3,2,1,0:T(8,128)(2,1)S(1)} collective-permute-done((bf16[2,2,96,896]{3,2,1,0:T(8,128)(2,1)S(1)}, bf16[2,2,96,896]{3,2,1,0:T(8,128)(2,1)S(1)}, u32[]{:S(2)}, u32[]{:S(2)}) %collective-permute-start.2) | collective-permute-done | bytes 688160 | tf_op jit(solution)/shard_map/ppermute | solution.py:352
  70.7 1.6 collective-permute-start.8
  73.4 1.5 collective-permute-start.7
  79.6 5.7 %attend.3 = (bf16[4,64,512]{2,1,0:T(8,128)(2,1)S(1)}, f32[4,1,512]{2,1,0:T(1,128)S(1)}) custom-call(s32[3]{0:T(128)S(1)} %get-tuple-element.353.info, bf16[4,576,512]{2,1,0:T(8,128)(2,1)S(1)} %pad_maximum_fusion.qkv), custom_call_target="tpu_custom_call" | custom-call | flops 1048576 | bytes 1048576 | tf_op jit(solution)/shard_map/attend/pallas_call | solution.py:61
  88.1 14.8 %all-to-all-start.1 = ((bf16[8,64,896]{2,1,0:T(8,128)(2,1)}), bf16[8,64,896]{2,1,0:T(8,128)(2,1)}, u32[]{:S(2)}, u32[]{:S(2)}) async-start(bf16[8,64,896]{2,1,0:T(8,128)(2,1)} %pad_maximum_fusion.1), calls=%async_computation.1 | async-start | bytes 1835008 | tf_op jit(solution)/shard_map/all_to_all | solution.py:439
  106.2 2.7 collective-permute-start.11
  108.9 5.7 %attend.4 = (bf16[4,64,512]{2,1,0:T(8,128)(2,1)S(1)}, f32[4,1,512]{2,1,0:T(1,128)S(1)}) custom-call(s32[3]{0:T(128)S(1)} %pad_add_fusion.3.info, bf16[4,576,512]{2,1,0:T(8,128)(2,1)S(1)} %pad_maximum_fusion.qkv), custom_call_target="tpu_custom_call" | custom-call | flops 1048576 | bytes 1048576 | tf_op jit(solution)/shard_map/attend/pallas_call | solution.py:61
  116.9 2.0 collective-permute-start.22
  119.6 1.8 collective-permute-done.15.refs_7_
  123.2 1.9 collective-permute-start.18
  125.1 1.7 collective-permute-done.13.refs_5_
  130.4 5.7 %attend.5 = (bf16[4,64,512]{2,1,0:T(8,128)(2,1)S(1)}, f32[4,1,512]{2,1,0:T(1,128)S(1)}) custom-call(s32[3]{0:T(128)S(1)} %get-tuple-element.352.info, bf16[4,576,512]{2,1,0:T(8,128)(2,1)S(1)} %pad_maximum_fusion.qkv), custom_call_target="tpu_custom_call" | custom-call | flops 1048576 | bytes 1048576 | tf_op jit(solution)/shard_map/attend/pallas_call | solution.py:61
  137.4 1.6 collective-permute-start.21
  145.7 2.1 slice.135.cot
  147.9 3.4 project_out.1
  153.0 4.9 %collective-permute-start.25 = (bf16[2,2,96,768]{3,2,1,0:T(8,128)(2,1)}, bf16[2,2,96,768]{3,2,1,0:T(8,128)(2,1)}, u32[]{:S(2)}, u32[]{:S(2)}) collective-permute-start(bf16[2,2,96,768]{3,2,1,0:T(8,128)(2,1)} %collective-permute-done.12), channel_id=1, source_target_pairs={{0,1},{1,0},{2,3},{3,2},{4,5},{5,4},{6,7},{7,6},{8,9},{9,8},{10,11... | collective-permute-start | bytes 1769480 | tf_op jit(solution)/shard_map/ppermute | solution.py:352
  157.9 1.5 bitcast_select_fusion.2.wd
  159.5 6.7 %mlp_part.5 = (f32[512,768]{1,0:T(8,128)S(1)}, f32[512,768]{1,0:T(8,128)S(1)}, bf16[768,768]{1,0:T(8,128)(2,1)S(1)}, bf16[768,768]{1,0:T(8,128)(2,1)S(1)}) custom-call(bf16[512,768]{1,0:T(8,128)(2,1)} %get-tuple-element.186.nm, bf16[512,768]{1,0:T(8,128)(2,1)} %slice.135.cot, bf16[768,768]{1,0:T(8,128)(2,1)S(1)} %copy-done.5, ...), custom_call_target="tpu_custom_call" | custom-call | flops 1048576 | bytes 1048576 | tf_op jit(solution)/shard_map/mlp_part/pallas_call | solution.py:201
  167.3 6.7 %mlp_part.4 = (f32[512,768]{1,0:T(8,128)S(1)}, f32[512,768]{1,0:T(8,128)S(1)}, bf16[768,768]{1,0:T(8,128)(2,1)S(1)}, bf16[768,768]{1,0:T(8,128)(2,1)S(1)}) custom-call(bf16[512,768]{1,0:T(8,128)(2,1)} %collective-permute-done.23.nm, bf16[512,768]{1,0:T(8,128)(2,1)} %collective-permute-done.24.cot, bf16[768,768]{1,0:T(8,128)(2,1)S(1)} %copy-done.5, ...), custom_call_target="tpu_custom_call" | custom-call | flops 1048576 | bytes 1048576 | tf_op jit(solution)/shard_map/mlp_part/pallas_call | solution.py:201
  174.0 1.8 bitcast_select_fusion.1.wd
  175.9 7.0 %mlp_part.7 = (f32[512,768]{1,0:T(8,128)S(1)}, f32[512,768]{1,0:T(8,128)S(1)}, bf16[768,768]{1,0:T(8,128)(2,1)S(1)}, bf16[768,768]{1,0:T(8,128)(2,1)S(1)}) custom-call(bf16[512,768]{1,0:T(8,128)(2,1)} %collective-permute-done.23.nm, bf16[512,768]{1,0:T(8,128)(2,1)} %collective-permute-done.24.cot, ...), custom_call_target="tpu_custom_call", output_to_operand_aliasing={{0}: (4, {}), {1}: (5, {})} | custom-call | flops 1048576 | bytes 1048576 | tf_op jit(solution)/shard_map/mlp_part/pallas_call | solution.py:201
  184.0 7.0 %mlp_part.6 = (f32[512,768]{1,0:T(8,128)S(1)}, f32[512,768]{1,0:T(8,128)S(1)}, bf16[768,768]{1,0:T(8,128)(2,1)S(1)}, bf16[768,768]{1,0:T(8,128)(2,1)S(1)}) custom-call(bf16[512,768]{1,0:T(8,128)(2,1)} %get-tuple-element.186.nm, bf16[512,768]{1,0:T(8,128)(2,1)} %slice.135.cot, ...), custom_call_target="tpu_custom_call", output_to_operand_aliasing={{0}: (4, {}), {1}: (5, {})} | custom-call | flops 1048576 | bytes 1048576 | tf_op jit(solution)/shard_map/mlp_part/pallas_call | solution.py:201
  193.7 2.5 collective-permute-start.32
  196.2 5.0 %turn.1 = (bf16[512,768]{1,0:T(8,128)(2,1)S(1)}, f32[512,768]{1,0:T(8,128)S(1)}, bf16[512,768]{1,0:T(8,128)(2,1)S(1)}, f32[1,768]{1,0:T(1,128)S(1)}, bf16[4,192,512]{2,1,0:T(8,128)(2,1)S(1)}) custom-call(s32[1]{0:T(128)} %bitcast.10.place, f32[512,768]{1,0:T(8,128)S(1)} %copy-done.28, f32[512,768]{1,0:T(8,128)S(1)} %get-tuple-element.198.sum_near, ...), custom_call_target="tpu_custom_call" | custom-call | flops 1048576 | bytes 1048576 | tf_op jit(solution)/shard_map/turn/pallas_call | solution.py:228
  209.8 3.0 collective-permute-done.29.refs_1_
  213.4 4.2 %all-to-all-start.2 = ((bf16[8,64,768]{2,1,0:T(8,128)(2,1)}), bf16[8,64,768]{2,1,0:T(8,128)(2,1)}, u32[]{:S(2)}, u32[]{:S(2)}) async-start(bf16[8,64,768]{2,1,0:T(8,128)(2,1)} %bitcast.204), calls=%async_computation.2 | async-start | bytes 1572864 | tf_op jit(solution)/shard_map/all_to_all | solution.py:439
  217.6 1.8 collective-permute-start.34
  222.9 8.3 %attend_back.3.refs_4_ = bf16[4,192,512]{2,1,0:T(8,128)(2,1)S(1)} custom-call(s32[3]{0:T(128)S(1)} %copy-done.87, bf16[4,576,512]{2,1,0:T(8,128)(2,1)S(1)} %pad_maximum_fusion.qkv, bf16[4,64,512]{2,1,0:T(8,128)(2,1)S(1)} %copy-done.40, bf16[192,512]{1,0:T(8,128)(2,1)S(1)} %get-tuple-element.245.refs_0_, bf16[192,512]{1,0:T(8,128)(2,1)S(1)} %copy-done.24, ...), custom_call_target="tpu_custom_call" | custom-call | flops 1048576 | bytes 1048576 | tf_op jit(solution)/shard_map/attend_back/pallas_call | solution.py:139
  232.1 2.1 fusion.32
  234.2 4.4 %collective-permute-start.35 = (bf16[2,2,96,768]{3,2,1,0:T(8,128)(2,1)}, bf16[2,2,96,768]{3,2,1,0:T(8,128)(2,1)}, u32[]{:S(2)}, u32[]{:S(2)}) collective-permute-start(bf16[2,2,96,768]{3,2,1,0:T(8,128)(2,1)} %fusion.32), channel_id=1, source_target_pairs={{0,2},{1,3},{2,0},{3,1},{4,6},{5,7},{6,4},{7,5},{8,10},{9,11},{10,... | collective-permute-start | bytes 1769480 | tf_op jit(solution)/shard_map/ppermute | solution.py:352
  238.6 1.8 add_convert_fusion.11
  240.8 2.4 slice.156.refs_3_
  243.2 2.0 fusion.29
  245.2 8.3 %attend_back.4.refs_5_ = bf16[4,192,512]{2,1,0:T(8,128)(2,1)S(1)} custom-call(s32[3]{0:T(128)S(1)} %copy-done.85, bf16[4,576,512]{2,1,0:T(8,128)(2,1)S(1)} %pad_maximum_fusion.qkv, bf16[4,64,512]{2,1,0:T(8,128)(2,1)S(1)} %copy-done.38, bf16[192,512]{1,0:T(8,128)(2,1)S(1)} %get-tuple-element.245.refs_0_, bf16[192,512]{1,0:T(8,128)(2,1)S(1)} %copy-done.25, ...), custom_call_target="tpu_custom_call" | custom-call | flops 1048576 | bytes 1048576 | tf_op jit(solution)/shard_map/attend_back/pallas_call | solution.py:139
  257.8 4.0 %collective-permute-start.38 = (bf16[2,2,96,768]{3,2,0,1:T(8,128)(2,1)S(1)}, bf16[2,2,96,768]{3,2,0,1:T(8,128)(2,1)S(1)}, u32[]{:S(2)}, u32[]{:S(2)}) collective-permute-start(bf16[2,2,96,768]{3,2,0,1:T(8,128)(2,1)S(1)} %fusion.31), channel_id=1, source_target_pairs={{0,1},{1,0},{2,3},{3,2},{4,5},{5,4},{6,7},{7,6},{8,9},{9,8},{10,11... | collective-permute-start | bytes 1769480 | tf_op jit(solution)/shard_map/ppermute | solution.py:352
  263.8 1.7 fusion.36
  265.8 8.5 %attend_back.5.refs_6_ = bf16[4,192,512]{2,1,0:T(8,128)(2,1)S(1)} custom-call(s32[3]{0:T(128)S(1)} %copy-done.89, bf16[4,576,512]{2,1,0:T(8,128)(2,1)S(1)} %pad_maximum_fusion.qkv, bf16[4,64,512]{2,1,0:T(8,128)(2,1)S(1)} %copy-done.35, bf16[192,512]{1,0:T(8,128)(2,1)S(1)} %get-tuple-element.245.refs_0_, bf16[192,512]{1,0:T(8,128)(2,1)S(1)} %copy-done.26, ...), custom_call_target="tpu_custom_call" | custom-call | flops 1048576 | bytes 1048576 | tf_op jit(solution)/shard_map/attend_back/pallas_call | solution.py:139
  274.3 4.5 %collective-permute-done.37 = bf16[2,96,768]{2,1,0:T(8,128)(2,1)S(1)} collective-permute-done((bf16[2,96,768]{2,1,0:T(8,128)(2,1)S(1)}, bf16[2,96,768]{2,1,0:T(8,128)(2,1)S(1)}, u32[]{:S(2)}, u32[]{:S(2)}) %collective-permute-start.37) | collective-permute-done | bytes 294944 | tf_op jit(solution)/shard_map/ppermute | solution.py:352
  285.6 3.7 %weight_grad.1 = bf16[768,768]{1,0:T(8,128)(2,1)S(1)} custom-call(s32[1]{0:T(128)} %bitcast.10.place, bf16[512,768]{1,0:T(8,128)(2,1)S(1)} %copy-done.12, bf16[512,768]{1,0:T(8,128)(2,1)S(1)} %copy-done.18, bf16[512,768]{1,0:T(8,128)(2,1)S(1)} %copy-done.14, bf16[512,768]{1,0:T(8,128)(2,1)S(1)} %copy-done.16, bf16[4,192,512]{2,1,0:T(8,128)(2,1)S(1)} %copy-done.8, ...), custom_call_target="tpu_custom_call" | custom-call | flops 1048576 | bytes 1048576 | tf_op jit(solution)/shard_map/weight_grad/pallas_call | solution.py:228
  289.3 2.0 collective-permute-done.40
  296.5 1.7 collective-permute-start.42
  298.2 9.5 %collective-permute-done.49 = bf16[2,2,96,768]{3,2,0,1:T(8,128)(2,1)} collective-permute-done((bf16[2,2,96,768]{3,2,0,1:T(8,128)(2,1)}, bf16[2,2,96,768]{3,2,0,1:T(8,128)(2,1)}, u32[]{:S(2)}, u32[]{:S(2)}) %collective-permute-start.49) | collective-permute-done | bytes 589856 | tf_op jit(solution)/shard_map/ppermute | solution.py:352
  311.0 1.8 collective-permute-start.48
  312.8 6.7 %collective-permute-done.50 = bf16[2,96,768]{2,1,0:T(8,128)(2,1)S(1)} collective-permute-done((bf16[2,96,768]{2,1,0:T(8,128)(2,1)S(1)}, bf16[2,96,768]{2,1,0:T(8,128)(2,1)S(1)}, u32[]{:S(2)}, u32[]{:S(2)}) %collective-permute-start.50) | collective-permute-done | bytes 294944 | tf_op jit(solution)/shard_map/ppermute | solution.py:352
  320.4 1.7 collective-permute-start.54
  322.4 1.6 add_convert_fusion.4
  324.0 5.0 %collective-permute-done.51 = bf16[96,768]{1,0:T(8,128)(2,1)S(1)} collective-permute-done((bf16[96,768]{1,0:T(8,128)(2,1)S(1)}, bf16[96,768]{1,0:T(8,128)(2,1)S(1)}, u32[]{:S(2)}, u32[]{:S(2)}) %collective-permute-start.51) | collective-permute-done | bytes 147488 | tf_op jit(solution)/shard_map/ppermute | solution.py:352
  331.1 3.6 all-to-all-start.3
  337.2 1.4 collective-permute-done.43
  340.1 2.5 collective-permute-done.44
  342.5 1.7 collective-permute-start.45
  344.3 3.2 collective-permute-done.45
  348.2 2.4 copy.149
  351.7 1.8 collective-permute-start.47
  353.6 1.7 collective-permute-start.52
  (465 shorter events, 98.7 us)
Async XLA Ops:
  4.1 33.7 %all-to-all-start = ((bf16[8,64,768]{2,1,0:T(8,128)(2,1)}), bf16[8,64,768]{2,1,0:T(8,128)(2,1)S(1)}, u32[]{:S(2)}, u32[]{:S(2)}) async-start(bf16[8,64,768]{2,1,0:T(8,128)(2,1)} %copy.123), calls=%async_computation | async-start | bytes 1572864 | tf_op jit(solution)/shard_map/all_to_all | solution.py:439
  12.7 28.7 %collective-permute-start = (bf16[96,896]{0,1:T(8,128)(2,1)S(1)}, bf16[96,896]{0,1:T(8,128)(2,1)S(1)}, u32[]{:S(2)}, u32[]{:S(2)}) collective-permute-start(bf16[96,896]{0,1:T(8,128)(2,1)S(1)} %concatenate.10), channel_id=1, source_target_pairs={{0,4},{1,5},{2,6},{3,7},{4,0},{5,1},{6,2},{7,3},{8,12},{9,13},{10,... | collective-permute-start | bytes 516104 | tf_op jit(solution)/shard_map/ppermute | solution.py:352
  17.2 62.4 %copy-start.84 = (s32[3]{0:T(128)}, s32[3]{0:T(128)S(1)}, u32[]{:S(2)}) copy-start(s32[3]{0:T(128)S(1)} %get-tuple-element.353.info) | copy-start | bytes 40
  17.2 113.1 %copy-start.86 = (s32[3]{0:T(128)}, s32[3]{0:T(128)S(1)}, u32[]{:S(2)}) copy-start(s32[3]{0:T(128)S(1)} %get-tuple-element.352.info) | copy-start | bytes 40
  18.2 50.6 %copy-start.114 = (pred[768]{0:T(1024)(128)(4,1)}, pred[768]{0:T(1024)(128)(4,1)S(1)}, u32[]{:S(2)}) copy-start(pred[768]{0:T(1024)(128)(4,1)S(1)} %iota.73) | copy-start | bytes 2308
  37.8 16.2 %collective-permute-start.4 = (bf16[512,768]{1,0:T(8,128)(2,1)S(1)}, bf16[512,768]{1,0:T(8,128)(2,1)S(1)}, u32[]{:S(2)}, u32[]{:S(2)}) collective-permute-start(bf16[512,768]{1,0:T(8,128)(2,1)S(1)} %bitcast.197), channel_id=1, source_target_pairs={{0,8},{8,0},{16,24},{24,16},{1,9},{9,1},{17,25},{25,17},{2,10},{10... | collective-permute-start | bytes 2359304 | tf_op jit(solution)/shard_map/ppermute | solution.py:352
  37.8 20.0 %collective-permute-start.3 = (bf16[512,768]{1,0:T(8,128)(2,1)S(1)}, bf16[512,768]{1,0:T(8,128)(2,1)S(1)}, u32[]{:S(2)}, u32[]{:S(2)}) collective-permute-start(bf16[512,768]{1,0:T(8,128)(2,1)S(1)} %bitcast.198), channel_id=1, source_target_pairs={{0,16},{8,24},{16,0},{24,8},{1,17},{9,25},{17,1},{25,9},{2,18},{10... | collective-permute-start | bytes 2359304 | tf_op jit(solution)/shard_map/ppermute | solution.py:352
  42.1 8.8 %collective-permute-start.1 = (bf16[2,96,896]{2,1,0:T(8,128)(2,1)S(1)}, bf16[2,96,896]{2,1,0:T(8,128)(2,1)S(1)}, u32[]{:S(2)}, u32[]{:S(2)}) collective-permute-start(bf16[2,96,896]{2,1,0:T(8,128)(2,1)S(1)} %broadcast_select_fusion.5), channel_id=1, source_target_pairs={{0,2},{1,3},{2,0},{3,1},{4,6},{5,7},{6,4},{7,5},{8,10},{9,11},{10,... | collective-permute-start | bytes 1032200 | tf_op jit(solution)/shard_map/ppermute | solution.py:352
  51.1 19.1 %collective-permute-start.6 = (bf16[2,96,768]{2,1,0:T(8,128)(2,1)}, bf16[2,96,768]{2,1,0:T(8,128)(2,1)S(1)}, u32[]{:S(2)}, u32[]{:S(2)}) collective-permute-start(bf16[2,96,768]{2,1,0:T(8,128)(2,1)} %pad_maximum_fusion.2), channel_id=1, source_target_pairs={{0,4},{1,5},{2,6},{3,7},{4,0},{5,1},{6,2},{7,3},{8,12},{9,13},{10,... | collective-permute-start | bytes 884744 | tf_op jit(solution)/shard_map/ppermute | solution.py:352
  52.1 16.8 %collective-permute-start.2 = (bf16[2,2,96,896]{3,2,1,0:T(8,128)(2,1)S(1)}, bf16[2,2,96,896]{3,2,1,0:T(8,128)(2,1)S(1)}, u32[]{:S(2)}, u32[]{:S(2)}) collective-permute-start(bf16[2,2,96,896]{3,2,1,0:T(8,128)(2,1)S(1)} %broadcast_select_fusion.2), channel_id=1, source_target_pairs={{0,1},{1,0},{2,3},{3,2},{4,5},{5,4},{6,7},{7,6},{8,9},{9,8},{10,11... | collective-permute-start | bytes 2064392 | tf_op jit(solution)/shard_map/ppermute | solution.py:352
  58.0 12.2 %collective-permute-start.5 = (bf16[512,768]{1,0:T(8,128)(2,1)S(1)}, bf16[512,768]{1,0:T(8,128)(2,1)S(1)}, u32[]{:S(2)}, u32[]{:S(2)}) collective-permute-start(bf16[512,768]{1,0:T(8,128)(2,1)S(1)} %collective-permute-done.3), channel_id=1, source_target_pairs={{0,8},{8,0},{16,24},{24,16},{1,9},{9,1},{17,25},{25,17},{2,10},{10... | collective-permute-start | bytes 2359304 | tf_op jit(solution)/shard_map/ppermute | solution.py:352
  70.7 17.4 %collective-permute-start.8 = (bf16[768,192]{1,0:T(8,128)(2,1)S(1)}, bf16[768,192]{1,0:T(8,128)(2,1)}, u32[]{:S(2)}, u32[]{:S(2)}) collective-permute-start(bf16[768,192]{1,0:T(8,128)(2,1)S(1)} %slice.158.refs_0_), channel_id=1, source_target_pairs={{0,16},{8,24},{16,0},{24,8},{1,17},{9,25},{17,1},{25,9},{2,18},{10... | collective-permute-start | bytes 884744 | tf_op jit(solution)/shard_map/ppermute | solution.py:352
  73.4 13.6 %collective-permute-start.7 = (bf16[2,2,96,768]{3,2,1,0:T(8,128)(2,1)S(1)}, bf16[2,2,96,768]{3,2,1,0:T(8,128)(2,1)S(1)}, u32[]{:S(2)}, u32[]{:S(2)}) collective-permute-start(bf16[2,2,96,768]{3,2,1,0:T(8,128)(2,1)S(1)} %broadcast_select_fusion.4), channel_id=1, source_target_pairs={{0,2},{1,3},{2,0},{3,1},{4,6},{5,7},{6,4},{7,5},{8,10},{9,11},{10,... | collective-permute-start | bytes 1769480 | tf_op jit(solution)/shard_map/ppermute | solution.py:352
  88.1 56.1 %all-to-all-start.1 = ((bf16[8,64,896]{2,1,0:T(8,128)(2,1)}), bf16[8,64,896]{2,1,0:T(8,128)(2,1)}, u32[]{:S(2)}, u32[]{:S(2)}) async-start(bf16[8,64,896]{2,1,0:T(8,128)(2,1)} %pad_maximum_fusion.1), calls=%async_computation.1 | async-start | bytes 1835008 | tf_op jit(solution)/shard_map/all_to_all | solution.py:439
  102.9 11.7 %collective-permute-start.9 = (bf16[768,192]{1,0:T(8,128)(2,1)S(1)}, bf16[768,192]{1,0:T(8,128)(2,1)S(1)}, u32[]{:S(2)}, u32[]{:S(2)}) collective-permute-start(bf16[768,192]{1,0:T(8,128)(2,1)S(1)} %slice.158.refs_0_), channel_id=1, source_target_pairs={{0,8},{8,0},{16,24},{24,16},{1,9},{9,1},{17,25},{25,17},{2,10},{10... | collective-permute-start | bytes 884744 | tf_op jit(solution)/shard_map/ppermute | solution.py:352
  103.0 11.6 %collective-permute-start.10 = (bf16[768,192]{1,0:T(8,128)(2,1)}, bf16[768,192]{1,0:T(8,128)(2,1)S(1)}, u32[]{:S(2)}, u32[]{:S(2)}) collective-permute-start(bf16[768,192]{1,0:T(8,128)(2,1)} %collective-permute-done.8.refs_1_), channel_id=1, source_target_pairs={{0,8},{8,0},{16,24},{24,16},{1,9},{9,1},{17,25},{25,17},{2,10},{10... | collective-permute-start | bytes 884744 | tf_op jit(solution)/shard_map/ppermute | solution.py:352
  105.6 30.6 %collective-permute-start.12 = (bf16[2,2,96,768]{3,2,1,0:T(8,128)(2,1)S(1)}, bf16[2,2,96,768]{3,2,1,0:T(8,128)(2,1)}, u32[]{:S(2)}, u32[]{:S(2)}) collective-permute-start(bf16[2,2,96,768]{3,2,1,0:T(8,128)(2,1)S(1)} %get-tuple-element.189), channel_id=1, source_target_pairs={{0,16},{8,24},{16,0},{24,8},{1,17},{9,25},{17,1},{25,9},{2,18},{10... | collective-permute-start | bytes 1769480 | tf_op jit(solution)/shard_map/ppermute | solution.py:352
  106.2 30.0 %collective-permute-start.11 = (bf16[2,2,96,768]{3,2,1,0:T(8,128)(2,1)S(1)}, bf16[2,2,96,768]{3,2,1,0:T(8,128)(2,1)S(1)}, u32[]{:S(2)}, u32[]{:S(2)}) collective-permute-start(bf16[2,2,96,768]{3,2,1,0:T(8,128)(2,1)S(1)} %get-tuple-element.168), channel_id=1, source_target_pairs={{0,1},{1,0},{2,3},{3,2},{4,5},{5,4},{6,7},{7,6},{8,9},{9,8},{10,11... | collective-permute-start | bytes 1769480 | tf_op jit(solution)/shard_map/ppermute | solution.py:352
  115.3 6.1 %collective-permute-start.15 = (bf16[64,512]{1,0:T(8,128)(2,1)S(1)}, bf16[64,512]{1,0:T(8,128)(2,1)S(1)}, u32[]{:S(2)}, u32[]{:S(2)}) collective-permute-start(bf16[64,512]{1,0:T(8,128)(2,1)S(1)} %get-tuple-element.342), channel_id=1, source_target_pairs={{0,24},{8,16},{16,8},{24,0},{1,25},{9,17},{17,9},{25,1},{2,26},{10... | collective-permute-start | bytes 196616 | tf_op jit(solution)/shard_map/ppermute | solution.py:352
  115.9 6.6 %collective-permute-start.14 = (bf16[64,512]{1,0:T(8,128)(2,1)S(1)}, bf16[64,512]{1,0:T(8,128)(2,1)S(1)}, u32[]{:S(2)}, u32[]{:S(2)}) collective-permute-start(bf16[64,512]{1,0:T(8,128)(2,1)S(1)} %get-tuple-element.343), channel_id=1, source_target_pairs={{0,8},{8,0},{16,24},{24,16},{1,9},{9,1},{17,25},{25,17},{2,10},{10... | collective-permute-start | bytes 196616 | tf_op jit(solution)/shard_map/ppermute | solution.py:352
  116.9 27.3 %collective-permute-start.22 = (bf16[2,2,96,768]{3,2,1,0:T(8,128)(2,1)S(1)}, bf16[2,2,96,768]{3,2,1,0:T(8,128)(2,1)}, u32[]{:S(2)}, u32[]{:S(2)}) collective-permute-start(bf16[2,2,96,768]{3,2,1,0:T(8,128)(2,1)S(1)} %get-tuple-element.189), channel_id=1, source_target_pairs={{0,1},{1,0},{2,3},{3,2},{4,5},{5,4},{6,7},{7,6},{8,9},{9,8},{10,11... | collective-permute-start | bytes 1769480 | tf_op jit(solution)/shard_map/ppermute | solution.py:352
  122.1 4.8 %collective-permute-start.13 = (bf16[64,512]{1,0:T(8,128)(2,1)S(1)}, bf16[64,512]{1,0:T(8,128)(2,1)S(1)}, u32[]{:S(2)}, u32[]{:S(2)}) collective-permute-start(bf16[64,512]{1,0:T(8,128)(2,1)S(1)} %get-tuple-element.344), channel_id=1, source_target_pairs={{0,16},{8,24},{16,0},{24,8},{1,17},{9,25},{17,1},{25,9},{2,18},{10... | collective-permute-start | bytes 196616 | tf_op jit(solution)/shard_map/ppermute | solution.py:352
  123.2 5.0 %collective-permute-start.18 = (bf16[64,512]{1,0:T(8,128)(2,1)S(1)}, bf16[64,512]{1,0:T(8,128)(2,1)S(1)}, u32[]{:S(2)}, u32[]{:S(2)}) collective-permute-start(bf16[64,512]{1,0:T(8,128)(2,1)S(1)} %get-tuple-element.338), channel_id=1, source_target_pairs={{0,24},{8,16},{16,8},{24,0},{1,25},{9,17},{17,9},{25,1},{2,26},{10... | collective-permute-start | bytes 196616 | tf_op jit(solution)/shard_map/ppermute | solution.py:352
  127.5 8.6 %collective-permute-start.17 = (bf16[64,512]{1,0:T(8,128)(2,1)S(1)}, bf16[64,512]{1,0:T(8,128)(2,1)S(1)}, u32[]{:S(2)}, u32[]{:S(2)}) collective-permute-start(bf16[64,512]{1,0:T(8,128)(2,1)S(1)} %get-tuple-element.339), channel_id=1, source_target_pairs={{0,8},{8,0},{16,24},{24,16},{1,9},{9,1},{17,25},{25,17},{2,10},{10... | collective-permute-start | bytes 196616 | tf_op jit(solution)/shard_map/ppermute | solution.py:352
  128.8 7.3 %collective-permute-start.16 = (bf16[64,512]{1,0:T(8,128)(2,1)S(1)}, bf16[64,512]{1,0:T(8,128)(2,1)S(1)}, u32[]{:S(2)}, u32[]{:S(2)}) collective-permute-start(bf16[64,512]{1,0:T(8,128)(2,1)S(1)} %get-tuple-element.340), channel_id=1, source_target_pairs={{0,16},{8,24},{16,0},{24,8},{1,17},{9,25},{17,1},{25,9},{2,18},{10... | collective-permute-start | bytes 196616 | tf_op jit(solution)/shard_map/ppermute | solution.py:352
  137.4 4.0 %collective-permute-start.21 = (bf16[64,512]{1,0:T(8,128)(2,1)S(1)}, bf16[64,512]{1,0:T(8,128)(2,1)S(1)}, u32[]{:S(2)}, u32[]{:S(2)}) collective-permute-start(bf16[64,512]{1,0:T(8,128)(2,1)S(1)} %get-tuple-element.334), channel_id=1, source_target_pairs={{0,24},{8,16},{16,8},{24,0},{1,25},{9,17},{17,9},{25,1},{2,26},{10... | collective-permute-start | bytes 196616 | tf_op jit(solution)/shard_map/ppermute | solution.py:352
  138.9 3.1 collective-permute-start.20
  139.3 4.3 %collective-permute-start.19 = (bf16[64,512]{1,0:T(8,128)(2,1)S(1)}, bf16[64,512]{1,0:T(8,128)(2,1)S(1)}, u32[]{:S(2)}, u32[]{:S(2)}) collective-permute-start(bf16[64,512]{1,0:T(8,128)(2,1)S(1)} %get-tuple-element.336), channel_id=1, source_target_pairs={{0,16},{8,24},{16,0},{24,8},{1,17},{9,25},{17,1},{25,9},{2,18},{10... | collective-permute-start | bytes 196616 | tf_op jit(solution)/shard_map/ppermute | solution.py:352
  144.3 29.7 %collective-permute-start.26 = (bf16[768,768]{1,0:T(8,128)(2,1)}, bf16[768,768]{1,0:T(8,128)(2,1)}, u32[]{:S(2)}, u32[]{:S(2)}) collective-permute-start(bf16[768,768]{1,0:T(8,128)(2,1)} %bitcast_select_fusion.3.wu), channel_id=1, source_target_pairs={{0,16},{8,24},{16,0},{24,8},{1,17},{9,25},{17,1},{25,9},{2,18},{10... | collective-permute-start | bytes 3538952 | tf_op jit(solution)/shard_map/ppermute | solution.py:352
  147.8 19.5 %collective-permute-start.24 = (bf16[512,768]{1,0:T(8,128)(2,1)}, bf16[512,768]{1,0:T(8,128)(2,1)}, u32[]{:S(2)}, u32[]{:S(2)}) collective-permute-start(bf16[512,768]{1,0:T(8,128)(2,1)} %slice.135.cot), channel_id=1, source_target_pairs={{0,8},{8,0},{16,24},{24,16},{1,9},{9,1},{17,25},{25,17},{2,10},{10... | collective-permute-start | bytes 2359304 | tf_op jit(solution)/shard_map/ppermute | solution.py:352
  152.5 14.7 %collective-permute-start.23 = (bf16[512,768]{1,0:T(8,128)(2,1)}, bf16[512,768]{1,0:T(8,128)(2,1)}, u32[]{:S(2)}, u32[]{:S(2)}) collective-permute-start(bf16[512,768]{1,0:T(8,128)(2,1)} %get-tuple-element.186.nm), channel_id=1, source_target_pairs={{0,8},{8,0},{16,24},{24,16},{1,9},{9,1},{17,25},{25,17},{2,10},{10... | collective-permute-start | bytes 2359304 | tf_op jit(solution)/shard_map/ppermute | solution.py:352
  153.0 21.0 %collective-permute-start.25 = (bf16[2,2,96,768]{3,2,1,0:T(8,128)(2,1)}, bf16[2,2,96,768]{3,2,1,0:T(8,128)(2,1)}, u32[]{:S(2)}, u32[]{:S(2)}) collective-permute-start(bf16[2,2,96,768]{3,2,1,0:T(8,128)(2,1)} %collective-permute-done.12), channel_id=1, source_target_pairs={{0,1},{1,0},{2,3},{3,2},{4,5},{5,4},{6,7},{7,6},{8,9},{9,8},{10,11... | collective-permute-start | bytes 1769480 | tf_op jit(solution)/shard_map/ppermute | solution.py:352
  183.1 13.0 %collective-permute-start.28 = (bf16[512,768]{1,0:T(8,128)(2,1)S(1)}, bf16[512,768]{1,0:T(8,128)(2,1)S(1)}, u32[]{:S(2)}, u32[]{:S(2)}) collective-permute-start(bf16[512,768]{1,0:T(8,128)(2,1)S(1)} %convert_element_type.480), channel_id=1, source_target_pairs={{0,8},{8,0},{16,24},{24,16},{1,9},{9,1},{17,25},{25,17},{2,10},{10... | collective-permute-start | bytes 2359304 | tf_op jit(solution)/shard_map/ppermute | solution.py:352
  183.2 13.0 %collective-permute-start.27 = (bf16[512,768]{1,0:T(8,128)(2,1)S(1)}, bf16[512,768]{1,0:T(8,128)(2,1)S(1)}, u32[]{:S(2)}, u32[]{:S(2)}) collective-permute-start(bf16[512,768]{1,0:T(8,128)(2,1)S(1)} %convert_element_type.479), channel_id=1, source_target_pairs={{0,8},{8,0},{16,24},{24,16},{1,9},{9,1},{17,25},{25,17},{2,10},{10... | collective-permute-start | bytes 2359304 | tf_op jit(solution)/shard_map/ppermute | solution.py:352
  193.7 38.5 %collective-permute-start.32 = (bf16[2,2,2,96,768]{4,3,0,1,2:T(8,128)(2,1)}, bf16[2,2,2,96,768]{4,3,0,1,2:T(8,128)(2,1)}, u32[]{:S(2)}, u32[]{:S(2)}) collective-permute-start(bf16[2,2,2,96,768]{4,3,0,1,2:T(8,128)(2,1)} %copy.136), channel_id=1, source_target_pairs={{0,1},{1,0},{2,3},{3,2},{4,5},{5,4},{6,7},{7,6},{8,9},{9,8},{10,11... | collective-permute-start | bytes 3538952 | tf_op jit(solution)/shard_map/ppermute | solution.py:352
  201.2 7.8 %collective-permute-start.31 = (bf16[192,512]{1,0:T(8,128)(2,1)S(1)}, bf16[192,512]{1,0:T(8,128)(2,1)S(1)}, u32[]{:S(2)}, u32[]{:S(2)}) collective-permute-start(bf16[192,512]{1,0:T(8,128)(2,1)S(1)} %get-tuple-element.326), channel_id=1, source_target_pairs={{0,24},{8,16},{16,8},{24,0},{1,25},{9,17},{17,9},{25,1},{2,26},{10... | collective-permute-start | bytes 589832 | tf_op jit(solution)/shard_map/ppermute | solution.py:352
  202.5 6.6 %collective-permute-start.30 = (bf16[192,512]{1,0:T(8,128)(2,1)S(1)}, bf16[192,512]{1,0:T(8,128)(2,1)S(1)}, u32[]{:S(2)}, u32[]{:S(2)}) collective-permute-start(bf16[192,512]{1,0:T(8,128)(2,1)S(1)} %get-tuple-element.327), channel_id=1, source_target_pairs={{0,8},{8,0},{16,24},{24,16},{1,9},{9,1},{17,25},{25,17},{2,10},{10... | collective-permute-start | bytes 589832 | tf_op jit(solution)/shard_map/ppermute | solution.py:352
  203.2 9.6 %collective-permute-start.29 = (bf16[192,512]{1,0:T(8,128)(2,1)S(1)}, bf16[192,512]{1,0:T(8,128)(2,1)S(1)}, u32[]{:S(2)}, u32[]{:S(2)}) collective-permute-start(bf16[192,512]{1,0:T(8,128)(2,1)S(1)} %get-tuple-element.328), channel_id=1, source_target_pairs={{0,16},{8,24},{16,0},{24,8},{1,17},{9,25},{17,1},{25,9},{2,18},{10... | collective-permute-start | bytes 589832 | tf_op jit(solution)/shard_map/ppermute | solution.py:352
  213.4 41.1 %all-to-all-start.2 = ((bf16[8,64,768]{2,1,0:T(8,128)(2,1)}), bf16[8,64,768]{2,1,0:T(8,128)(2,1)}, u32[]{:S(2)}, u32[]{:S(2)}) async-start(bf16[8,64,768]{2,1,0:T(8,128)(2,1)} %bitcast.204), calls=%async_computation.2 | async-start | bytes 1572864 | tf_op jit(solution)/shard_map/all_to_all | solution.py:439
  217.6 36.9 %collective-permute-start.34 = (bf16[768,768]{1,0:T(8,128)(2,1)}, bf16[768,768]{1,0:T(8,128)(2,1)}, u32[]{:S(2)}, u32[]{:S(2)}) collective-permute-start(bf16[768,768]{1,0:T(8,128)(2,1)} %add_convert_fusion.3), channel_id=1, source_target_pairs={{0,16},{8,24},{16,0},{24,8},{1,17},{9,25},{17,1},{25,9},{2,18},{10... | collective-permute-start | bytes 3538952 | tf_op jit(solution)/shard_map/ppermute | solution.py:352
  219.4 12.7 %collective-permute-start.33 = (bf16[768,192]{1,0:T(8,128)(2,1)}, bf16[768,192]{1,0:T(8,128)(2,1)}, u32[]{:S(2)}, u32[]{:S(2)}) collective-permute-start(bf16[768,192]{1,0:T(8,128)(2,1)} %copy-done.92), channel_id=1, source_target_pairs={{0,8},{8,0},{16,24},{24,16},{1,9},{9,1},{17,25},{25,17},{2,10},{10... | collective-permute-start | bytes 884744 | tf_op jit(solution)/shard_map/ppermute | solution.py:352
  234.2 20.3 %collective-permute-start.35 = (bf16[2,2,96,768]{3,2,1,0:T(8,128)(2,1)}, bf16[2,2,96,768]{3,2,1,0:T(8,128)(2,1)}, u32[]{:S(2)}, u32[]{:S(2)}) collective-permute-start(bf16[2,2,96,768]{3,2,1,0:T(8,128)(2,1)} %fusion.32), channel_id=1, source_target_pairs={{0,2},{1,3},{2,0},{3,1},{4,6},{5,7},{6,4},{7,5},{8,10},{9,11},{10,... | collective-permute-start | bytes 1769480 | tf_op jit(solution)/shard_map/ppermute | solution.py:352
  240.5 14.0 %collective-permute-start.36 = (bf16[768,192]{1,0:T(8,128)(2,1)}, bf16[768,192]{1,0:T(8,128)(2,1)}, u32[]{:S(2)}, u32[]{:S(2)}) collective-permute-start(bf16[768,192]{1,0:T(8,128)(2,1)} %add_convert_fusion.11), channel_id=1, source_target_pairs={{0,16},{8,24},{16,0},{24,8},{1,17},{9,25},{17,1},{25,9},{2,18},{10... | collective-permute-start | bytes 884744 | tf_op jit(solution)/shard_map/ppermute | solution.py:352
  257.8 21.0 %collective-permute-start.38 = (bf16[2,2,96,768]{3,2,0,1:T(8,128)(2,1)S(1)}, bf16[2,2,96,768]{3,2,0,1:T(8,128)(2,1)S(1)}, u32[]{:S(2)}, u32[]{:S(2)}) collective-permute-start(bf16[2,2,96,768]{3,2,0,1:T(8,128)(2,1)S(1)} %fusion.31), channel_id=1, source_target_pairs={{0,1},{1,0},{2,3},{3,2},{4,5},{5,4},{6,7},{7,6},{8,9},{9,8},{10,11... | collective-permute-start | bytes 1769480 | tf_op jit(solution)/shard_map/ppermute | solution.py:352
  262.9 15.9 %collective-permute-start.37 = (bf16[2,96,768]{2,1,0:T(8,128)(2,1)S(1)}, bf16[2,96,768]{2,1,0:T(8,128)(2,1)S(1)}, u32[]{:S(2)}, u32[]{:S(2)}) collective-permute-start(bf16[2,96,768]{2,1,0:T(8,128)(2,1)S(1)} %fusion.39), channel_id=1, source_target_pairs={{0,4},{1,5},{2,6},{3,7},{4,0},{5,1},{6,2},{7,3},{8,12},{9,13},{10,... | collective-permute-start | bytes 884744 | tf_op jit(solution)/shard_map/ppermute | solution.py:352
  281.6 12.5 %collective-permute-start.41 = (bf16[2,512,768]{2,1,0:T(8,128)(2,1)S(1)}, bf16[2,512,768]{2,1,0:T(8,128)(2,1)S(1)}, u32[]{:S(2)}, u32[]{:S(2)}) collective-permute-start(bf16[2,512,768]{2,1,0:T(8,128)(2,1)S(1)} %rows_grad.3), channel_id=1, source_target_pairs={{0,8},{8,0},{16,24},{24,16},{1,9},{9,1},{17,25},{25,17},{2,10},{10... | collective-permute-start | bytes 4718600 | tf_op jit(solution)/shard_map/ppermute | solution.py:352
  281.7 3.9 %collective-permute-start.39 = (bf16[768,192]{1,0:T(8,128)(2,1)S(1)}, bf16[768,192]{1,0:T(8,128)(2,1)S(1)}, u32[]{:S(2)}, u32[]{:S(2)}) collective-permute-start(bf16[768,192]{1,0:T(8,128)(2,1)S(1)} %copy-done.91), channel_id=1, source_target_pairs={{0,8},{8,0},{16,24},{24,16},{1,9},{9,1},{17,25},{25,17},{2,10},{10... | collective-permute-start | bytes 884744 | tf_op jit(solution)/shard_map/ppermute | solution.py:352
  282.3 9.1 %collective-permute-start.40 = (bf16[2,96,768]{2,1,0:T(8,128)(2,1)S(1)}, bf16[2,96,768]{2,1,0:T(8,128)(2,1)S(1)}, u32[]{:S(2)}, u32[]{:S(2)}) collective-permute-start(bf16[2,96,768]{2,1,0:T(8,128)(2,1)S(1)} %get-tuple-element.310), channel_id=1, source_target_pairs={{0,2},{1,3},{2,0},{3,1},{4,6},{5,7},{6,4},{7,5},{8,10},{9,11},{10,... | collective-permute-start | bytes 884744 | tf_op jit(solution)/shard_map/ppermute | solution.py:352
  293.0 14.8 %collective-permute-start.49 = (bf16[2,2,96,768]{3,2,0,1:T(8,128)(2,1)}, bf16[2,2,96,768]{3,2,0,1:T(8,128)(2,1)}, u32[]{:S(2)}, u32[]{:S(2)}) collective-permute-start(bf16[2,2,96,768]{3,2,0,1:T(8,128)(2,1)} %copy_bitcast_fusion.1), channel_id=1, source_target_pairs={{0,1},{1,0},{2,3},{3,2},{4,5},{5,4},{6,7},{7,6},{8,9},{9,8},{10,11... | collective-permute-start | bytes 1769480 | tf_op jit(solution)/shard_map/ppermute | solution.py:352
  296.5 22.9 %collective-permute-start.42 = (bf16[512,768]{1,0:T(8,128)(2,1)}, bf16[512,768]{1,0:T(8,128)(2,1)S(1)}, u32[]{:S(2)}, u32[]{:S(2)}) collective-permute-start(bf16[512,768]{1,0:T(8,128)(2,1)} %slice_bitcast_fusion), channel_id=1, source_target_pairs={{0,16},{8,24},{16,0},{24,8},{1,17},{9,25},{17,1},{25,9},{2,18},{10... | collective-permute-start | bytes 2359304 | tf_op jit(solution)/shard_map/ppermute | solution.py:352
  309.0 10.5 %collective-permute-start.50 = (bf16[2,96,768]{2,1,0:T(8,128)(2,1)S(1)}, bf16[2,96,768]{2,1,0:T(8,128)(2,1)S(1)}, u32[]{:S(2)}, u32[]{:S(2)}) collective-permute-start(bf16[2,96,768]{2,1,0:T(8,128)(2,1)S(1)} %get-tuple-element.306), channel_id=1, source_target_pairs={{0,2},{1,3},{2,0},{3,1},{4,6},{5,7},{6,4},{7,5},{8,10},{9,11},{10,... | collective-permute-start | bytes 884744 | tf_op jit(solution)/shard_map/ppermute | solution.py:352
  311.0 13.0 %collective-permute-start.48 = (bf16[96,768]{1,0:T(8,128)(2,1)}, bf16[96,768]{1,0:T(8,128)(2,1)S(1)}, u32[]{:S(2)}, u32[]{:S(2)}) collective-permute-start(bf16[96,768]{1,0:T(8,128)(2,1)} %get-tuple-element.332), channel_id=1, source_target_pairs={{0,4},{1,5},{2,6},{3,7},{4,0},{5,1},{6,2},{7,3},{8,12},{9,13},{10,... | collective-permute-start | bytes 442376 | tf_op jit(solution)/shard_map/ppermute | solution.py:352
  320.4 8.6 %collective-permute-start.54 = (bf16[96,768]{1,0:T(8,128)(2,1)S(1)}, bf16[96,768]{1,0:T(8,128)(2,1)S(1)}, u32[]{:S(2)}, u32[]{:S(2)}) collective-permute-start(bf16[96,768]{1,0:T(8,128)(2,1)S(1)} %slice_bitcast_fusion.9), channel_id=1, source_target_pairs={{0,16},{8,24},{16,0},{24,8},{1,17},{9,25},{17,1},{25,9},{2,18},{10... | collective-permute-start | bytes 442376 | tf_op jit(solution)/shard_map/ppermute | solution.py:352
  322.2 6.8 %collective-permute-start.51 = (bf16[96,768]{1,0:T(8,128)(2,1)S(1)}, bf16[96,768]{1,0:T(8,128)(2,1)S(1)}, u32[]{:S(2)}, u32[]{:S(2)}) collective-permute-start(bf16[96,768]{1,0:T(8,128)(2,1)S(1)} %get-tuple-element.330), channel_id=1, source_target_pairs={{0,4},{1,5},{2,6},{3,7},{4,0},{5,1},{6,2},{7,3},{8,12},{9,13},{10,... | collective-permute-start | bytes 442376 | tf_op jit(solution)/shard_map/ppermute | solution.py:352
  329.7 6.7 %collective-permute-start.55 = (bf16[2,96,768]{2,1,0:T(8,128)(2,1)S(1)}, bf16[2,96,768]{2,1,0:T(8,128)(2,1)S(1)}, u32[]{:S(2)}, u32[]{:S(2)}) collective-permute-start(bf16[2,96,768]{2,1,0:T(8,128)(2,1)S(1)} %pad_maximum_fusion.3), channel_id=1, source_target_pairs={{0,16},{8,24},{16,0},{24,8},{1,17},{9,25},{17,1},{25,9},{2,18},{10... | collective-permute-start | bytes 884744 | tf_op jit(solution)/shard_map/ppermute | solution.py:352
  331.1 20.7 %all-to-all-start.3 = ((bf16[8,64,768]{2,1,0:T(8,128)(2,1)}), bf16[8,64,768]{2,1,0:T(8,128)(2,1)S(1)}, u32[]{:S(2)}, u32[]{:S(2)}) async-start(bf16[8,64,768]{2,1,0:T(8,128)(2,1)} %bitcast.67), calls=%async_computation.3 | async-start | bytes 1572864 | tf_op jit(solution)/shard_map/all_to_all | solution.py:439
  336.5 14.7 %collective-permute-start.56 = (bf16[2,2,96,768]{3,2,0,1:T(8,128)(2,1)S(1)}, bf16[2,2,96,768]{3,2,0,1:T(8,128)(2,1)S(1)}, u32[]{:S(2)}, u32[]{:S(2)}) collective-permute-start(bf16[2,2,96,768]{3,2,0,1:T(8,128)(2,1)S(1)} %broadcast_select_fusion.3), channel_id=1, source_target_pairs={{0,8},{8,0},{16,24},{24,16},{1,9},{9,1},{17,25},{25,17},{2,10},{10... | collective-permute-start | bytes 1769480 | tf_op jit(solution)/shard_map/ppermute | solution.py:352
  336.7 2.0 collective-permute-start.43
  338.7 3.8 %collective-permute-start.44 = (f32[8,768]{1,0:T(8,128)S(1)}, f32[8,768]{1,0:T(8,128)S(1)}, u32[]{:S(2)}, u32[]{:S(2)}) collective-permute-start(f32[8,768]{1,0:T(8,128)S(1)} %fusion.69), channel_id=1, source_target_pairs={{0,16},{8,24},{16,0},{24,8},{1,17},{9,25},{17,1},{25,9},{2,18},{10... | collective-permute-start | bytes 73736 | tf_op jit(solution)/shard_map/ppermute | solution.py:352
  342.5 4.9 %collective-permute-start.45 = (f32[8,768]{1,0:T(8,128)S(1)}, f32[8,768]{1,0:T(8,128)S(1)}, u32[]{:S(2)}, u32[]{:S(2)}) collective-permute-start(f32[8,768]{1,0:T(8,128)S(1)} %add.261), channel_id=1, source_target_pairs={{0,1},{1,0},{2,3},{3,2},{4,5},{5,4},{6,7},{7,6},{8,9},{9,8},{10,11... | collective-permute-start | bytes 73736 | tf_op jit(solution)/shard_map/ppermute | solution.py:352
  347.4 3.8 %collective-permute-start.46 = (f32[8,768]{1,0:T(8,128)S(1)}, f32[8,768]{1,0:T(8,128)S(1)}, u32[]{:S(2)}, u32[]{:S(2)}) collective-permute-start(f32[8,768]{1,0:T(8,128)S(1)} %add.262), channel_id=1, source_target_pairs={{0,2},{1,3},{2,0},{3,1},{4,6},{5,7},{6,4},{7,5},{8,10},{9,11},{10,... | collective-permute-start | bytes 73736 | tf_op jit(solution)/shard_map/ppermute | solution.py:352
  351.7 7.4 %collective-permute-start.47 = (f32[8,768]{1,0:T(8,128)S(1)}, f32[8,768]{1,0:T(8,128)S(1)}, u32[]{:S(2)}, u32[]{:S(2)}) collective-permute-start(f32[8,768]{1,0:T(8,128)S(1)} %add.263), channel_id=1, source_target_pairs={{0,4},{1,5},{2,6},{3,7},{4,0},{5,1},{6,2},{7,3},{8,12},{9,13},{10,... | collective-permute-start | bytes 73736 | tf_op jit(solution)/shard_map/ppermute | solution.py:352
  353.6 5.6 %collective-permute-start.52 = (bf16[96,768]{1,0:T(8,128)(2,1)S(1)}, bf16[96,768]{1,0:T(8,128)(2,1)S(1)}, u32[]{:S(2)}, u32[]{:S(2)}) collective-permute-start(bf16[96,768]{1,0:T(8,128)(2,1)S(1)} %add_convert_fusion.17), channel_id=1, source_target_pairs={{0,16},{8,24},{16,0},{24,8},{1,17},{9,25},{17,1},{25,9},{2,18},{10... | collective-permute-start | bytes 442376 | tf_op jit(solution)/shard_map/ppermute | solution.py:352
  359.3 1.6 collective-permute-start.53
  (123 other events, 682.5 us)
where the time goes:
time: 367 us; the launch traced here: 362 us
  starting transfers between devices  94.1 us (26%)
  Pallas kernels  89.8 us (24%)
  waiting for transfers between devices  87.5 us (24%)
  local copies, waits for them, and re-layouts  46.6 us (13%)
  other arithmetic  35.7 us (10%)
  matrix products  6.01 us (2%)
    ppermute x57, waiting for transfers between devices, swap(): return lax.ppermute(value, axis, [(i, i ^ bit) for i in range(count)])  70.4 us
    ppermute x57, starting transfers between devices, swap(): return lax.ppermute(value, axis, [(i, i ^ bit) for i in range(count)])  64.2 us
    all_to_all x4, starting transfers between devices, per_device(): lax.all_to_all(a, 'fsdp', split_axis=0, concat_axis=0, tiled=True)  29.9 us
    pallas_call x4, Pallas kernels, mlp_part(): pl.pallas_call(functools.partial(mlp_body, begun=bool(sums)), grid=(ff //...  27.5 us
    unnamed x258, local copies, waits for them, and re-layouts  27.5 us
    pallas_call x3, Pallas kernels, attend_back(): pl.pallas_call(functools.partial(attend_back_body, blocks=blocks, blk=blk...  25.1 us
    pallas_call x10, Pallas kernels, row_call(): pl.pallas_call(body, grid=(steps,), in_specs=[pl.BlockSpec(memory_space=p...  20 us
    all_to_all x4, waiting for transfers between devices, per_device(): lax.all_to_all(a, 'fsdp', split_axis=0, concat_axis=0, tiled=True)  17.1 us
  transfers between devices with their start and end apart: 61, of which 25 were waited for; matrix products, arithmetic and copies ran while one was open for 16% of the time, Pallas kernels for 22%

commit v1 on v0

--- a/solution.py
+++ b/solution.py
@@ -254,8 +254,8 @@
 
 
 def turn_body(place, residual, sum_near, sum_far, grad_near, grad_far, cot, gain, w, *refs):
-    result, d_residual, d_branch, d_gain, d_heads = refs
-    part = d_heads.shape[1]
+    result, d_residual, d_branch, d_gain, *d_heads = refs
+    part = d_heads[0].shape[0]
     result[...] = (residual[...] + sum_near[...] + sum_far[...].astype(jnp.float32)).astype(jnp.bfloat16)
     z, inverse = norm_stats(residual[...])
     back, gain_part = norm_back(z, inverse, gain[...], grad_near[...] + grad_far[...].astype(jnp.float32))
@@ -268,7 +268,7 @@
     d_residual[...] = cot[...].astype(jnp.float32) + back
     d_branch[...] = d_residual[...].astype(jnp.bfloat16)
     for s in range(4):
-        d_heads[s] = dotg(w[rows_at(place, s, part), :], d_branch[...], 1, 1).astype(jnp.bfloat16)
+        d_heads[s][...] = dotg(w[rows_at(place, s, part), :], d_branch[...], 1, 1).astype(jnp.bfloat16)
 
 
 def join_columns_body(place, *refs):
@@ -306,7 +306,7 @@
     *heads, w, out = refs
     for s in range(out.shape[0]):
         grad = jnp.concatenate([h[s] for h in heads], axis=0)
-        out[s] = dotg(grad, w[...], 0, 1).astype(jnp.bfloat16)
+        out[s] = dotg(grad, w[:, : grad.shape[0]], 0, 1).astype(jnp.bfloat16)
 
 
 def weight_grad_body(place, *refs):
@@ -535,15 +535,15 @@
     up_2 = add(up_2, d_up_2)
     down = jnp.stack((add(down_0, down_1), add(down_2, d_down_2))).reshape(2, *sizes, ff_each, width)
     down = halve(down, "fsdp", low, last + 1)
-    head_rows = jax.ShapeDtypeStruct((parts, part, span), bf16)
-    result, d_residual, d_branch, d_gain_mlp, d_heads = row_call(
+    head_rows = jax.ShapeDtypeStruct((part, span), bf16)
+    result, d_residual, d_branch, d_gain_mlp, *d_heads = row_call(
         turn_body,
         "turn",
-        [rows_bf16, rows_f32, rows_bf16, jax.ShapeDtypeStruct((1, width), f32), head_rows],
+        [rows_bf16, rows_f32, rows_bf16, jax.ShapeDtypeStruct((1, width), f32)] + [head_rows] * parts,
         place,
         [residual, near[0], far[0], near[1], far[1], cot, gain_two[None], w_out_full],
         [0] * 6 + [None] * 2,
-        [0, 0, 0, None, 2],
+        [0, 0, 0, None] + [1] * parts,
         parts,
     )
     d_heads = across(d_heads)
@@ -577,7 +577,7 @@
     d_qkv, down, up = lax.optimization_barrier((d_qkv, down, up))
 
     half = jax.ShapeDtypeStruct((2, span, width), bf16)
-    project_back = lambda a: row_call(rows_grad_body, "rows_grad", [half], place, [*a, wq], [None] * (heads + 1), [None])[0]
+    project_back = lambda a: row_call(rows_grad_body, "rows_grad", [half], place, [*a, packet], [None] * (heads + 1), [None])[0]
     d_far = swap(project_back([d[2:] for d in d_qkv]), "seq", 1)
     d_near = project_back([d[:2] for d in d_qkv])
     (d_tail,) = after(d_near, d_qkv)

time: 367 us -> 366 us (level)
  Pallas kernels: 89.8 us -> 104 us
  starting transfers between devices: 94.1 us -> 83.3 us
    ppermute x57, starting transfers between devices: 64.2 us -> 52.6 us  [swap(): return lax.ppermute(value, axis, [(i, i ^ bit) for i in range(count)])]
    pallas_call x3, Pallas kernels: 25.1 us -> 32.9 us  [attend_back(): pl.pallas_call(functools.partial(attend_back_body, blocks=blocks, blk=blk...]
    pallas_call x3, Pallas kernels: 17.1 us -> 23.2 us  [attend(): pl.pallas_call(functools.partial(attend_body, blk=blk), grid_spec=pltpu.P...]
    unnamed x258 -> x256, local copies, waits for them, and re-layouts: 27.5 us -> 28.8 us
  transfers between devices with their start and end apart: 61 -> 61, of which waited for: 25 -> 25; matrix products, arithmetic and copies ran while one was open for 16% -> 15% of each run, Pallas kernels for 22% -> 26%
where the time goes in v1:
time: 366 us; the launch traced here: 361 us
  Pallas kernels  104 us (28%)
  waiting for transfers between devices  84.7 us (23%)
  starting transfers between devices  83.3 us (23%)
  local copies, waits for them, and re-layouts  45.4 us (12%)
  other arithmetic  35.5 us (10%)
  matrix products  6.01 us (2%)
    ppermute x57, waiting for transfers between devices, swap(): return lax.ppermute(value, axis, [(i, i ^ bit) for i in range(count)])  67.5 us
    ppermute x57, starting transfers between devices, swap(): return lax.ppermute(value, axis, [(i, i ^ bit) for i in range(count)])  52.6 us
    pallas_call x3, Pallas kernels, attend_back(): pl.pallas_call(functools.partial(attend_back_body, blocks=blocks, blk=blk...  32.9 us
    all_to_all x4, starting transfers between devices, per_device(): lax.all_to_all(a, 'fsdp', split_axis=0, concat_axis=0, tiled=True)  30.7 us
    unnamed x256, local copies, waits for them, and re-layouts  28.8 us
    pallas_call x4, Pallas kernels, mlp_part(): pl.pallas_call(functools.partial(mlp_body, begun=bool(sums)), grid=(ff //...  27.5 us
    pallas_call x3, Pallas kernels, attend(): pl.pallas_call(functools.partial(attend_body, blk=blk), grid_spec=pltpu.P...  23.2 us
    pallas_call x10, Pallas kernels, row_call(): pl.pallas_call(body, grid=(steps,), in_specs=[pl.BlockSpec(memory_space=p...  20.1 us
  transfers between devices with their start and end apart: 61, of which 25 were waited for; matrix products, arithmetic and copies ran while one was open for 15% of the time, Pallas kernels for 26%

profile of v1, /device:TPU:0, one launch (start us, length us, event | category | flops | bytes accessed | tf_op | source)
XLA Modules:
  0.0 361.2 jit_solution(15394438751718372139)
XLA Ops:
  1.5 1.6 fusion.18
  4.1 7.3 %all-to-all-start = ((bf16[8,64,768]{2,1,0:T(8,128)(2,1)}), bf16[8,64,768]{2,1,0:T(8,128)(2,1)S(1)}, u32[]{:S(2)}, u32[]{:S(2)}) async-start(bf16[8,64,768]{2,1,0:T(8,128)(2,1)} %copy.123), calls=%async_computation | async-start | bytes 1572864 | tf_op jit(solution)/shard_map/all_to_all | solution.py:439
  12.7 3.0 collective-permute-start
  20.7 17.2 %all-to-all-done = bf16[8,64,768]{2,1,0:T(8,128)(2,1)S(1)} async-done(((bf16[8,64,768]{2,1,0:T(8,128)(2,1)}), bf16[8,64,768]{2,1,0:T(8,128)(2,1)S(1)}, u32[]{:S(2)}, u32[]{:S(2)}) %all-to-all-start) | async-done | bytes 786464 | tf_op jit(solution)/shard_map/all_to_all | solution.py:439
  37.8 1.5 collective-permute-start.3
  39.3 2.1 collective-permute-done
  42.6 8.3 %collective-permute-done.1 = bf16[2,96,896]{2,1,0:T(8,128)(2,1)S(1)} collective-permute-done((bf16[2,96,896]{2,1,0:T(8,128)(2,1)S(1)}, bf16[2,96,896]{2,1,0:T(8,128)(2,1)S(1)}, u32[]{:S(2)}, u32[]{:S(2)}) %collective-permute-start.1) | collective-permute-done | bytes 344096 | tf_op jit(solution)/shard_map/ppermute | solution.py:352
  52.1 2.0 collective-permute-start.2
  54.3 3.5 collective-permute-done.3
  58.8 10.0 %collective-permute-done.2 = bf16[2,2,96,896]{3,2,1,0:T(8,128)(2,1)S(1)} collective-permute-done((bf16[2,2,96,896]{3,2,1,0:T(8,128)(2,1)S(1)}, bf16[2,2,96,896]{3,2,1,0:T(8,128)(2,1)S(1)}, u32[]{:S(2)}, u32[]{:S(2)}) %collective-permute-start.2) | collective-permute-done | bytes 688160 | tf_op jit(solution)/shard_map/ppermute | solution.py:352
  70.7 1.6 collective-permute-start.8
  73.4 1.5 collective-permute-start.7
  79.6 7.7 %attend.3 = (bf16[4,64,512]{2,1,0:T(8,128)(2,1)S(1)}, f32[4,1,512]{2,1,0:T(1,128)S(1)}) custom-call(s32[3]{0:T(128)S(1)} %get-tuple-element.355.info, bf16[4,576,512]{2,1,0:T(8,128)(2,1)S(1)} %pad_maximum_fusion.qkv), custom_call_target="tpu_custom_call" | custom-call | flops 1048576 | bytes 1048576 | tf_op jit(solution)/shard_map/attend/pallas_call | solution.py:61
  89.2 14.8 %all-to-all-start.1 = ((bf16[8,64,896]{2,1,0:T(8,128)(2,1)}), bf16[8,64,896]{2,1,0:T(8,128)(2,1)}, u32[]{:S(2)}, u32[]{:S(2)}) async-start(bf16[8,64,896]{2,1,0:T(8,128)(2,1)} %pad_maximum_fusion.1), calls=%async_computation.1 | async-start | bytes 1835008 | tf_op jit(solution)/shard_map/all_to_all | solution.py:439
  107.2 1.7 collective-permute-start.11
  108.9 7.7 %attend.4 = (bf16[4,64,512]{2,1,0:T(8,128)(2,1)S(1)}, f32[4,1,512]{2,1,0:T(1,128)S(1)}) custom-call(s32[3]{0:T(128)S(1)} %pad_add_fusion.3.info, bf16[4,576,512]{2,1,0:T(8,128)(2,1)S(1)} %pad_maximum_fusion.qkv), custom_call_target="tpu_custom_call" | custom-call | flops 1048576 | bytes 1048576 | tf_op jit(solution)/shard_map/attend/pallas_call | solution.py:61
  119.9 2.5 collective-permute-done.15.refs_7_
  124.5 1.6 collective-permute-start.18
  126.1 1.9 collective-permute-done.13.refs_5_
  131.4 7.7 %attend.5 = (bf16[4,64,512]{2,1,0:T(8,128)(2,1)S(1)}, f32[4,1,512]{2,1,0:T(1,128)S(1)}) custom-call(s32[3]{0:T(128)S(1)} %get-tuple-element.354.info, bf16[4,576,512]{2,1,0:T(8,128)(2,1)S(1)} %pad_maximum_fusion.qkv), custom_call_target="tpu_custom_call" | custom-call | flops 1048576 | bytes 1048576 | tf_op jit(solution)/shard_map/attend/pallas_call | solution.py:61
  140.4 1.6 collective-permute-start.21
  148.9 2.1 slice.123.cot
  151.1 3.4 project_out.1
  156.2 1.6 collective-permute-start.25
  157.8 1.5 bitcast_select_fusion.2.wd
  159.4 6.7 %mlp_part.5 = (f32[512,768]{1,0:T(8,128)S(1)}, f32[512,768]{1,0:T(8,128)S(1)}, bf16[768,768]{1,0:T(8,128)(2,1)S(1)}, bf16[768,768]{1,0:T(8,128)(2,1)S(1)}) custom-call(bf16[512,768]{1,0:T(8,128)(2,1)} %get-tuple-element.189.nm, bf16[512,768]{1,0:T(8,128)(2,1)} %slice.123.cot, bf16[768,768]{1,0:T(8,128)(2,1)S(1)} %copy-done.7, ...), custom_call_target="tpu_custom_call" | custom-call | flops 1048576 | bytes 1048576 | tf_op jit(solution)/shard_map/mlp_part/pallas_call | solution.py:201
  167.2 6.7 %mlp_part.4 = (f32[512,768]{1,0:T(8,128)S(1)}, f32[512,768]{1,0:T(8,128)S(1)}, bf16[768,768]{1,0:T(8,128)(2,1)S(1)}, bf16[768,768]{1,0:T(8,128)(2,1)S(1)}) custom-call(bf16[512,768]{1,0:T(8,128)(2,1)} %collective-permute-done.23.nm, bf16[512,768]{1,0:T(8,128)(2,1)} %collective-permute-done.24.cot, bf16[768,768]{1,0:T(8,128)(2,1)S(1)} %copy-done.7, ...), custom_call_target="tpu_custom_call" | custom-call | flops 1048576 | bytes 1048576 | tf_op jit(solution)/shard_map/mlp_part/pallas_call | solution.py:201
  176.7 7.0 %mlp_part.7 = (f32[512,768]{1,0:T(8,128)S(1)}, f32[512,768]{1,0:T(8,128)S(1)}, bf16[768,768]{1,0:T(8,128)(2,1)S(1)}, bf16[768,768]{1,0:T(8,128)(2,1)S(1)}) custom-call(bf16[512,768]{1,0:T(8,128)(2,1)} %collective-permute-done.23.nm, bf16[512,768]{1,0:T(8,128)(2,1)} %collective-permute-done.24.cot, ...), custom_call_target="tpu_custom_call", output_to_operand_aliasing={{0}: (4, {}), {1}: (5, {})} | custom-call | flops 1048576 | bytes 1048576 | tf_op jit(solution)/shard_map/mlp_part/pallas_call | solution.py:201
  184.8 7.0 %mlp_part.6 = (f32[512,768]{1,0:T(8,128)S(1)}, f32[512,768]{1,0:T(8,128)S(1)}, bf16[768,768]{1,0:T(8,128)(2,1)S(1)}, bf16[768,768]{1,0:T(8,128)(2,1)S(1)}) custom-call(bf16[512,768]{1,0:T(8,128)(2,1)} %get-tuple-element.189.nm, bf16[512,768]{1,0:T(8,128)(2,1)} %slice.123.cot, ...), custom_call_target="tpu_custom_call", output_to_operand_aliasing={{0}: (4, {}), {1}: (5, {})} | custom-call | flops 1048576 | bytes 1048576 | tf_op jit(solution)/shard_map/mlp_part/pallas_call | solution.py:201
  194.4 1.8 collective-permute-start.32
  196.2 5.0 %turn.1 = (bf16[512,768]{1,0:T(8,128)(2,1)S(1)}, f32[512,768]{1,0:T(8,128)S(1)}, bf16[512,768]{1,0:T(8,128)(2,1)S(1)}, f32[1,768]{1,0:T(1,128)S(1)}, bf16[192,51...) custom-call(s32[1]{0:T(128)} %bitcast.10.place, ...), custom_call_target="tpu_custom_call" | custom-call | flops 1048576 | bytes 1048576 | tf_op jit(solution)/shard_map/turn/pallas_call | solution.py:228
  201.3 1.7 collective-permute-start.29
  209.8 1.5 collective-permute-done.31.refs_3_
  212.0 5.0 %all-to-all-start.2 = ((bf16[8,64,768]{2,1,0:T(8,128)(2,1)}), bf16[8,64,768]{2,1,0:T(8,128)(2,1)}, u32[]{:S(2)}, u32[]{:S(2)}) async-start(bf16[8,64,768]{2,1,0:T(8,128)(2,1)} %bitcast.196), calls=%async_computation.2 | async-start | bytes 1572864 | tf_op jit(solution)/shard_map/all_to_all | solution.py:439
  217.0 1.6 collective-permute-start.34
  222.6 10.9 %attend_back.3.refs_4_ = bf16[4,192,512]{2,1,0:T(8,128)(2,1)S(1)} custom-call(s32[3]{0:T(128)S(1)} %copy-done.88, bf16[4,576,512]{2,1,0:T(8,128)(2,1)S(1)} %pad_maximum_fusion.qkv, bf16[4,64,512]{2,1,0:T(8,128)(2,1)S(1)} %copy-done.41, bf16[192,512]{1,0:T(8,128)(2,1)S(1)} %get-tuple-element.251.refs_0_, ...), custom_call_target="tpu_custom_call" | custom-call | flops 1048576 | bytes 1048576 | tf_op jit(solution)/shard_map/attend_back/pallas_call | solution.py:139
  234.4 2.1 fusion.36
  237.4 1.8 add_convert_fusion.11
  239.5 2.3 fusion.33
  241.8 10.9 %attend_back.4.refs_5_ = bf16[4,192,512]{2,1,0:T(8,128)(2,1)S(1)} custom-call(s32[3]{0:T(128)S(1)} %copy-done.86, bf16[4,576,512]{2,1,0:T(8,128)(2,1)S(1)} %pad_maximum_fusion.qkv, bf16[4,64,512]{2,1,0:T(8,128)(2,1)S(1)} %copy-done.39, bf16[192,512]{1,0:T(8,128)(2,1)S(1)} %get-tuple-element.251.refs_0_, ...), custom_call_target="tpu_custom_call" | custom-call | flops 1048576 | bytes 1048576 | tf_op jit(solution)/shard_map/attend_back/pallas_call | solution.py:139
  254.3 1.4 constant_dynamic-slice_fusion.3
  257.6 1.8 collective-permute-start.38
  260.5 2.4 collective-permute-start.37
  262.9 1.7 fusion.40
  264.9 11.1 %attend_back.5.refs_6_ = bf16[4,192,512]{2,1,0:T(8,128)(2,1)S(1)} custom-call(s32[3]{0:T(128)S(1)} %copy-done.90, bf16[4,576,512]{2,1,0:T(8,128)(2,1)S(1)} %pad_maximum_fusion.qkv, bf16[4,64,512]{2,1,0:T(8,128)(2,1)S(1)} %copy-done.36, bf16[192,512]{1,0:T(8,128)(2,1)S(1)} %get-tuple-element.251.refs_0_, ...), custom_call_target="tpu_custom_call" | custom-call | flops 1048576 | bytes 1048576 | tf_op jit(solution)/shard_map/attend_back/pallas_call | solution.py:139
  281.4 1.4 rows_grad.2
  284.1 3.7 %weight_grad.1 = bf16[768,768]{1,0:T(8,128)(2,1)S(1)} custom-call(s32[1]{0:T(128)} %bitcast.10.place, bf16[512,768]{1,0:T(8,128)(2,1)S(1)} %copy-done.13, bf16[512,768]{1,0:T(8,128)(2,1)S(1)} %copy-done.19, bf16[512,768]{1,0:T(8,128)(2,1)S(1)} %copy-done.15, bf16[512,768]{1,0:T(8,128)(2,1)S(1)} %copy-done.17, bf16[4,192,512]{2,1,0:T(8,128)(2,1)S(1)} %copy-done.9, ...), custom_call_target="tpu_custom_call" | custom-call | flops 1048576 | bytes 1048576 | tf_op jit(solution)/shard_map/weight_grad/pallas_call | solution.py:228
  287.8 2.0 collective-permute-done.40
  294.7 1.7 collective-permute-start.42
  296.4 9.8 %collective-permute-done.49 = bf16[2,2,96,768]{3,2,0,1:T(8,128)(2,1)} collective-permute-done((bf16[2,2,96,768]{3,2,0,1:T(8,128)(2,1)}, bf16[2,2,96,768]{3,2,0,1:T(8,128)(2,1)}, u32[]{:S(2)}, u32[]{:S(2)}) %collective-permute-start.49) | collective-permute-done | bytes 589856 | tf_op jit(solution)/shard_map/ppermute | solution.py:352
  309.2 2.1 collective-permute-start.48
  311.3 6.6 %collective-permute-done.50 = bf16[2,96,768]{2,1,0:T(8,128)(2,1)S(1)} collective-permute-done((bf16[2,96,768]{2,1,0:T(8,128)(2,1)S(1)}, bf16[2,96,768]{2,1,0:T(8,128)(2,1)S(1)}, u32[]{:S(2)}, u32[]{:S(2)}) %collective-permute-start.50) | collective-permute-done | bytes 294944 | tf_op jit(solution)/shard_map/ppermute | solution.py:352
  318.9 1.8 collective-permute-start.54
  321.1 1.6 add_convert_fusion.4
  322.7 5.0 %collective-permute-done.51 = bf16[96,768]{1,0:T(8,128)(2,1)S(1)} collective-permute-done((bf16[96,768]{1,0:T(8,128)(2,1)S(1)}, bf16[96,768]{1,0:T(8,128)(2,1)S(1)}, u32[]{:S(2)}, u32[]{:S(2)}) %collective-permute-start.51) | collective-permute-done | bytes 147488 | tf_op jit(solution)/shard_map/ppermute | solution.py:352
  329.6 3.7 %all-to-all-start.3 = ((bf16[8,64,768]{2,1,0:T(8,128)(2,1)}), bf16[8,64,768]{2,1,0:T(8,128)(2,1)S(1)}, u32[]{:S(2)}, u32[]{:S(2)}) async-start(bf16[8,64,768]{2,1,0:T(8,128)(2,1)} %bitcast.63), calls=%async_computation.3 | async-start | bytes 1572864 | tf_op jit(solution)/shard_map/all_to_all | solution.py:439
  335.9 1.4 collective-permute-done.43
  337.5 1.4 collective-permute-start.44
  338.9 2.4 collective-permute-done.44
  341.3 1.6 collective-permute-start.45
  342.9 3.3 collective-permute-done.45
  346.8 2.4 copy.149
  350.5 1.7 collective-permute-start.47
  352.2 2.0 collective-permute-start.52
  (461 shorter events, 96.8 us)
Async XLA Ops:
  4.1 33.7 %all-to-all-start = ((bf16[8,64,768]{2,1,0:T(8,128)(2,1)}), bf16[8,64,768]{2,1,0:T(8,128)(2,1)S(1)}, u32[]{:S(2)}, u32[]{:S(2)}) async-start(bf16[8,64,768]{2,1,0:T(8,128)(2,1)} %copy.123), calls=%async_computation | async-start | bytes 1572864 | tf_op jit(solution)/shard_map/all_to_all | solution.py:439
  12.7 28.7 %collective-permute-start = (bf16[96,896]{0,1:T(8,128)(2,1)S(1)}, bf16[96,896]{0,1:T(8,128)(2,1)S(1)}, u32[]{:S(2)}, u32[]{:S(2)}) collective-permute-start(bf16[96,896]{0,1:T(8,128)(2,1)S(1)} %concatenate.10), channel_id=1, source_target_pairs={{0,4},{1,5},{2,6},{3,7},{4,0},{5,1},{6,2},{7,3},{8,12},{9,13},{10,... | collective-permute-start | bytes 516104 | tf_op jit(solution)/shard_map/ppermute | solution.py:352
  17.2 62.4 %copy-start.85 = (s32[3]{0:T(128)}, s32[3]{0:T(128)S(1)}, u32[]{:S(2)}) copy-start(s32[3]{0:T(128)S(1)} %get-tuple-element.355.info) | copy-start | bytes 40
  17.2 114.1 %copy-start.87 = (s32[3]{0:T(128)}, s32[3]{0:T(128)S(1)}, u32[]{:S(2)}) copy-start(s32[3]{0:T(128)S(1)} %get-tuple-element.354.info) | copy-start | bytes 40
  18.2 50.6 %copy-start.113 = (pred[768]{0:T(1024)(128)(4,1)}, pred[768]{0:T(1024)(128)(4,1)S(1)}, u32[]{:S(2)}) copy-start(pred[768]{0:T(1024)(128)(4,1)S(1)} %iota.73) | copy-start | bytes 2308
  37.8 16.2 %collective-permute-start.4 = (bf16[512,768]{1,0:T(8,128)(2,1)S(1)}, bf16[512,768]{1,0:T(8,128)(2,1)S(1)}, u32[]{:S(2)}, u32[]{:S(2)}) collective-permute-start(bf16[512,768]{1,0:T(8,128)(2,1)S(1)} %bitcast.189), channel_id=1, source_target_pairs={{0,8},{8,0},{16,24},{24,16},{1,9},{9,1},{17,25},{25,17},{2,10},{10... | collective-permute-start | bytes 2359304 | tf_op jit(solution)/shard_map/ppermute | solution.py:352
  37.8 20.0 %collective-permute-start.3 = (bf16[512,768]{1,0:T(8,128)(2,1)S(1)}, bf16[512,768]{1,0:T(8,128)(2,1)S(1)}, u32[]{:S(2)}, u32[]{:S(2)}) collective-permute-start(bf16[512,768]{1,0:T(8,128)(2,1)S(1)} %bitcast.190), channel_id=1, source_target_pairs={{0,16},{8,24},{16,0},{24,8},{1,17},{9,25},{17,1},{25,9},{2,18},{10... | collective-permute-start | bytes 2359304 | tf_op jit(solution)/shard_map/ppermute | solution.py:352
  42.1 8.8 %collective-permute-start.1 = (bf16[2,96,896]{2,1,0:T(8,128)(2,1)S(1)}, bf16[2,96,896]{2,1,0:T(8,128)(2,1)S(1)}, u32[]{:S(2)}, u32[]{:S(2)}) collective-permute-start(bf16[2,96,896]{2,1,0:T(8,128)(2,1)S(1)} %broadcast_select_fusion.5), channel_id=1, source_target_pairs={{0,2},{1,3},{2,0},{3,1},{4,6},{5,7},{6,4},{7,5},{8,10},{9,11},{10,... | collective-permute-start | bytes 1032200 | tf_op jit(solution)/shard_map/ppermute | solution.py:352
  51.1 19.1 %collective-permute-start.6 = (bf16[2,96,768]{2,1,0:T(8,128)(2,1)}, bf16[2,96,768]{2,1,0:T(8,128)(2,1)S(1)}, u32[]{:S(2)}, u32[]{:S(2)}) collective-permute-start(bf16[2,96,768]{2,1,0:T(8,128)(2,1)} %pad_maximum_fusion.2), channel_id=1, source_target_pairs={{0,4},{1,5},{2,6},{3,7},{4,0},{5,1},{6,2},{7,3},{8,12},{9,13},{10,... | collective-permute-start | bytes 884744 | tf_op jit(solution)/shard_map/ppermute | solution.py:352
  52.1 16.8 %collective-permute-start.2 = (bf16[2,2,96,896]{3,2,1,0:T(8,128)(2,1)S(1)}, bf16[2,2,96,896]{3,2,1,0:T(8,128)(2,1)S(1)}, u32[]{:S(2)}, u32[]{:S(2)}) collective-permute-start(bf16[2,2,96,896]{3,2,1,0:T(8,128)(2,1)S(1)} %broadcast_select_fusion.2), channel_id=1, source_target_pairs={{0,1},{1,0},{2,3},{3,2},{4,5},{5,4},{6,7},{7,6},{8,9},{9,8},{10,11... | collective-permute-start | bytes 2064392 | tf_op jit(solution)/shard_map/ppermute | solution.py:352
  58.0 12.2 %collective-permute-start.5 = (bf16[512,768]{1,0:T(8,128)(2,1)S(1)}, bf16[512,768]{1,0:T(8,128)(2,1)S(1)}, u32[]{:S(2)}, u32[]{:S(2)}) collective-permute-start(bf16[512,768]{1,0:T(8,128)(2,1)S(1)} %collective-permute-done.3), channel_id=1, source_target_pairs={{0,8},{8,0},{16,24},{24,16},{1,9},{9,1},{17,25},{25,17},{2,10},{10... | collective-permute-start | bytes 2359304 | tf_op jit(solution)/shard_map/ppermute | solution.py:352
  70.7 18.4 %collective-permute-start.8 = (bf16[768,192]{1,0:T(8,128)(2,1)S(1)}, bf16[768,192]{1,0:T(8,128)(2,1)}, u32[]{:S(2)}, u32[]{:S(2)}) collective-permute-start(bf16[768,192]{1,0:T(8,128)(2,1)S(1)} %slice.142.refs_0_), channel_id=1, source_target_pairs={{0,16},{8,24},{16,0},{24,8},{1,17},{9,25},{17,1},{25,9},{2,18},{10... | collective-permute-start | bytes 884744 | tf_op jit(solution)/shard_map/ppermute | solution.py:352
  73.4 14.6 %collective-permute-start.7 = (bf16[2,2,96,768]{3,2,1,0:T(8,128)(2,1)S(1)}, bf16[2,2,96,768]{3,2,1,0:T(8,128)(2,1)S(1)}, u32[]{:S(2)}, u32[]{:S(2)}) collective-permute-start(bf16[2,2,96,768]{3,2,1,0:T(8,128)(2,1)S(1)} %broadcast_select_fusion.4), channel_id=1, source_target_pairs={{0,2},{1,3},{2,0},{3,1},{4,6},{5,7},{6,4},{7,5},{8,10},{9,11},{10,... | collective-permute-start | bytes 1769480 | tf_op jit(solution)/shard_map/ppermute | solution.py:352
  89.2 58.3 %all-to-all-start.1 = ((bf16[8,64,896]{2,1,0:T(8,128)(2,1)}), bf16[8,64,896]{2,1,0:T(8,128)(2,1)}, u32[]{:S(2)}, u32[]{:S(2)}) async-start(bf16[8,64,896]{2,1,0:T(8,128)(2,1)} %pad_maximum_fusion.1), calls=%async_computation.1 | async-start | bytes 1835008 | tf_op jit(solution)/shard_map/all_to_all | solution.py:439
  103.9 12.7 %collective-permute-start.9 = (bf16[768,192]{1,0:T(8,128)(2,1)S(1)}, bf16[768,192]{1,0:T(8,128)(2,1)S(1)}, u32[]{:S(2)}, u32[]{:S(2)}) collective-permute-start(bf16[768,192]{1,0:T(8,128)(2,1)S(1)} %slice.142.refs_0_), channel_id=1, source_target_pairs={{0,8},{8,0},{16,24},{24,16},{1,9},{9,1},{17,25},{25,17},{2,10},{10... | collective-permute-start | bytes 884744 | tf_op jit(solution)/shard_map/ppermute | solution.py:352
  104.0 12.6 %collective-permute-start.10 = (bf16[768,192]{1,0:T(8,128)(2,1)}, bf16[768,192]{1,0:T(8,128)(2,1)S(1)}, u32[]{:S(2)}, u32[]{:S(2)}) collective-permute-start(bf16[768,192]{1,0:T(8,128)(2,1)} %collective-permute-done.8.refs_1_), channel_id=1, source_target_pairs={{0,8},{8,0},{16,24},{24,16},{1,9},{9,1},{17,25},{25,17},{2,10},{10... | collective-permute-start | bytes 884744 | tf_op jit(solution)/shard_map/ppermute | solution.py:352
  106.6 32.6 %collective-permute-start.12 = (bf16[2,2,96,768]{3,2,1,0:T(8,128)(2,1)S(1)}, bf16[2,2,96,768]{3,2,1,0:T(8,128)(2,1)}, u32[]{:S(2)}, u32[]{:S(2)}) collective-permute-start(bf16[2,2,96,768]{3,2,1,0:T(8,128)(2,1)S(1)} %get-tuple-element.192), channel_id=1, source_target_pairs={{0,16},{8,24},{16,0},{24,8},{1,17},{9,25},{17,1},{25,9},{2,18},{10... | collective-permute-start | bytes 1769480 | tf_op jit(solution)/shard_map/ppermute | solution.py:352
  107.2 32.0 %collective-permute-start.11 = (bf16[2,2,96,768]{3,2,1,0:T(8,128)(2,1)S(1)}, bf16[2,2,96,768]{3,2,1,0:T(8,128)(2,1)S(1)}, u32[]{:S(2)}, u32[]{:S(2)}) collective-permute-start(bf16[2,2,96,768]{3,2,1,0:T(8,128)(2,1)S(1)} %get-tuple-element.171), channel_id=1, source_target_pairs={{0,1},{1,0},{2,3},{3,2},{4,5},{5,4},{6,7},{7,6},{8,9},{9,8},{10,11... | collective-permute-start | bytes 1769480 | tf_op jit(solution)/shard_map/ppermute | solution.py:352
  117.3 5.1 %collective-permute-start.15 = (bf16[64,512]{1,0:T(8,128)(2,1)S(1)}, bf16[64,512]{1,0:T(8,128)(2,1)S(1)}, u32[]{:S(2)}, u32[]{:S(2)}) collective-permute-start(bf16[64,512]{1,0:T(8,128)(2,1)S(1)} %get-tuple-element.344), channel_id=1, source_target_pairs={{0,24},{8,16},{16,8},{24,0},{1,25},{9,17},{17,9},{25,1},{2,26},{10... | collective-permute-start | bytes 196616 | tf_op jit(solution)/shard_map/ppermute | solution.py:352
  118.0 5.9 %collective-permute-start.14 = (bf16[64,512]{1,0:T(8,128)(2,1)S(1)}, bf16[64,512]{1,0:T(8,128)(2,1)S(1)}, u32[]{:S(2)}, u32[]{:S(2)}) collective-permute-start(bf16[64,512]{1,0:T(8,128)(2,1)S(1)} %get-tuple-element.345), channel_id=1, source_target_pairs={{0,8},{8,0},{16,24},{24,16},{1,9},{9,1},{17,25},{25,17},{2,10},{10... | collective-permute-start | bytes 196616 | tf_op jit(solution)/shard_map/ppermute | solution.py:352
  118.9 28.5 %collective-permute-start.22 = (bf16[2,2,96,768]{3,2,1,0:T(8,128)(2,1)S(1)}, bf16[2,2,96,768]{3,2,1,0:T(8,128)(2,1)}, u32[]{:S(2)}, u32[]{:S(2)}) collective-permute-start(bf16[2,2,96,768]{3,2,1,0:T(8,128)(2,1)S(1)} %get-tuple-element.192), channel_id=1, source_target_pairs={{0,1},{1,0},{2,3},{3,2},{4,5},{5,4},{6,7},{7,6},{8,9},{9,8},{10,11... | collective-permute-start | bytes 1769480 | tf_op jit(solution)/shard_map/ppermute | solution.py:352
  123.1 4.9 %collective-permute-start.13 = (bf16[64,512]{1,0:T(8,128)(2,1)S(1)}, bf16[64,512]{1,0:T(8,128)(2,1)S(1)}, u32[]{:S(2)}, u32[]{:S(2)}) collective-permute-start(bf16[64,512]{1,0:T(8,128)(2,1)S(1)} %get-tuple-element.346), channel_id=1, source_target_pairs={{0,16},{8,24},{16,0},{24,8},{1,17},{9,25},{17,1},{25,9},{2,18},{10... | collective-permute-start | bytes 196616 | tf_op jit(solution)/shard_map/ppermute | solution.py:352
  124.5 4.9 %collective-permute-start.18 = (bf16[64,512]{1,0:T(8,128)(2,1)S(1)}, bf16[64,512]{1,0:T(8,128)(2,1)S(1)}, u32[]{:S(2)}, u32[]{:S(2)}) collective-permute-start(bf16[64,512]{1,0:T(8,128)(2,1)S(1)} %get-tuple-element.340), channel_id=1, source_target_pairs={{0,24},{8,16},{16,8},{24,0},{1,25},{9,17},{17,9},{25,1},{2,26},{10... | collective-permute-start | bytes 196616 | tf_op jit(solution)/shard_map/ppermute | solution.py:352
  128.6 10.5 %collective-permute-start.17 = (bf16[64,512]{1,0:T(8,128)(2,1)S(1)}, bf16[64,512]{1,0:T(8,128)(2,1)S(1)}, u32[]{:S(2)}, u32[]{:S(2)}) collective-permute-start(bf16[64,512]{1,0:T(8,128)(2,1)S(1)} %get-tuple-element.341), channel_id=1, source_target_pairs={{0,8},{8,0},{16,24},{24,16},{1,9},{9,1},{17,25},{25,17},{2,10},{10... | collective-permute-start | bytes 196616 | tf_op jit(solution)/shard_map/ppermute | solution.py:352
  130.0 9.2 %collective-permute-start.16 = (bf16[64,512]{1,0:T(8,128)(2,1)S(1)}, bf16[64,512]{1,0:T(8,128)(2,1)S(1)}, u32[]{:S(2)}, u32[]{:S(2)}) collective-permute-start(bf16[64,512]{1,0:T(8,128)(2,1)S(1)} %get-tuple-element.342), channel_id=1, source_target_pairs={{0,16},{8,24},{16,0},{24,8},{1,17},{9,25},{17,1},{25,9},{2,18},{10... | collective-permute-start | bytes 196616 | tf_op jit(solution)/shard_map/ppermute | solution.py:352
  140.4 4.0 %collective-permute-start.21 = (bf16[64,512]{1,0:T(8,128)(2,1)S(1)}, bf16[64,512]{1,0:T(8,128)(2,1)S(1)}, u32[]{:S(2)}, u32[]{:S(2)}) collective-permute-start(bf16[64,512]{1,0:T(8,128)(2,1)S(1)} %get-tuple-element.336), channel_id=1, source_target_pairs={{0,24},{8,16},{16,8},{24,0},{1,25},{9,17},{17,9},{25,1},{2,26},{10... | collective-permute-start | bytes 196616 | tf_op jit(solution)/shard_map/ppermute | solution.py:352
  142.0 3.1 collective-permute-start.20
  142.5 4.3 %collective-permute-start.19 = (bf16[64,512]{1,0:T(8,128)(2,1)S(1)}, bf16[64,512]{1,0:T(8,128)(2,1)S(1)}, u32[]{:S(2)}, u32[]{:S(2)}) collective-permute-start(bf16[64,512]{1,0:T(8,128)(2,1)S(1)} %get-tuple-element.338), channel_id=1, source_target_pairs={{0,16},{8,24},{16,0},{24,8},{1,17},{9,25},{17,1},{25,9},{2,18},{10... | collective-permute-start | bytes 196616 | tf_op jit(solution)/shard_map/ppermute | solution.py:352
  147.5 27.7 %collective-permute-start.26 = (bf16[768,768]{1,0:T(8,128)(2,1)}, bf16[768,768]{1,0:T(8,128)(2,1)}, u32[]{:S(2)}, u32[]{:S(2)}) collective-permute-start(bf16[768,768]{1,0:T(8,128)(2,1)} %bitcast_select_fusion.3.wu), channel_id=1, source_target_pairs={{0,16},{8,24},{16,0},{24,8},{1,17},{9,25},{17,1},{25,9},{2,18},{10... | collective-permute-start | bytes 3538952 | tf_op jit(solution)/shard_map/ppermute | solution.py:352
  151.0 16.2 %collective-permute-start.24 = (bf16[512,768]{1,0:T(8,128)(2,1)}, bf16[512,768]{1,0:T(8,128)(2,1)}, u32[]{:S(2)}, u32[]{:S(2)}) collective-permute-start(bf16[512,768]{1,0:T(8,128)(2,1)} %slice.123.cot), channel_id=1, source_target_pairs={{0,8},{8,0},{16,24},{24,16},{1,9},{9,1},{17,25},{25,17},{2,10},{10... | collective-permute-start | bytes 2359304 | tf_op jit(solution)/shard_map/ppermute | solution.py:352
  155.7 11.5 %collective-permute-start.23 = (bf16[512,768]{1,0:T(8,128)(2,1)}, bf16[512,768]{1,0:T(8,128)(2,1)}, u32[]{:S(2)}, u32[]{:S(2)}) collective-permute-start(bf16[512,768]{1,0:T(8,128)(2,1)} %get-tuple-element.189.nm), channel_id=1, source_target_pairs={{0,8},{8,0},{16,24},{24,16},{1,9},{9,1},{17,25},{25,17},{2,10},{10... | collective-permute-start | bytes 2359304 | tf_op jit(solution)/shard_map/ppermute | solution.py:352
  156.2 17.8 %collective-permute-start.25 = (bf16[2,2,96,768]{3,2,1,0:T(8,128)(2,1)}, bf16[2,2,96,768]{3,2,1,0:T(8,128)(2,1)}, u32[]{:S(2)}, u32[]{:S(2)}) collective-permute-start(bf16[2,2,96,768]{3,2,1,0:T(8,128)(2,1)} %collective-permute-done.12), channel_id=1, source_target_pairs={{0,1},{1,0},{2,3},{3,2},{4,5},{5,4},{6,7},{7,6},{8,9},{9,8},{10,11... | collective-permute-start | bytes 1769480 | tf_op jit(solution)/shard_map/ppermute | solution.py:352
  183.9 12.3 %collective-permute-start.28 = (bf16[512,768]{1,0:T(8,128)(2,1)S(1)}, bf16[512,768]{1,0:T(8,128)(2,1)S(1)}, u32[]{:S(2)}, u32[]{:S(2)}) collective-permute-start(bf16[512,768]{1,0:T(8,128)(2,1)S(1)} %convert_element_type.480), channel_id=1, source_target_pairs={{0,8},{8,0},{16,24},{24,16},{1,9},{9,1},{17,25},{25,17},{2,10},{10... | collective-permute-start | bytes 2359304 | tf_op jit(solution)/shard_map/ppermute | solution.py:352
  184.0 12.2 %collective-permute-start.27 = (bf16[512,768]{1,0:T(8,128)(2,1)S(1)}, bf16[512,768]{1,0:T(8,128)(2,1)S(1)}, u32[]{:S(2)}, u32[]{:S(2)}) collective-permute-start(bf16[512,768]{1,0:T(8,128)(2,1)S(1)} %convert_element_type.479), channel_id=1, source_target_pairs={{0,8},{8,0},{16,24},{24,16},{1,9},{9,1},{17,25},{25,17},{2,10},{10... | collective-permute-start | bytes 2359304 | tf_op jit(solution)/shard_map/ppermute | solution.py:352
  194.4 40.0 %collective-permute-start.32 = (bf16[2,2,2,96,768]{4,3,0,1,2:T(8,128)(2,1)}, bf16[2,2,2,96,768]{4,3,0,1,2:T(8,128)(2,1)}, u32[]{:S(2)}, u32[]{:S(2)}) collective-permute-start(bf16[2,2,2,96,768]{4,3,0,1,2:T(8,128)(2,1)} %copy.136), channel_id=1, source_target_pairs={{0,1},{1,0},{2,3},{3,2},{4,5},{5,4},{6,7},{7,6},{8,9},{9,8},{10,11... | collective-permute-start | bytes 3538952 | tf_op jit(solution)/shard_map/ppermute | solution.py:352
  201.3 7.9 %collective-permute-start.29 = (bf16[192,512]{1,0:T(8,128)(2,1)S(1)}, bf16[192,512]{1,0:T(8,128)(2,1)S(1)}, u32[]{:S(2)}, u32[]{:S(2)}) collective-permute-start(bf16[192,512]{1,0:T(8,128)(2,1)S(1)} %get-tuple-element.207), channel_id=1, source_target_pairs={{0,16},{8,24},{16,0},{24,8},{1,17},{9,25},{17,1},{25,9},{2,18},{10... | collective-permute-start | bytes 589832 | tf_op jit(solution)/shard_map/ppermute | solution.py:352
  203.0 6.1 %collective-permute-start.30 = (bf16[192,512]{1,0:T(8,128)(2,1)S(1)}, bf16[192,512]{1,0:T(8,128)(2,1)S(1)}, u32[]{:S(2)}, u32[]{:S(2)}) collective-permute-start(bf16[192,512]{1,0:T(8,128)(2,1)S(1)} %get-tuple-element.208), channel_id=1, source_target_pairs={{0,8},{8,0},{16,24},{24,16},{1,9},{9,1},{17,25},{25,17},{2,10},{10... | collective-permute-start | bytes 589832 | tf_op jit(solution)/shard_map/ppermute | solution.py:352
  203.0 8.3 %collective-permute-start.31 = (bf16[192,512]{1,0:T(8,128)(2,1)S(1)}, bf16[192,512]{1,0:T(8,128)(2,1)S(1)}, u32[]{:S(2)}, u32[]{:S(2)}) collective-permute-start(bf16[192,512]{1,0:T(8,128)(2,1)S(1)} %get-tuple-element.209), channel_id=1, source_target_pairs={{0,24},{8,16},{16,8},{24,0},{1,25},{9,17},{17,9},{25,1},{2,26},{10... | collective-permute-start | bytes 589832 | tf_op jit(solution)/shard_map/ppermute | solution.py:352
  212.0 42.3 %all-to-all-start.2 = ((bf16[8,64,768]{2,1,0:T(8,128)(2,1)}), bf16[8,64,768]{2,1,0:T(8,128)(2,1)}, u32[]{:S(2)}, u32[]{:S(2)}) async-start(bf16[8,64,768]{2,1,0:T(8,128)(2,1)} %bitcast.196), calls=%async_computation.2 | async-start | bytes 1572864 | tf_op jit(solution)/shard_map/all_to_all | solution.py:439
  217.0 37.3 %collective-permute-start.34 = (bf16[768,768]{1,0:T(8,128)(2,1)}, bf16[768,768]{1,0:T(8,128)(2,1)}, u32[]{:S(2)}, u32[]{:S(2)}) collective-permute-start(bf16[768,768]{1,0:T(8,128)(2,1)} %add_convert_fusion.3), channel_id=1, source_target_pairs={{0,16},{8,24},{16,0},{24,8},{1,17},{9,25},{17,1},{25,9},{2,18},{10... | collective-permute-start | bytes 3538952 | tf_op jit(solution)/shard_map/ppermute | solution.py:352
  218.6 15.8 %collective-permute-start.33 = (bf16[768,192]{1,0:T(8,128)(2,1)}, bf16[768,192]{1,0:T(8,128)(2,1)}, u32[]{:S(2)}, u32[]{:S(2)}) collective-permute-start(bf16[768,192]{1,0:T(8,128)(2,1)} %copy-done.93), channel_id=1, source_target_pairs={{0,8},{8,0},{16,24},{24,16},{1,9},{9,1},{17,25},{25,17},{2,10},{10... | collective-permute-start | bytes 884744 | tf_op jit(solution)/shard_map/ppermute | solution.py:352
  236.5 17.8 %collective-permute-start.35 = (bf16[2,2,96,768]{3,2,1,0:T(8,128)(2,1)}, bf16[2,2,96,768]{3,2,1,0:T(8,128)(2,1)}, u32[]{:S(2)}, u32[]{:S(2)}) collective-permute-start(bf16[2,2,96,768]{3,2,1,0:T(8,128)(2,1)} %fusion.36), channel_id=1, source_target_pairs={{0,2},{1,3},{2,0},{3,1},{4,6},{5,7},{6,4},{7,5},{8,10},{9,11},{10,... | collective-permute-start | bytes 1769480 | tf_op jit(solution)/shard_map/ppermute | solution.py:352
  239.2 15.1 %collective-permute-start.36 = (bf16[768,192]{1,0:T(8,128)(2,1)}, bf16[768,192]{1,0:T(8,128)(2,1)}, u32[]{:S(2)}, u32[]{:S(2)}) collective-permute-start(bf16[768,192]{1,0:T(8,128)(2,1)} %add_convert_fusion.11), channel_id=1, source_target_pairs={{0,16},{8,24},{16,0},{24,8},{1,17},{9,25},{17,1},{25,9},{2,18},{10... | collective-permute-start | bytes 884744 | tf_op jit(solution)/shard_map/ppermute | solution.py:352
  257.6 18.6 %collective-permute-start.38 = (bf16[2,2,96,768]{3,2,0,1:T(8,128)(2,1)S(1)}, bf16[2,2,96,768]{3,2,0,1:T(8,128)(2,1)S(1)}, u32[]{:S(2)}, u32[]{:S(2)}) collective-permute-start(bf16[2,2,96,768]{3,2,0,1:T(8,128)(2,1)S(1)} %fusion.35), channel_id=1, source_target_pairs={{0,1},{1,0},{2,3},{3,2},{4,5},{5,4},{6,7},{7,6},{8,9},{9,8},{10,11... | collective-permute-start | bytes 1769480 | tf_op jit(solution)/shard_map/ppermute | solution.py:352
  260.5 15.7 %collective-permute-start.37 = (bf16[2,96,768]{2,1,0:T(8,128)(2,1)S(1)}, bf16[2,96,768]{2,1,0:T(8,128)(2,1)S(1)}, u32[]{:S(2)}, u32[]{:S(2)}) collective-permute-start(bf16[2,96,768]{2,1,0:T(8,128)(2,1)S(1)} %fusion.43), channel_id=1, source_target_pairs={{0,4},{1,5},{2,6},{3,7},{4,0},{5,1},{6,2},{7,3},{8,12},{9,13},{10,... | collective-permute-start | bytes 884744 | tf_op jit(solution)/shard_map/ppermute | solution.py:352
  280.0 12.1 %collective-permute-start.41 = (bf16[2,512,768]{2,1,0:T(8,128)(2,1)S(1)}, bf16[2,512,768]{2,1,0:T(8,128)(2,1)S(1)}, u32[]{:S(2)}, u32[]{:S(2)}) collective-permute-start(bf16[2,512,768]{2,1,0:T(8,128)(2,1)S(1)} %rows_grad.3), channel_id=1, source_target_pairs={{0,8},{8,0},{16,24},{24,16},{1,9},{9,1},{17,25},{25,17},{2,10},{10... | collective-permute-start | bytes 4718600 | tf_op jit(solution)/shard_map/ppermute | solution.py:352
  280.1 3.9 %collective-permute-start.39 = (bf16[768,192]{1,0:T(8,128)(2,1)S(1)}, bf16[768,192]{1,0:T(8,128)(2,1)S(1)}, u32[]{:S(2)}, u32[]{:S(2)}) collective-permute-start(bf16[768,192]{1,0:T(8,128)(2,1)S(1)} %copy-done.92), channel_id=1, source_target_pairs={{0,8},{8,0},{16,24},{24,16},{1,9},{9,1},{17,25},{25,17},{2,10},{10... | collective-permute-start | bytes 884744 | tf_op jit(solution)/shard_map/ppermute | solution.py:352
  280.8 9.1 %collective-permute-start.40 = (bf16[2,96,768]{2,1,0:T(8,128)(2,1)S(1)}, bf16[2,96,768]{2,1,0:T(8,128)(2,1)S(1)}, u32[]{:S(2)}, u32[]{:S(2)}) collective-permute-start(bf16[2,96,768]{2,1,0:T(8,128)(2,1)S(1)} %get-tuple-element.316), channel_id=1, source_target_pairs={{0,2},{1,3},{2,0},{3,1},{4,6},{5,7},{6,4},{7,5},{8,10},{9,11},{10,... | collective-permute-start | bytes 884744 | tf_op jit(solution)/shard_map/ppermute | solution.py:352
  291.5 14.8 %collective-permute-start.49 = (bf16[2,2,96,768]{3,2,0,1:T(8,128)(2,1)}, bf16[2,2,96,768]{3,2,0,1:T(8,128)(2,1)}, u32[]{:S(2)}, u32[]{:S(2)}) collective-permute-start(bf16[2,2,96,768]{3,2,0,1:T(8,128)(2,1)} %copy_bitcast_fusion.1), channel_id=1, source_target_pairs={{0,1},{1,0},{2,3},{3,2},{4,5},{5,4},{6,7},{7,6},{8,9},{9,8},{10,11... | collective-permute-start | bytes 1769480 | tf_op jit(solution)/shard_map/ppermute | solution.py:352
  294.7 23.3 %collective-permute-start.42 = (bf16[512,768]{1,0:T(8,128)(2,1)}, bf16[512,768]{1,0:T(8,128)(2,1)S(1)}, u32[]{:S(2)}, u32[]{:S(2)}) collective-permute-start(bf16[512,768]{1,0:T(8,128)(2,1)} %slice_bitcast_fusion), channel_id=1, source_target_pairs={{0,16},{8,24},{16,0},{24,8},{1,17},{9,25},{17,1},{25,9},{2,18},{10... | collective-permute-start | bytes 2359304 | tf_op jit(solution)/shard_map/ppermute | solution.py:352
  307.4 10.5 %collective-permute-start.50 = (bf16[2,96,768]{2,1,0:T(8,128)(2,1)S(1)}, bf16[2,96,768]{2,1,0:T(8,128)(2,1)S(1)}, u32[]{:S(2)}, u32[]{:S(2)}) collective-permute-start(bf16[2,96,768]{2,1,0:T(8,128)(2,1)S(1)} %get-tuple-element.312), channel_id=1, source_target_pairs={{0,2},{1,3},{2,0},{3,1},{4,6},{5,7},{6,4},{7,5},{8,10},{9,11},{10,... | collective-permute-start | bytes 884744 | tf_op jit(solution)/shard_map/ppermute | solution.py:352
  309.2 13.6 %collective-permute-start.48 = (bf16[96,768]{1,0:T(8,128)(2,1)}, bf16[96,768]{1,0:T(8,128)(2,1)S(1)}, u32[]{:S(2)}, u32[]{:S(2)}) collective-permute-start(bf16[96,768]{1,0:T(8,128)(2,1)} %get-tuple-element.334), channel_id=1, source_target_pairs={{0,4},{1,5},{2,6},{3,7},{4,0},{5,1},{6,2},{7,3},{8,12},{9,13},{10,... | collective-permute-start | bytes 442376 | tf_op jit(solution)/shard_map/ppermute | solution.py:352
  318.9 8.9 %collective-permute-start.54 = (bf16[96,768]{1,0:T(8,128)(2,1)S(1)}, bf16[96,768]{1,0:T(8,128)(2,1)S(1)}, u32[]{:S(2)}, u32[]{:S(2)}) collective-permute-start(bf16[96,768]{1,0:T(8,128)(2,1)S(1)} %slice_bitcast_fusion.5), channel_id=1, source_target_pairs={{0,16},{8,24},{16,0},{24,8},{1,17},{9,25},{17,1},{25,9},{2,18},{10... | collective-permute-start | bytes 442376 | tf_op jit(solution)/shard_map/ppermute | solution.py:352
  320.8 7.0 %collective-permute-start.51 = (bf16[96,768]{1,0:T(8,128)(2,1)S(1)}, bf16[96,768]{1,0:T(8,128)(2,1)S(1)}, u32[]{:S(2)}, u32[]{:S(2)}) collective-permute-start(bf16[96,768]{1,0:T(8,128)(2,1)S(1)} %get-tuple-element.332), channel_id=1, source_target_pairs={{0,4},{1,5},{2,6},{3,7},{4,0},{5,1},{6,2},{7,3},{8,12},{9,13},{10,... | collective-permute-start | bytes 442376 | tf_op jit(solution)/shard_map/ppermute | solution.py:352
  328.4 6.7 %collective-permute-start.55 = (bf16[2,96,768]{2,1,0:T(8,128)(2,1)S(1)}, bf16[2,96,768]{2,1,0:T(8,128)(2,1)S(1)}, u32[]{:S(2)}, u32[]{:S(2)}) collective-permute-start(bf16[2,96,768]{2,1,0:T(8,128)(2,1)S(1)} %pad_maximum_fusion.3), channel_id=1, source_target_pairs={{0,16},{8,24},{16,0},{24,8},{1,17},{9,25},{17,1},{25,9},{2,18},{10... | collective-permute-start | bytes 884744 | tf_op jit(solution)/shard_map/ppermute | solution.py:352
  329.6 20.9 %all-to-all-start.3 = ((bf16[8,64,768]{2,1,0:T(8,128)(2,1)}), bf16[8,64,768]{2,1,0:T(8,128)(2,1)S(1)}, u32[]{:S(2)}, u32[]{:S(2)}) async-start(bf16[8,64,768]{2,1,0:T(8,128)(2,1)} %bitcast.63), calls=%async_computation.3 | async-start | bytes 1572864 | tf_op jit(solution)/shard_map/all_to_all | solution.py:439
  335.3 14.7 %collective-permute-start.56 = (bf16[2,2,96,768]{3,2,0,1:T(8,128)(2,1)S(1)}, bf16[2,2,96,768]{3,2,0,1:T(8,128)(2,1)S(1)}, u32[]{:S(2)}, u32[]{:S(2)}) collective-permute-start(bf16[2,2,96,768]{3,2,0,1:T(8,128)(2,1)S(1)} %broadcast_select_fusion.3), channel_id=1, source_target_pairs={{0,8},{8,0},{16,24},{24,16},{1,9},{9,1},{17,25},{25,17},{2,10},{10... | collective-permute-start | bytes 1769480 | tf_op jit(solution)/shard_map/ppermute | solution.py:352
  335.4 2.0 collective-permute-start.43
  337.5 3.8 %collective-permute-start.44 = (f32[8,768]{1,0:T(8,128)S(1)}, f32[8,768]{1,0:T(8,128)S(1)}, u32[]{:S(2)}, u32[]{:S(2)}) collective-permute-start(f32[8,768]{1,0:T(8,128)S(1)} %fusion.69), channel_id=1, source_target_pairs={{0,16},{8,24},{16,0},{24,8},{1,17},{9,25},{17,1},{25,9},{2,18},{10... | collective-permute-start | bytes 73736 | tf_op jit(solution)/shard_map/ppermute | solution.py:352
  341.3 4.9 %collective-permute-start.45 = (f32[8,768]{1,0:T(8,128)S(1)}, f32[8,768]{1,0:T(8,128)S(1)}, u32[]{:S(2)}, u32[]{:S(2)}) collective-permute-start(f32[8,768]{1,0:T(8,128)S(1)} %add.261), channel_id=1, source_target_pairs={{0,1},{1,0},{2,3},{3,2},{4,5},{5,4},{6,7},{7,6},{8,9},{9,8},{10,11... | collective-permute-start | bytes 73736 | tf_op jit(solution)/shard_map/ppermute | solution.py:352
  346.2 3.8 %collective-permute-start.46 = (f32[8,768]{1,0:T(8,128)S(1)}, f32[8,768]{1,0:T(8,128)S(1)}, u32[]{:S(2)}, u32[]{:S(2)}) collective-permute-start(f32[8,768]{1,0:T(8,128)S(1)} %add.262), channel_id=1, source_target_pairs={{0,2},{1,3},{2,0},{3,1},{4,6},{5,7},{6,4},{7,5},{8,10},{9,11},{10,... | collective-permute-start | bytes 73736 | tf_op jit(solution)/shard_map/ppermute | solution.py:352
  350.5 7.5 %collective-permute-start.47 = (f32[8,768]{1,0:T(8,128)S(1)}, f32[8,768]{1,0:T(8,128)S(1)}, u32[]{:S(2)}, u32[]{:S(2)}) collective-permute-start(f32[8,768]{1,0:T(8,128)S(1)} %add.263), channel_id=1, source_target_pairs={{0,4},{1,5},{2,6},{3,7},{4,0},{5,1},{6,2},{7,3},{8,12},{9,13},{10,... | collective-permute-start | bytes 73736 | tf_op jit(solution)/shard_map/ppermute | solution.py:352
  352.2 5.8 %collective-permute-start.52 = (bf16[96,768]{1,0:T(8,128)(2,1)S(1)}, bf16[96,768]{1,0:T(8,128)(2,1)S(1)}, u32[]{:S(2)}, u32[]{:S(2)}) collective-permute-start(bf16[96,768]{1,0:T(8,128)(2,1)S(1)} %add_convert_fusion.17), channel_id=1, source_target_pairs={{0,16},{8,24},{16,0},{24,8},{1,17},{9,25},{17,1},{25,9},{2,18},{10... | collective-permute-start | bytes 442376 | tf_op jit(solution)/shard_map/ppermute | solution.py:352
  358.1 1.6 collective-permute-start.53
  (122 other events, 672.7 us)

commit v2 on v1

--- a/solution.py
+++ b/solution.py
@@ -605,7 +605,6 @@
     d_inputs = (d_residual + d_in_norm).astype(bf16)
     d_back = deal(d_inputs.reshape(groups, local_len, width))
     up, d_wq = after(d_inputs, up, d_wq)
-    (d_wq,) = after(d_back, d_wq)
     pair = jnp.stack((add(*up), add(down[0], down_came)))
     grads = gather(pair, "seq", (2, 1)).reshape(parts, 2, own_rows, width)
     (g_up,) = row_call(

time: 366 us -> 380 us (1.038)
  waiting for transfers between devices: 84.7 us -> 102 us
  Pallas kernels: 104 us -> 89.8 us
  starting transfers between devices: 83.3 us -> 94.1 us
    ppermute x57, waiting for transfers between devices: 67.5 us -> 84.7 us  [swap(): return lax.ppermute(value, axis, [(i, i ^ bit) for i in range(count)])]
    ppermute x57, starting transfers between devices: 52.6 us -> 62.7 us  [swap(): return lax.ppermute(value, axis, [(i, i ^ bit) for i in range(count)])]
    pallas_call x3, Pallas kernels: 32.9 us -> 25.1 us  [attend_back(): pl.pallas_call(functools.partial(attend_back_body, blocks=blocks, blk=blk...]
    pallas_call x3, Pallas kernels: 23.2 us -> 17.1 us  [attend(): pl.pallas_call(functools.partial(attend_body, blk=blk), grid_spec=pltpu.P...]
    unnamed x256 -> x254, local copies, waits for them, and re-layouts: 28.8 us -> 27.6 us
  transfers between devices with their start and end apart: 61 -> 61, of which waited for: 25 -> 24; matrix products, arithmetic and copies ran while one was open for 15% -> 15% of each run, Pallas kernels for 26% -> 22%
where the time goes in v2:
time: 380 us; the launch traced here: 375 us
  waiting for transfers between devices  102 us (27%)
  starting transfers between devices  94.1 us (25%)
  Pallas kernels  89.8 us (24%)
  local copies, waits for them, and re-layouts  44.2 us (12%)
  other arithmetic  36.7 us (10%)
  matrix products  5.98 us (2%)
    ppermute x57, waiting for transfers between devices, swap(): return lax.ppermute(value, axis, [(i, i ^ bit) for i in range(count)])  84.7 us
    ppermute x57, starting transfers between devices, swap(): return lax.ppermute(value, axis, [(i, i ^ bit) for i in range(count)])  62.7 us
    all_to_all x4, starting transfers between devices, per_device(): lax.all_to_all(a, 'fsdp', split_axis=0, concat_axis=0, tiled=True)  31.5 us
    unnamed x254, local copies, waits for them, and re-layouts  27.6 us
    pallas_call x4, Pallas kernels, mlp_part(): pl.pallas_call(functools.partial(mlp_body, begun=bool(sums)), grid=(ff //...  27.5 us
    pallas_call x3, Pallas kernels, attend_back(): pl.pallas_call(functools.partial(attend_back_body, blocks=blocks, blk=blk...  25.1 us
    pallas_call x10, Pallas kernels, row_call(): pl.pallas_call(body, grid=(steps,), in_specs=[pl.BlockSpec(memory_space=p...  20.1 us
    all_to_all x4, waiting for transfers between devices, per_device(): lax.all_to_all(a, 'fsdp', split_axis=0, concat_axis=0, tiled=True)  17.2 us
  transfers between devices with their start and end apart: 61, of which 24 were waited for; matrix products, arithmetic and copies ran while one was open for 15% of the time, Pallas kernels for 22%

profile of v2, /device:TPU:0, one launch (start us, length us, event | category | flops | bytes accessed | tf_op | source)
XLA Modules:
  0.0 375.5 jit_solution(15892781980552728390)
XLA Ops:
  1.5 1.6 fusion.18
  4.1 7.3 %all-to-all-start = ((bf16[8,64,768]{2,1,0:T(8,128)(2,1)}), bf16[8,64,768]{2,1,0:T(8,128)(2,1)S(1)}, u32[]{:S(2)}, u32[]{:S(2)}) async-start(bf16[8,64,768]{2,1,0:T(8,128)(2,1)} %copy.123), calls=%async_computation | async-start | bytes 1572864 | tf_op jit(solution)/shard_map/all_to_all | solution.py:439
  12.7 3.0 collective-permute-start
  20.7 17.2 %all-to-all-done = bf16[8,64,768]{2,1,0:T(8,128)(2,1)S(1)} async-done(((bf16[8,64,768]{2,1,0:T(8,128)(2,1)}), bf16[8,64,768]{2,1,0:T(8,128)(2,1)S(1)}, u32[]{:S(2)}, u32[]{:S(2)}) %all-to-all-start) | async-done | bytes 786464 | tf_op jit(solution)/shard_map/all_to_all | solution.py:439
  39.3 2.1 collective-permute-done
  42.6 8.3 %collective-permute-done.1 = bf16[2,96,896]{2,1,0:T(8,128)(2,1)S(1)} collective-permute-done((bf16[2,96,896]{2,1,0:T(8,128)(2,1)S(1)}, bf16[2,96,896]{2,1,0:T(8,128)(2,1)S(1)}, u32[]{:S(2)}, u32[]{:S(2)}) %collective-permute-start.1) | collective-permute-done | bytes 344096 | tf_op jit(solution)/shard_map/ppermute | solution.py:352
  52.1 2.0 collective-permute-start.2
  54.3 3.5 collective-permute-done.3
  58.8 10.0 %collective-permute-done.2 = bf16[2,2,96,896]{3,2,1,0:T(8,128)(2,1)S(1)} collective-permute-done((bf16[2,2,96,896]{3,2,1,0:T(8,128)(2,1)S(1)}, bf16[2,2,96,896]{3,2,1,0:T(8,128)(2,1)S(1)}, u32[]{:S(2)}, u32[]{:S(2)}) %collective-permute-start.2) | collective-permute-done | bytes 688160 | tf_op jit(solution)/shard_map/ppermute | solution.py:352
  70.7 1.6 collective-permute-start.8
  73.4 1.5 collective-permute-start.7
  79.6 5.7 %attend.3 = (bf16[4,64,512]{2,1,0:T(8,128)(2,1)S(1)}, f32[4,1,512]{2,1,0:T(1,128)S(1)}) custom-call(s32[3]{0:T(128)S(1)} %get-tuple-element.351.info, bf16[4,576,512]{2,1,0:T(8,128)(2,1)S(1)} %pad_maximum_fusion.qkv), custom_call_target="tpu_custom_call" | custom-call | flops 1048576 | bytes 1048576 | tf_op jit(solution)/shard_map/attend/pallas_call | solution.py:61
  88.1 14.8 %all-to-all-start.1 = ((bf16[8,64,896]{2,1,0:T(8,128)(2,1)}), bf16[8,64,896]{2,1,0:T(8,128)(2,1)}, u32[]{:S(2)}, u32[]{:S(2)}) async-start(bf16[8,64,896]{2,1,0:T(8,128)(2,1)} %pad_maximum_fusion.1), calls=%async_computation.1 | async-start | bytes 1835008 | tf_op jit(solution)/shard_map/all_to_all | solution.py:439
  106.2 2.0 collective-permute-start.11
  108.2 5.7 %attend.4 = (bf16[4,64,512]{2,1,0:T(8,128)(2,1)S(1)}, f32[4,1,512]{2,1,0:T(1,128)S(1)}) custom-call(s32[3]{0:T(128)S(1)} %pad_add_fusion.3.info, bf16[4,576,512]{2,1,0:T(8,128)(2,1)S(1)} %pad_maximum_fusion.qkv), custom_call_target="tpu_custom_call" | custom-call | flops 1048576 | bytes 1048576 | tf_op jit(solution)/shard_map/attend/pallas_call | solution.py:61
  118.2 3.2 collective-permute-done.15.refs_7_
  123.2 1.9 collective-permute-start.18
  125.1 1.7 collective-permute-done.13.refs_5_
  130.3 5.7 %attend.5 = (bf16[4,64,512]{2,1,0:T(8,128)(2,1)S(1)}, f32[4,1,512]{2,1,0:T(1,128)S(1)}) custom-call(s32[3]{0:T(128)S(1)} %get-tuple-element.350.info, bf16[4,576,512]{2,1,0:T(8,128)(2,1)S(1)} %pad_maximum_fusion.qkv), custom_call_target="tpu_custom_call" | custom-call | flops 1048576 | bytes 1048576 | tf_op jit(solution)/shard_map/attend/pallas_call | solution.py:61
  137.3 1.6 collective-permute-start.21
  145.7 2.1 slice.123.cot
  147.9 3.5 project_out.1
  153.0 3.4 collective-permute-start.25
  156.4 1.5 bitcast_select_fusion.2.wd
  158.1 6.7 %mlp_part.5 = (f32[512,768]{1,0:T(8,128)S(1)}, f32[512,768]{1,0:T(8,128)S(1)}, bf16[768,768]{1,0:T(8,128)(2,1)S(1)}, bf16[768,768]{1,0:T(8,128)(2,1)S(1)}) custom-call(bf16[512,768]{1,0:T(8,128)(2,1)} %get-tuple-element.187.nm, bf16[512,768]{1,0:T(8,128)(2,1)} %slice.123.cot, bf16[768,768]{1,0:T(8,128)(2,1)S(1)} %copy-done.7, ...), custom_call_target="tpu_custom_call" | custom-call | flops 1048576 | bytes 1048576 | tf_op jit(solution)/shard_map/mlp_part/pallas_call | solution.py:201
  165.8 6.7 %mlp_part.4 = (f32[512,768]{1,0:T(8,128)S(1)}, f32[512,768]{1,0:T(8,128)S(1)}, bf16[768,768]{1,0:T(8,128)(2,1)S(1)}, bf16[768,768]{1,0:T(8,128)(2,1)S(1)}) custom-call(bf16[512,768]{1,0:T(8,128)(2,1)} %collective-permute-done.23.nm, bf16[512,768]{1,0:T(8,128)(2,1)} %collective-permute-done.24.cot, bf16[768,768]{1,0:T(8,128)(2,1)S(1)} %copy-done.7, ...), custom_call_target="tpu_custom_call" | custom-call | flops 1048576 | bytes 1048576 | tf_op jit(solution)/shard_map/mlp_part/pallas_call | solution.py:201
  172.6 1.8 bitcast_select_fusion.1.wd
  174.5 7.0 %mlp_part.7 = (f32[512,768]{1,0:T(8,128)S(1)}, f32[512,768]{1,0:T(8,128)S(1)}, bf16[768,768]{1,0:T(8,128)(2,1)S(1)}, bf16[768,768]{1,0:T(8,128)(2,1)S(1)}) custom-call(bf16[512,768]{1,0:T(8,128)(2,1)} %collective-permute-done.23.nm, bf16[512,768]{1,0:T(8,128)(2,1)} %collective-permute-done.24.cot, ...), custom_call_target="tpu_custom_call", output_to_operand_aliasing={{0}: (4, {}), {1}: (5, {})} | custom-call | flops 1048576 | bytes 1048576 | tf_op jit(solution)/shard_map/mlp_part/pallas_call | solution.py:201
  182.6 7.0 %mlp_part.6 = (f32[512,768]{1,0:T(8,128)S(1)}, f32[512,768]{1,0:T(8,128)S(1)}, bf16[768,768]{1,0:T(8,128)(2,1)S(1)}, bf16[768,768]{1,0:T(8,128)(2,1)S(1)}) custom-call(bf16[512,768]{1,0:T(8,128)(2,1)} %get-tuple-element.187.nm, bf16[512,768]{1,0:T(8,128)(2,1)} %slice.123.cot, ...), custom_call_target="tpu_custom_call", output_to_operand_aliasing={{0}: (4, {}), {1}: (5, {})} | custom-call | flops 1048576 | bytes 1048576 | tf_op jit(solution)/shard_map/mlp_part/pallas_call | solution.py:201
  192.2 2.6 collective-permute-start.32
  194.9 5.0 %turn.1 = (bf16[512,768]{1,0:T(8,128)(2,1)S(1)}, f32[512,768]{1,0:T(8,128)S(1)}, bf16[512,768]{1,0:T(8,128)(2,1)S(1)}, f32[1,768]{1,0:T(1,128)S(1)}, bf16[192,51...) custom-call(s32[1]{0:T(128)} %bitcast.10.place, ...), custom_call_target="tpu_custom_call" | custom-call | flops 1048576 | bytes 1048576 | tf_op jit(solution)/shard_map/turn/pallas_call | solution.py:228
  199.9 1.7 collective-permute-start.29
  210.6 5.3 %all-to-all-start.2 = ((bf16[8,64,768]{2,1,0:T(8,128)(2,1)}), bf16[8,64,768]{2,1,0:T(8,128)(2,1)}, u32[]{:S(2)}, u32[]{:S(2)}) async-start(bf16[8,64,768]{2,1,0:T(8,128)(2,1)} %bitcast.196), calls=%async_computation.2 | async-start | bytes 1572864 | tf_op jit(solution)/shard_map/all_to_all | solution.py:439
  216.0 1.6 collective-permute-start.34
  221.6 8.3 %attend_back.3.refs_4_ = bf16[4,192,512]{2,1,0:T(8,128)(2,1)S(1)} custom-call(s32[3]{0:T(128)S(1)} %copy-done.88, bf16[4,576,512]{2,1,0:T(8,128)(2,1)S(1)} %pad_maximum_fusion.qkv, bf16[4,64,512]{2,1,0:T(8,128)(2,1)S(1)} %copy-done.41, bf16[192,512]{1,0:T(8,128)(2,1)S(1)} %get-tuple-element.249.refs_0_, ...), custom_call_target="tpu_custom_call" | custom-call | flops 1048576 | bytes 1048576 | tf_op jit(solution)/shard_map/attend_back/pallas_call | solution.py:139
  230.8 2.1 fusion.36
  232.9 4.3 %collective-permute-start.35 = (bf16[2,2,96,768]{3,2,1,0:T(8,128)(2,1)}, bf16[2,2,96,768]{3,2,1,0:T(8,128)(2,1)}, u32[]{:S(2)}, u32[]{:S(2)}) collective-permute-start(bf16[2,2,96,768]{3,2,1,0:T(8,128)(2,1)} %fusion.36), channel_id=1, source_target_pairs={{0,2},{1,3},{2,0},{3,1},{4,6},{5,7},{6,4},{7,5},{8,10},{9,11},{10,... | collective-permute-start | bytes 1769480 | tf_op jit(solution)/shard_map/ppermute | solution.py:352
  237.2 1.8 add_convert_fusion.11
  239.3 2.3 fusion.33
  241.6 8.3 %attend_back.4.refs_5_ = bf16[4,192,512]{2,1,0:T(8,128)(2,1)S(1)} custom-call(s32[3]{0:T(128)S(1)} %copy-done.86, bf16[4,576,512]{2,1,0:T(8,128)(2,1)S(1)} %pad_maximum_fusion.qkv, bf16[4,64,512]{2,1,0:T(8,128)(2,1)S(1)} %copy-done.39, bf16[192,512]{1,0:T(8,128)(2,1)S(1)} %get-tuple-element.249.refs_0_, ...), custom_call_target="tpu_custom_call" | custom-call | flops 1048576 | bytes 1048576 | tf_op jit(solution)/shard_map/attend_back/pallas_call | solution.py:139
  250.8 2.4 collective-permute-done.36.refs_9_
  256.5 1.8 collective-permute-start.38
  259.4 2.4 collective-permute-start.37
  261.9 1.7 fusion.40
  263.9 8.5 %attend_back.5.refs_6_ = bf16[4,192,512]{2,1,0:T(8,128)(2,1)S(1)} custom-call(s32[3]{0:T(128)S(1)} %copy-done.90, bf16[4,576,512]{2,1,0:T(8,128)(2,1)S(1)} %pad_maximum_fusion.qkv, bf16[4,64,512]{2,1,0:T(8,128)(2,1)S(1)} %copy-done.36, bf16[192,512]{1,0:T(8,128)(2,1)S(1)} %get-tuple-element.249.refs_0_, ...), custom_call_target="tpu_custom_call" | custom-call | flops 1048576 | bytes 1048576 | tf_op jit(solution)/shard_map/attend_back/pallas_call | solution.py:139
  272.4 2.5 collective-permute-done.37
  278.5 2.7 collective-permute-start.40
  283.2 3.7 weight_grad.1
  286.9 1.6 collective-permute-done.40
  292.8 1.9 collective-permute-start.42
  294.8 10.4 %collective-permute-done.49 = bf16[2,2,96,768]{3,2,0,1:T(8,128)(2,1)} collective-permute-done((bf16[2,2,96,768]{3,2,0,1:T(8,128)(2,1)}, bf16[2,2,96,768]{3,2,0,1:T(8,128)(2,1)}, u32[]{:S(2)}, u32[]{:S(2)}) %collective-permute-start.49) | collective-permute-done | bytes 589856 | tf_op jit(solution)/shard_map/ppermute | solution.py:352
  305.2 1.9 fusion.37
  312.0 5.4 %collective-permute-done.50 = bf16[2,96,768]{2,1,0:T(8,128)(2,1)S(1)} collective-permute-done((bf16[2,96,768]{2,1,0:T(8,128)(2,1)S(1)}, bf16[2,96,768]{2,1,0:T(8,128)(2,1)S(1)}, u32[]{:S(2)}, u32[]{:S(2)}) %collective-permute-start.50) | collective-permute-done | bytes 294944 | tf_op jit(solution)/shard_map/ppermute | solution.py:352
  318.4 1.6 add_convert_fusion.4
  320.0 4.0 %all-to-all-start.3 = ((bf16[8,64,768]{2,1,0:T(8,128)(2,1)}), bf16[8,64,768]{2,1,0:T(8,128)(2,1)S(1)}, u32[]{:S(2)}, u32[]{:S(2)}) async-start(bf16[8,64,768]{2,1,0:T(8,128)(2,1)} %bitcast.63), calls=%async_computation.3 | async-start | bytes 1572864 | tf_op jit(solution)/shard_map/all_to_all | solution.py:439
  324.0 1.9 collective-permute-start.54
  325.9 3.0 collective-permute-start.51
  330.3 15.3 %collective-permute-done.51 = bf16[96,768]{1,0:T(8,128)(2,1)S(1)} collective-permute-done((bf16[96,768]{1,0:T(8,128)(2,1)S(1)}, bf16[96,768]{1,0:T(8,128)(2,1)S(1)}, u32[]{:S(2)}, u32[]{:S(2)}) %collective-permute-start.51) | collective-permute-done | bytes 147488 | tf_op jit(solution)/shard_map/ppermute | solution.py:352
  345.8 1.8 collective-permute-start.55
  348.1 6.1 %collective-permute-done.55 = bf16[2,96,768]{2,1,0:T(8,128)(2,1)S(1)} collective-permute-done((bf16[2,96,768]{2,1,0:T(8,128)(2,1)S(1)}, bf16[2,96,768]{2,1,0:T(8,128)(2,1)S(1)}, u32[]{:S(2)}, u32[]{:S(2)}) %collective-permute-start.55) | collective-permute-done | bytes 294944 | tf_op jit(solution)/shard_map/ppermute | solution.py:352
  356.0 1.7 collective-permute-start.44
  357.7 2.1 collective-permute-done.44
  361.2 2.5 collective-permute-done.45
  363.8 2.4 copy.149
  (459 shorter events, 99.8 us)
Async XLA Ops:
  4.1 33.7 %all-to-all-start = ((bf16[8,64,768]{2,1,0:T(8,128)(2,1)}), bf16[8,64,768]{2,1,0:T(8,128)(2,1)S(1)}, u32[]{:S(2)}, u32[]{:S(2)}) async-start(bf16[8,64,768]{2,1,0:T(8,128)(2,1)} %copy.123), calls=%async_computation | async-start | bytes 1572864 | tf_op jit(solution)/shard_map/all_to_all | solution.py:439
  12.7 28.7 %collective-permute-start = (bf16[96,896]{0,1:T(8,128)(2,1)S(1)}, bf16[96,896]{0,1:T(8,128)(2,1)S(1)}, u32[]{:S(2)}, u32[]{:S(2)}) collective-permute-start(bf16[96,896]{0,1:T(8,128)(2,1)S(1)} %concatenate.10), channel_id=1, source_target_pairs={{0,4},{1,5},{2,6},{3,7},{4,0},{5,1},{6,2},{7,3},{8,12},{9,13},{10,... | collective-permute-start | bytes 516104 | tf_op jit(solution)/shard_map/ppermute | solution.py:352
  17.2 62.4 %copy-start.85 = (s32[3]{0:T(128)}, s32[3]{0:T(128)S(1)}, u32[]{:S(2)}) copy-start(s32[3]{0:T(128)S(1)} %get-tuple-element.351.info) | copy-start | bytes 40
  17.2 113.1 %copy-start.87 = (s32[3]{0:T(128)}, s32[3]{0:T(128)S(1)}, u32[]{:S(2)}) copy-start(s32[3]{0:T(128)S(1)} %get-tuple-element.350.info) | copy-start | bytes 40
  18.2 50.6 %copy-start.112 = (pred[768]{0:T(1024)(128)(4,1)}, pred[768]{0:T(1024)(128)(4,1)S(1)}, u32[]{:S(2)}) copy-start(pred[768]{0:T(1024)(128)(4,1)S(1)} %iota.73) | copy-start | bytes 2308
  37.8 16.2 %collective-permute-start.4 = (bf16[512,768]{1,0:T(8,128)(2,1)S(1)}, bf16[512,768]{1,0:T(8,128)(2,1)S(1)}, u32[]{:S(2)}, u32[]{:S(2)}) collective-permute-start(bf16[512,768]{1,0:T(8,128)(2,1)S(1)} %bitcast.189), channel_id=1, source_target_pairs={{0,8},{8,0},{16,24},{24,16},{1,9},{9,1},{17,25},{25,17},{2,10},{10... | collective-permute-start | bytes 2359304 | tf_op jit(solution)/shard_map/ppermute | solution.py:352
  37.8 20.0 %collective-permute-start.3 = (bf16[512,768]{1,0:T(8,128)(2,1)S(1)}, bf16[512,768]{1,0:T(8,128)(2,1)S(1)}, u32[]{:S(2)}, u32[]{:S(2)}) collective-permute-start(bf16[512,768]{1,0:T(8,128)(2,1)S(1)} %bitcast.190), channel_id=1, source_target_pairs={{0,16},{8,24},{16,0},{24,8},{1,17},{9,25},{17,1},{25,9},{2,18},{10... | collective-permute-start | bytes 2359304 | tf_op jit(solution)/shard_map/ppermute | solution.py:352
  42.1 8.8 %collective-permute-start.1 = (bf16[2,96,896]{2,1,0:T(8,128)(2,1)S(1)}, bf16[2,96,896]{2,1,0:T(8,128)(2,1)S(1)}, u32[]{:S(2)}, u32[]{:S(2)}) collective-permute-start(bf16[2,96,896]{2,1,0:T(8,128)(2,1)S(1)} %broadcast_select_fusion.5), channel_id=1, source_target_pairs={{0,2},{1,3},{2,0},{3,1},{4,6},{5,7},{6,4},{7,5},{8,10},{9,11},{10,... | collective-permute-start | bytes 1032200 | tf_op jit(solution)/shard_map/ppermute | solution.py:352
  51.1 19.1 %collective-permute-start.6 = (bf16[2,96,768]{2,1,0:T(8,128)(2,1)}, bf16[2,96,768]{2,1,0:T(8,128)(2,1)S(1)}, u32[]{:S(2)}, u32[]{:S(2)}) collective-permute-start(bf16[2,96,768]{2,1,0:T(8,128)(2,1)} %pad_maximum_fusion.2), channel_id=1, source_target_pairs={{0,4},{1,5},{2,6},{3,7},{4,0},{5,1},{6,2},{7,3},{8,12},{9,13},{10,... | collective-permute-start | bytes 884744 | tf_op jit(solution)/shard_map/ppermute | solution.py:352
  52.1 16.8 %collective-permute-start.2 = (bf16[2,2,96,896]{3,2,1,0:T(8,128)(2,1)S(1)}, bf16[2,2,96,896]{3,2,1,0:T(8,128)(2,1)S(1)}, u32[]{:S(2)}, u32[]{:S(2)}) collective-permute-start(bf16[2,2,96,896]{3,2,1,0:T(8,128)(2,1)S(1)} %broadcast_select_fusion.2), channel_id=1, source_target_pairs={{0,1},{1,0},{2,3},{3,2},{4,5},{5,4},{6,7},{7,6},{8,9},{9,8},{10,11... | collective-permute-start | bytes 2064392 | tf_op jit(solution)/shard_map/ppermute | solution.py:352
  58.0 12.2 %collective-permute-start.5 = (bf16[512,768]{1,0:T(8,128)(2,1)S(1)}, bf16[512,768]{1,0:T(8,128)(2,1)S(1)}, u32[]{:S(2)}, u32[]{:S(2)}) collective-permute-start(bf16[512,768]{1,0:T(8,128)(2,1)S(1)} %collective-permute-done.3), channel_id=1, source_target_pairs={{0,8},{8,0},{16,24},{24,16},{1,9},{9,1},{17,25},{25,17},{2,10},{10... | collective-permute-start | bytes 2359304 | tf_op jit(solution)/shard_map/ppermute | solution.py:352
  70.7 17.4 %collective-permute-start.8 = (bf16[768,192]{1,0:T(8,128)(2,1)S(1)}, bf16[768,192]{1,0:T(8,128)(2,1)}, u32[]{:S(2)}, u32[]{:S(2)}) collective-permute-start(bf16[768,192]{1,0:T(8,128)(2,1)S(1)} %slice.142.refs_0_), channel_id=1, source_target_pairs={{0,16},{8,24},{16,0},{24,8},{1,17},{9,25},{17,1},{25,9},{2,18},{10... | collective-permute-start | bytes 884744 | tf_op jit(solution)/shard_map/ppermute | solution.py:352
  73.4 13.6 %collective-permute-start.7 = (bf16[2,2,96,768]{3,2,1,0:T(8,128)(2,1)S(1)}, bf16[2,2,96,768]{3,2,1,0:T(8,128)(2,1)S(1)}, u32[]{:S(2)}, u32[]{:S(2)}) collective-permute-start(bf16[2,2,96,768]{3,2,1,0:T(8,128)(2,1)S(1)} %broadcast_select_fusion.4), channel_id=1, source_target_pairs={{0,2},{1,3},{2,0},{3,1},{4,6},{5,7},{6,4},{7,5},{8,10},{9,11},{10,... | collective-permute-start | bytes 1769480 | tf_op jit(solution)/shard_map/ppermute | solution.py:352
  88.1 56.1 %all-to-all-start.1 = ((bf16[8,64,896]{2,1,0:T(8,128)(2,1)}), bf16[8,64,896]{2,1,0:T(8,128)(2,1)}, u32[]{:S(2)}, u32[]{:S(2)}) async-start(bf16[8,64,896]{2,1,0:T(8,128)(2,1)} %pad_maximum_fusion.1), calls=%async_computation.1 | async-start | bytes 1835008 | tf_op jit(solution)/shard_map/all_to_all | solution.py:439
  102.9 11.0 %collective-permute-start.9 = (bf16[768,192]{1,0:T(8,128)(2,1)S(1)}, bf16[768,192]{1,0:T(8,128)(2,1)S(1)}, u32[]{:S(2)}, u32[]{:S(2)}) collective-permute-start(bf16[768,192]{1,0:T(8,128)(2,1)S(1)} %slice.142.refs_0_), channel_id=1, source_target_pairs={{0,8},{8,0},{16,24},{24,16},{1,9},{9,1},{17,25},{25,17},{2,10},{10... | collective-permute-start | bytes 884744 | tf_op jit(solution)/shard_map/ppermute | solution.py:352
  103.0 10.9 %collective-permute-start.10 = (bf16[768,192]{1,0:T(8,128)(2,1)}, bf16[768,192]{1,0:T(8,128)(2,1)S(1)}, u32[]{:S(2)}, u32[]{:S(2)}) collective-permute-start(bf16[768,192]{1,0:T(8,128)(2,1)} %collective-permute-done.8.refs_1_), channel_id=1, source_target_pairs={{0,8},{8,0},{16,24},{24,16},{1,9},{9,1},{17,25},{25,17},{2,10},{10... | collective-permute-start | bytes 884744 | tf_op jit(solution)/shard_map/ppermute | solution.py:352
  105.5 30.6 %collective-permute-start.12 = (bf16[2,2,96,768]{3,2,1,0:T(8,128)(2,1)S(1)}, bf16[2,2,96,768]{3,2,1,0:T(8,128)(2,1)}, u32[]{:S(2)}, u32[]{:S(2)}) collective-permute-start(bf16[2,2,96,768]{3,2,1,0:T(8,128)(2,1)S(1)} %get-tuple-element.190), channel_id=1, source_target_pairs={{0,16},{8,24},{16,0},{24,8},{1,17},{9,25},{17,1},{25,9},{2,18},{10... | collective-permute-start | bytes 1769480 | tf_op jit(solution)/shard_map/ppermute | solution.py:352
  106.2 30.0 %collective-permute-start.11 = (bf16[2,2,96,768]{3,2,1,0:T(8,128)(2,1)S(1)}, bf16[2,2,96,768]{3,2,1,0:T(8,128)(2,1)S(1)}, u32[]{:S(2)}, u32[]{:S(2)}) collective-permute-start(bf16[2,2,96,768]{3,2,1,0:T(8,128)(2,1)S(1)} %get-tuple-element.169), channel_id=1, source_target_pairs={{0,1},{1,0},{2,3},{3,2},{4,5},{5,4},{6,7},{7,6},{8,9},{9,8},{10,11... | collective-permute-start | bytes 1769480 | tf_op jit(solution)/shard_map/ppermute | solution.py:352
  114.6 6.8 %collective-permute-start.15 = (bf16[64,512]{1,0:T(8,128)(2,1)S(1)}, bf16[64,512]{1,0:T(8,128)(2,1)S(1)}, u32[]{:S(2)}, u32[]{:S(2)}) collective-permute-start(bf16[64,512]{1,0:T(8,128)(2,1)S(1)} %get-tuple-element.340), channel_id=1, source_target_pairs={{0,24},{8,16},{16,8},{24,0},{1,25},{9,17},{17,9},{25,1},{2,26},{10... | collective-permute-start | bytes 196616 | tf_op jit(solution)/shard_map/ppermute | solution.py:352
  115.2 7.4 %collective-permute-start.14 = (bf16[64,512]{1,0:T(8,128)(2,1)S(1)}, bf16[64,512]{1,0:T(8,128)(2,1)S(1)}, u32[]{:S(2)}, u32[]{:S(2)}) collective-permute-start(bf16[64,512]{1,0:T(8,128)(2,1)S(1)} %get-tuple-element.341), channel_id=1, source_target_pairs={{0,8},{8,0},{16,24},{24,16},{1,9},{9,1},{17,25},{25,17},{2,10},{10... | collective-permute-start | bytes 196616 | tf_op jit(solution)/shard_map/ppermute | solution.py:352
  116.2 28.0 %collective-permute-start.22 = (bf16[2,2,96,768]{3,2,1,0:T(8,128)(2,1)S(1)}, bf16[2,2,96,768]{3,2,1,0:T(8,128)(2,1)}, u32[]{:S(2)}, u32[]{:S(2)}) collective-permute-start(bf16[2,2,96,768]{3,2,1,0:T(8,128)(2,1)S(1)} %get-tuple-element.190), channel_id=1, source_target_pairs={{0,1},{1,0},{2,3},{3,2},{4,5},{5,4},{6,7},{7,6},{8,9},{9,8},{10,11... | collective-permute-start | bytes 1769480 | tf_op jit(solution)/shard_map/ppermute | solution.py:352
  122.1 4.8 %collective-permute-start.13 = (bf16[64,512]{1,0:T(8,128)(2,1)S(1)}, bf16[64,512]{1,0:T(8,128)(2,1)S(1)}, u32[]{:S(2)}, u32[]{:S(2)}) collective-permute-start(bf16[64,512]{1,0:T(8,128)(2,1)S(1)} %get-tuple-element.342), channel_id=1, source_target_pairs={{0,16},{8,24},{16,0},{24,8},{1,17},{9,25},{17,1},{25,9},{2,18},{10... | collective-permute-start | bytes 196616 | tf_op jit(solution)/shard_map/ppermute | solution.py:352
  123.2 5.0 %collective-permute-start.18 = (bf16[64,512]{1,0:T(8,128)(2,1)S(1)}, bf16[64,512]{1,0:T(8,128)(2,1)S(1)}, u32[]{:S(2)}, u32[]{:S(2)}) collective-permute-start(bf16[64,512]{1,0:T(8,128)(2,1)S(1)} %get-tuple-element.336), channel_id=1, source_target_pairs={{0,24},{8,16},{16,8},{24,0},{1,25},{9,17},{17,9},{25,1},{2,26},{10... | collective-permute-start | bytes 196616 | tf_op jit(solution)/shard_map/ppermute | solution.py:352
  127.5 8.6 %collective-permute-start.17 = (bf16[64,512]{1,0:T(8,128)(2,1)S(1)}, bf16[64,512]{1,0:T(8,128)(2,1)S(1)}, u32[]{:S(2)}, u32[]{:S(2)}) collective-permute-start(bf16[64,512]{1,0:T(8,128)(2,1)S(1)} %get-tuple-element.337), channel_id=1, source_target_pairs={{0,8},{8,0},{16,24},{24,16},{1,9},{9,1},{17,25},{25,17},{2,10},{10... | collective-permute-start | bytes 196616 | tf_op jit(solution)/shard_map/ppermute | solution.py:352
  128.8 7.2 %collective-permute-start.16 = (bf16[64,512]{1,0:T(8,128)(2,1)S(1)}, bf16[64,512]{1,0:T(8,128)(2,1)S(1)}, u32[]{:S(2)}, u32[]{:S(2)}) collective-permute-start(bf16[64,512]{1,0:T(8,128)(2,1)S(1)} %get-tuple-element.338), channel_id=1, source_target_pairs={{0,16},{8,24},{16,0},{24,8},{1,17},{9,25},{17,1},{25,9},{2,18},{10... | collective-permute-start | bytes 196616 | tf_op jit(solution)/shard_map/ppermute | solution.py:352
  137.3 4.1 %collective-permute-start.21 = (bf16[64,512]{1,0:T(8,128)(2,1)S(1)}, bf16[64,512]{1,0:T(8,128)(2,1)S(1)}, u32[]{:S(2)}, u32[]{:S(2)}) collective-permute-start(bf16[64,512]{1,0:T(8,128)(2,1)S(1)} %get-tuple-element.332), channel_id=1, source_target_pairs={{0,24},{8,16},{16,8},{24,0},{1,25},{9,17},{17,9},{25,1},{2,26},{10... | collective-permute-start | bytes 196616 | tf_op jit(solution)/shard_map/ppermute | solution.py:352
  138.9 3.1 collective-permute-start.20
  139.3 4.3 %collective-permute-start.19 = (bf16[64,512]{1,0:T(8,128)(2,1)S(1)}, bf16[64,512]{1,0:T(8,128)(2,1)S(1)}, u32[]{:S(2)}, u32[]{:S(2)}) collective-permute-start(bf16[64,512]{1,0:T(8,128)(2,1)S(1)} %get-tuple-element.334), channel_id=1, source_target_pairs={{0,16},{8,24},{16,0},{24,8},{1,17},{9,25},{17,1},{25,9},{2,18},{10... | collective-permute-start | bytes 196616 | tf_op jit(solution)/shard_map/ppermute | solution.py:352
  144.3 28.3 %collective-permute-start.26 = (bf16[768,768]{1,0:T(8,128)(2,1)}, bf16[768,768]{1,0:T(8,128)(2,1)}, u32[]{:S(2)}, u32[]{:S(2)}) collective-permute-start(bf16[768,768]{1,0:T(8,128)(2,1)} %bitcast_select_fusion.3.wu), channel_id=1, source_target_pairs={{0,16},{8,24},{16,0},{24,8},{1,17},{9,25},{17,1},{25,9},{2,18},{10... | collective-permute-start | bytes 3538952 | tf_op jit(solution)/shard_map/ppermute | solution.py:352
  147.8 18.0 %collective-permute-start.24 = (bf16[512,768]{1,0:T(8,128)(2,1)}, bf16[512,768]{1,0:T(8,128)(2,1)}, u32[]{:S(2)}, u32[]{:S(2)}) collective-permute-start(bf16[512,768]{1,0:T(8,128)(2,1)} %slice.123.cot), channel_id=1, source_target_pairs={{0,8},{8,0},{16,24},{24,16},{1,9},{9,1},{17,25},{25,17},{2,10},{10... | collective-permute-start | bytes 2359304 | tf_op jit(solution)/shard_map/ppermute | solution.py:352
  152.6 13.3 %collective-permute-start.23 = (bf16[512,768]{1,0:T(8,128)(2,1)}, bf16[512,768]{1,0:T(8,128)(2,1)}, u32[]{:S(2)}, u32[]{:S(2)}) collective-permute-start(bf16[512,768]{1,0:T(8,128)(2,1)} %get-tuple-element.187.nm), channel_id=1, source_target_pairs={{0,8},{8,0},{16,24},{24,16},{1,9},{9,1},{17,25},{25,17},{2,10},{10... | collective-permute-start | bytes 2359304 | tf_op jit(solution)/shard_map/ppermute | solution.py:352
  153.0 19.6 %collective-permute-start.25 = (bf16[2,2,96,768]{3,2,1,0:T(8,128)(2,1)}, bf16[2,2,96,768]{3,2,1,0:T(8,128)(2,1)}, u32[]{:S(2)}, u32[]{:S(2)}) collective-permute-start(bf16[2,2,96,768]{3,2,1,0:T(8,128)(2,1)} %collective-permute-done.12), channel_id=1, source_target_pairs={{0,1},{1,0},{2,3},{3,2},{4,5},{5,4},{6,7},{7,6},{8,9},{9,8},{10,11... | collective-permute-start | bytes 1769480 | tf_op jit(solution)/shard_map/ppermute | solution.py:352
  181.7 13.1 %collective-permute-start.28 = (bf16[512,768]{1,0:T(8,128)(2,1)S(1)}, bf16[512,768]{1,0:T(8,128)(2,1)S(1)}, u32[]{:S(2)}, u32[]{:S(2)}) collective-permute-start(bf16[512,768]{1,0:T(8,128)(2,1)S(1)} %convert_element_type.480), channel_id=1, source_target_pairs={{0,8},{8,0},{16,24},{24,16},{1,9},{9,1},{17,25},{25,17},{2,10},{10... | collective-permute-start | bytes 2359304 | tf_op jit(solution)/shard_map/ppermute | solution.py:352
  181.8 13.1 %collective-permute-start.27 = (bf16[512,768]{1,0:T(8,128)(2,1)S(1)}, bf16[512,768]{1,0:T(8,128)(2,1)S(1)}, u32[]{:S(2)}, u32[]{:S(2)}) collective-permute-start(bf16[512,768]{1,0:T(8,128)(2,1)S(1)} %convert_element_type.479), channel_id=1, source_target_pairs={{0,8},{8,0},{16,24},{24,16},{1,9},{9,1},{17,25},{25,17},{2,10},{10... | collective-permute-start | bytes 2359304 | tf_op jit(solution)/shard_map/ppermute | solution.py:352
  192.2 38.6 %collective-permute-start.32 = (bf16[2,2,2,96,768]{4,3,0,1,2:T(8,128)(2,1)}, bf16[2,2,2,96,768]{4,3,0,1,2:T(8,128)(2,1)}, u32[]{:S(2)}, u32[]{:S(2)}) collective-permute-start(bf16[2,2,2,96,768]{4,3,0,1,2:T(8,128)(2,1)} %copy.136), channel_id=1, source_target_pairs={{0,1},{1,0},{2,3},{3,2},{4,5},{5,4},{6,7},{7,6},{8,9},{9,8},{10,11... | collective-permute-start | bytes 3538952 | tf_op jit(solution)/shard_map/ppermute | solution.py:352
  199.9 7.9 %collective-permute-start.29 = (bf16[192,512]{1,0:T(8,128)(2,1)S(1)}, bf16[192,512]{1,0:T(8,128)(2,1)S(1)}, u32[]{:S(2)}, u32[]{:S(2)}) collective-permute-start(bf16[192,512]{1,0:T(8,128)(2,1)S(1)} %get-tuple-element.205), channel_id=1, source_target_pairs={{0,16},{8,24},{16,0},{24,8},{1,17},{9,25},{17,1},{25,9},{2,18},{10... | collective-permute-start | bytes 589832 | tf_op jit(solution)/shard_map/ppermute | solution.py:352
  201.6 6.2 %collective-permute-start.30 = (bf16[192,512]{1,0:T(8,128)(2,1)S(1)}, bf16[192,512]{1,0:T(8,128)(2,1)S(1)}, u32[]{:S(2)}, u32[]{:S(2)}) collective-permute-start(bf16[192,512]{1,0:T(8,128)(2,1)S(1)} %get-tuple-element.206), channel_id=1, source_target_pairs={{0,8},{8,0},{16,24},{24,16},{1,9},{9,1},{17,25},{25,17},{2,10},{10... | collective-permute-start | bytes 589832 | tf_op jit(solution)/shard_map/ppermute | solution.py:352
  201.6 8.3 %collective-permute-start.31 = (bf16[192,512]{1,0:T(8,128)(2,1)S(1)}, bf16[192,512]{1,0:T(8,128)(2,1)S(1)}, u32[]{:S(2)}, u32[]{:S(2)}) collective-permute-start(bf16[192,512]{1,0:T(8,128)(2,1)S(1)} %get-tuple-element.207), channel_id=1, source_target_pairs={{0,24},{8,16},{16,8},{24,0},{1,25},{9,17},{17,9},{25,1},{2,26},{10... | collective-permute-start | bytes 589832 | tf_op jit(solution)/shard_map/ppermute | solution.py:352
  210.6 42.7 %all-to-all-start.2 = ((bf16[8,64,768]{2,1,0:T(8,128)(2,1)}), bf16[8,64,768]{2,1,0:T(8,128)(2,1)}, u32[]{:S(2)}, u32[]{:S(2)}) async-start(bf16[8,64,768]{2,1,0:T(8,128)(2,1)} %bitcast.196), calls=%async_computation.2 | async-start | bytes 1572864 | tf_op jit(solution)/shard_map/all_to_all | solution.py:439
  216.0 37.3 %collective-permute-start.34 = (bf16[768,768]{1,0:T(8,128)(2,1)}, bf16[768,768]{1,0:T(8,128)(2,1)}, u32[]{:S(2)}, u32[]{:S(2)}) collective-permute-start(bf16[768,768]{1,0:T(8,128)(2,1)} %add_convert_fusion.3), channel_id=1, source_target_pairs={{0,16},{8,24},{16,0},{24,8},{1,17},{9,25},{17,1},{25,9},{2,18},{10... | collective-permute-start | bytes 3538952 | tf_op jit(solution)/shard_map/ppermute | solution.py:352
  217.5 13.3 %collective-permute-start.33 = (bf16[768,192]{1,0:T(8,128)(2,1)}, bf16[768,192]{1,0:T(8,128)(2,1)}, u32[]{:S(2)}, u32[]{:S(2)}) collective-permute-start(bf16[768,192]{1,0:T(8,128)(2,1)} %copy-done.93), channel_id=1, source_target_pairs={{0,8},{8,0},{16,24},{24,16},{1,9},{9,1},{17,25},{25,17},{2,10},{10... | collective-permute-start | bytes 884744 | tf_op jit(solution)/shard_map/ppermute | solution.py:352
  232.9 20.4 %collective-permute-start.35 = (bf16[2,2,96,768]{3,2,1,0:T(8,128)(2,1)}, bf16[2,2,96,768]{3,2,1,0:T(8,128)(2,1)}, u32[]{:S(2)}, u32[]{:S(2)}) collective-permute-start(bf16[2,2,96,768]{3,2,1,0:T(8,128)(2,1)} %fusion.36), channel_id=1, source_target_pairs={{0,2},{1,3},{2,0},{3,1},{4,6},{5,7},{6,4},{7,5},{8,10},{9,11},{10,... | collective-permute-start | bytes 1769480 | tf_op jit(solution)/shard_map/ppermute | solution.py:352
  239.0 14.2 %collective-permute-start.36 = (bf16[768,192]{1,0:T(8,128)(2,1)}, bf16[768,192]{1,0:T(8,128)(2,1)}, u32[]{:S(2)}, u32[]{:S(2)}) collective-permute-start(bf16[768,192]{1,0:T(8,128)(2,1)} %add_convert_fusion.11), channel_id=1, source_target_pairs={{0,16},{8,24},{16,0},{24,8},{1,17},{9,25},{17,1},{25,9},{2,18},{10... | collective-permute-start | bytes 884744 | tf_op jit(solution)/shard_map/ppermute | solution.py:352
  256.5 18.4 %collective-permute-start.38 = (bf16[2,2,96,768]{3,2,0,1:T(8,128)(2,1)S(1)}, bf16[2,2,96,768]{3,2,0,1:T(8,128)(2,1)S(1)}, u32[]{:S(2)}, u32[]{:S(2)}) collective-permute-start(bf16[2,2,96,768]{3,2,0,1:T(8,128)(2,1)S(1)} %fusion.35), channel_id=1, source_target_pairs={{0,1},{1,0},{2,3},{3,2},{4,5},{5,4},{6,7},{7,6},{8,9},{9,8},{10,11... | collective-permute-start | bytes 1769480 | tf_op jit(solution)/shard_map/ppermute | solution.py:352
  259.4 15.5 %collective-permute-start.37 = (bf16[2,96,768]{2,1,0:T(8,128)(2,1)S(1)}, bf16[2,96,768]{2,1,0:T(8,128)(2,1)S(1)}, u32[]{:S(2)}, u32[]{:S(2)}) collective-permute-start(bf16[2,96,768]{2,1,0:T(8,128)(2,1)S(1)} %fusion.43), channel_id=1, source_target_pairs={{0,4},{1,5},{2,6},{3,7},{4,0},{5,1},{6,2},{7,3},{8,12},{9,13},{10,... | collective-permute-start | bytes 884744 | tf_op jit(solution)/shard_map/ppermute | solution.py:352
  277.8 12.5 %collective-permute-start.41 = (bf16[2,512,768]{2,1,0:T(8,128)(2,1)S(1)}, bf16[2,512,768]{2,1,0:T(8,128)(2,1)S(1)}, u32[]{:S(2)}, u32[]{:S(2)}) collective-permute-start(bf16[2,512,768]{2,1,0:T(8,128)(2,1)S(1)} %rows_grad.3), channel_id=1, source_target_pairs={{0,8},{8,0},{16,24},{24,16},{1,9},{9,1},{17,25},{25,17},{2,10},{10... | collective-permute-start | bytes 4718600 | tf_op jit(solution)/shard_map/ppermute | solution.py:352
  277.9 4.8 %collective-permute-start.39 = (bf16[768,192]{1,0:T(8,128)(2,1)S(1)}, bf16[768,192]{1,0:T(8,128)(2,1)S(1)}, u32[]{:S(2)}, u32[]{:S(2)}) collective-permute-start(bf16[768,192]{1,0:T(8,128)(2,1)S(1)} %copy-done.92), channel_id=1, source_target_pairs={{0,8},{8,0},{16,24},{24,16},{1,9},{9,1},{17,25},{25,17},{2,10},{10... | collective-permute-start | bytes 884744 | tf_op jit(solution)/shard_map/ppermute | solution.py:352
  278.5 10.0 %collective-permute-start.40 = (bf16[2,96,768]{2,1,0:T(8,128)(2,1)S(1)}, bf16[2,96,768]{2,1,0:T(8,128)(2,1)S(1)}, u32[]{:S(2)}, u32[]{:S(2)}) collective-permute-start(bf16[2,96,768]{2,1,0:T(8,128)(2,1)S(1)} %get-tuple-element.312), channel_id=1, source_target_pairs={{0,2},{1,3},{2,0},{3,1},{4,6},{5,7},{6,4},{7,5},{8,10},{9,11},{10,... | collective-permute-start | bytes 884744 | tf_op jit(solution)/shard_map/ppermute | solution.py:352
  290.1 15.1 %collective-permute-start.49 = (bf16[2,2,96,768]{3,2,0,1:T(8,128)(2,1)}, bf16[2,2,96,768]{3,2,0,1:T(8,128)(2,1)}, u32[]{:S(2)}, u32[]{:S(2)}) collective-permute-start(bf16[2,2,96,768]{3,2,0,1:T(8,128)(2,1)} %copy_bitcast_fusion.1), channel_id=1, source_target_pairs={{0,1},{1,0},{2,3},{3,2},{4,5},{5,4},{6,7},{7,6},{8,9},{9,8},{10,11... | collective-permute-start | bytes 1769480 | tf_op jit(solution)/shard_map/ppermute | solution.py:352
  292.8 24.6 %collective-permute-start.42 = (bf16[512,768]{1,0:T(8,128)(2,1)}, bf16[512,768]{1,0:T(8,128)(2,1)S(1)}, u32[]{:S(2)}, u32[]{:S(2)}) collective-permute-start(bf16[512,768]{1,0:T(8,128)(2,1)} %slice_bitcast_fusion), channel_id=1, source_target_pairs={{0,16},{8,24},{16,0},{24,8},{1,17},{9,25},{17,1},{25,9},{2,18},{10... | collective-permute-start | bytes 2359304 | tf_op jit(solution)/shard_map/ppermute | solution.py:352
  307.1 10.3 %collective-permute-start.50 = (bf16[2,96,768]{2,1,0:T(8,128)(2,1)S(1)}, bf16[2,96,768]{2,1,0:T(8,128)(2,1)S(1)}, u32[]{:S(2)}, u32[]{:S(2)}) collective-permute-start(bf16[2,96,768]{2,1,0:T(8,128)(2,1)S(1)} %get-tuple-element.308), channel_id=1, source_target_pairs={{0,2},{1,3},{2,0},{3,1},{4,6},{5,7},{6,4},{7,5},{8,10},{9,11},{10,... | collective-permute-start | bytes 884744 | tf_op jit(solution)/shard_map/ppermute | solution.py:352
  310.8 19.6 %collective-permute-start.48 = (bf16[96,768]{1,0:T(8,128)(2,1)}, bf16[96,768]{1,0:T(8,128)(2,1)S(1)}, u32[]{:S(2)}, u32[]{:S(2)}) collective-permute-start(bf16[96,768]{1,0:T(8,128)(2,1)} %get-tuple-element.330), channel_id=1, source_target_pairs={{0,4},{1,5},{2,6},{3,7},{4,0},{5,1},{6,2},{7,3},{8,12},{9,13},{10,... | collective-permute-start | bytes 442376 | tf_op jit(solution)/shard_map/ppermute | solution.py:352
  320.0 49.3 %all-to-all-start.3 = ((bf16[8,64,768]{2,1,0:T(8,128)(2,1)}), bf16[8,64,768]{2,1,0:T(8,128)(2,1)S(1)}, u32[]{:S(2)}, u32[]{:S(2)}) async-start(bf16[8,64,768]{2,1,0:T(8,128)(2,1)} %bitcast.63), calls=%async_computation.3 | async-start | bytes 1572864 | tf_op jit(solution)/shard_map/all_to_all | solution.py:439
  324.0 21.7 %collective-permute-start.54 = (bf16[96,768]{1,0:T(8,128)(2,1)S(1)}, bf16[96,768]{1,0:T(8,128)(2,1)S(1)}, u32[]{:S(2)}, u32[]{:S(2)}) collective-permute-start(bf16[96,768]{1,0:T(8,128)(2,1)S(1)} %slice_bitcast_fusion.5), channel_id=1, source_target_pairs={{0,16},{8,24},{16,0},{24,8},{1,17},{9,25},{17,1},{25,9},{2,18},{10... | collective-permute-start | bytes 442376 | tf_op jit(solution)/shard_map/ppermute | solution.py:352
  325.9 19.7 %collective-permute-start.51 = (bf16[96,768]{1,0:T(8,128)(2,1)S(1)}, bf16[96,768]{1,0:T(8,128)(2,1)S(1)}, u32[]{:S(2)}, u32[]{:S(2)}) collective-permute-start(bf16[96,768]{1,0:T(8,128)(2,1)S(1)} %get-tuple-element.328), channel_id=1, source_target_pairs={{0,4},{1,5},{2,6},{3,7},{4,0},{5,1},{6,2},{7,3},{8,12},{9,13},{10,... | collective-permute-start | bytes 442376 | tf_op jit(solution)/shard_map/ppermute | solution.py:352
  345.8 8.4 %collective-permute-start.55 = (bf16[2,96,768]{2,1,0:T(8,128)(2,1)S(1)}, bf16[2,96,768]{2,1,0:T(8,128)(2,1)S(1)}, u32[]{:S(2)}, u32[]{:S(2)}) collective-permute-start(bf16[2,96,768]{2,1,0:T(8,128)(2,1)S(1)} %pad_maximum_fusion.3), channel_id=1, source_target_pairs={{0,16},{8,24},{16,0},{24,8},{1,17},{9,25},{17,1},{25,9},{2,18},{10... | collective-permute-start | bytes 884744 | tf_op jit(solution)/shard_map/ppermute | solution.py:352
  347.6 8.3 %collective-permute-start.43 = (f32[8,768]{1,0:T(8,128)S(1)}, f32[8,768]{1,0:T(8,128)S(1)}, u32[]{:S(2)}, u32[]{:S(2)}) collective-permute-start(f32[8,768]{1,0:T(8,128)S(1)} %maximum_maximum_fusion), channel_id=1, source_target_pairs={{0,8},{8,0},{16,24},{24,16},{1,9},{9,1},{17,25},{25,17},{2,10},{10... | collective-permute-start | bytes 73736 | tf_op jit(solution)/shard_map/ppermute | solution.py:352
  347.7 8.0 %collective-permute-start.52 = (bf16[96,768]{1,0:T(8,128)(2,1)S(1)}, bf16[96,768]{1,0:T(8,128)(2,1)S(1)}, u32[]{:S(2)}, u32[]{:S(2)}) collective-permute-start(bf16[96,768]{1,0:T(8,128)(2,1)S(1)} %add_convert_fusion.17), channel_id=1, source_target_pairs={{0,16},{8,24},{16,0},{24,8},{1,17},{9,25},{17,1},{25,9},{2,18},{10... | collective-permute-start | bytes 442376 | tf_op jit(solution)/shard_map/ppermute | solution.py:352
  354.3 14.5 %collective-permute-start.56 = (bf16[2,2,96,768]{3,2,0,1:T(8,128)(2,1)S(1)}, bf16[2,2,96,768]{3,2,0,1:T(8,128)(2,1)S(1)}, u32[]{:S(2)}, u32[]{:S(2)}) collective-permute-start(bf16[2,2,96,768]{3,2,0,1:T(8,128)(2,1)S(1)} %broadcast_select_fusion.3), channel_id=1, source_target_pairs={{0,8},{8,0},{16,24},{24,16},{1,9},{9,1},{17,25},{25,17},{2,10},{10... | collective-permute-start | bytes 1769480 | tf_op jit(solution)/shard_map/ppermute | solution.py:352
  355.8 11.7 %collective-permute-start.53 = (bf16[2,96,768]{2,1,0:T(8,128)(2,1)S(1)}, bf16[2,96,768]{2,1,0:T(8,128)(2,1)S(1)}, u32[]{:S(2)}, u32[]{:S(2)}) collective-permute-start(bf16[2,96,768]{2,1,0:T(8,128)(2,1)S(1)} %broadcast_select_fusion.6), channel_id=1, source_target_pairs={{0,8},{8,0},{16,24},{24,16},{1,9},{9,1},{17,25},{25,17},{2,10},{10... | collective-permute-start | bytes 884744 | tf_op jit(solution)/shard_map/ppermute | solution.py:352
  356.0 3.8 %collective-permute-start.44 = (f32[8,768]{1,0:T(8,128)S(1)}, f32[8,768]{1,0:T(8,128)S(1)}, u32[]{:S(2)}, u32[]{:S(2)}) collective-permute-start(f32[8,768]{1,0:T(8,128)S(1)} %fusion.69), channel_id=1, source_target_pairs={{0,16},{8,24},{16,0},{24,8},{1,17},{9,25},{17,1},{25,9},{2,18},{10... | collective-permute-start | bytes 73736 | tf_op jit(solution)/shard_map/ppermute | solution.py:352
  359.8 3.8 %collective-permute-start.45 = (f32[8,768]{1,0:T(8,128)S(1)}, f32[8,768]{1,0:T(8,128)S(1)}, u32[]{:S(2)}, u32[]{:S(2)}) collective-permute-start(f32[8,768]{1,0:T(8,128)S(1)} %add.261), channel_id=1, source_target_pairs={{0,1},{1,0},{2,3},{3,2},{4,5},{5,4},{6,7},{7,6},{8,9},{9,8},{10,11... | collective-permute-start | bytes 73736 | tf_op jit(solution)/shard_map/ppermute | solution.py:352
  363.7 3.8 %collective-permute-start.46 = (f32[8,768]{1,0:T(8,128)S(1)}, f32[8,768]{1,0:T(8,128)S(1)}, u32[]{:S(2)}, u32[]{:S(2)}) collective-permute-start(f32[8,768]{1,0:T(8,128)S(1)} %add.262), channel_id=1, source_target_pairs={{0,2},{1,3},{2,0},{3,1},{4,6},{5,7},{6,4},{7,5},{8,10},{9,11},{10,... | collective-permute-start | bytes 73736 | tf_op jit(solution)/shard_map/ppermute | solution.py:352
  369.3 4.8 %collective-permute-start.47 = (f32[8,768]{1,0:T(8,128)S(1)}, f32[8,768]{1,0:T(8,128)S(1)}, u32[]{:S(2)}, u32[]{:S(2)}) collective-permute-start(f32[8,768]{1,0:T(8,128)S(1)} %add.263), channel_id=1, source_target_pairs={{0,4},{1,5},{2,6},{3,7},{4,0},{5,1},{6,2},{7,3},{8,12},{9,13},{10,... | collective-permute-start | bytes 73736 | tf_op jit(solution)/shard_map/ppermute | solution.py:352
  (121 other events, 703.5 us)
